TPU v7x, 32 devices: a whole 2x2x4 slice. The times are simulated.
32 devices in a mesh: dp: 8 (over z, core), seq: 4 (over y, x).
Axes of the slice: x: 2, y: 2, z: 4, core: 2. Of those that a mesh axis runs over, the one named last changes fastest.
Arguments:
- tokens: bfloat16 [32, 1024, 768], P('dp', 'seq'), may hold values from -6 to 6
- cotangent: bfloat16 [32, 1024, 768], P('dp', 'seq'), may hold values from -6 to 6
- segment_ids: int32 [32, 1024], P('dp'), may hold values from 0 to 5, never falling along the last dimension, each value on 1 to 512 neighbouring positions
- w_qkv: float32 [768, 2304], P(('dp', 'seq')), may hold values from -0.21875 to 0.21875
- m_qkv: float32 [768, 2304], P(('dp', 'seq')), may hold values from -160 to 160
- v_qkv: float32 [768, 2304], P(('dp', 'seq')), may hold values from 65.536 to 262.144
- w_out: float32 [768, 768], P(('dp', 'seq')), may hold values from -1.25 to 1.25
- m_out: float32 [768, 768], P(('dp', 'seq')), may hold values from -40 to 40
- v_out: float32 [768, 768], P(('dp', 'seq')), may hold values from 3.2768 to 13.1072
- w_up: float32 [768, 3072], P(('dp', 'seq')), may hold values from -0.21875 to 0.21875
- m_up: float32 [768, 3072], P(('dp', 'seq')), may hold values from -40 to 40
- v_up: float32 [768, 3072], P(('dp', 'seq')), may hold values from 3.2768 to 13.1072
- w_down: float32 [3072, 768], P(('dp', 'seq')), may hold values from -0.109375 to 0.109375
- m_down: float32 [3072, 768], P(('dp', 'seq')), may hold values from -64 to 64
- v_down: float32 [3072, 768], P(('dp', 'seq')), may hold values from 11.79648 to 47.18592
- vectors: float32 [8, 768], P(None, ('dp', 'seq')), may hold values from -1.2 to 1.8
- m_vectors: float32 [8, 768], P(None, ('dp', 'seq')), may hold values from -160 to 160
- v_vectors: float32 [8, 768], P(None, ('dp', 'seq')), may hold values from 65.536 to 262.144
- up_bias: float32 [3072], P(('dp', 'seq')), may hold values from -1.75 to 1.75
- m_up_bias: float32 [3072], P(('dp', 'seq')), may hold values from -40 to 40
- v_up_bias: float32 [3072], P(('dp', 'seq')), may hold values from 3.2768 to 13.1072
Outputs:
- mixed: bfloat16 [32, 1024, 768], P('dp', 'seq')
- input_grad: float32 [32, 1024, 768], P('dp', 'seq')
- grad_qkv: float32 [768, 2304], P(('dp', 'seq'))
- grad_out: float32 [768, 768], P(('dp', 'seq'))
- grad_up: float32 [768, 3072], P(('dp', 'seq'))
- grad_down: float32 [3072, 768], P(('dp', 'seq'))
- grad_vectors: float32 [8, 768], P(None, ('dp', 'seq'))
- grad_up_bias: float32 [3072], P(('dp', 'seq'))
- first_qkv: float32 [768, 2304], P(('dp', 'seq'))
- first_out: float32 [768, 768], P(('dp', 'seq'))
- first_up: float32 [768, 3072], P(('dp', 'seq'))
- first_down: float32 [3072, 768], P(('dp', 'seq'))
- first_vectors: float32 [8, 768], P(None, ('dp', 'seq'))
- first_up_bias: float32 [3072], P(('dp', 'seq'))
- second_qkv: float32 [768, 2304], P(('dp', 'seq'))
- second_out: float32 [768, 768], P(('dp', 'seq'))
- second_up: float32 [768, 3072], P(('dp', 'seq'))
- second_down: float32 [3072, 768], P(('dp', 'seq'))
- second_vectors: float32 [8, 768], P(None, ('dp', 'seq'))
- second_up_bias: float32 [3072], P(('dp', 'seq'))
- new_qkv: float32 [768, 2304], P(('dp', 'seq'))
- new_out: float32 [768, 768], P(('dp', 'seq'))
- new_up: float32 [768, 3072], P(('dp', 'seq'))
- new_down: float32 [3072, 768], P(('dp', 'seq'))
- new_vectors: float32 [8, 768], P(None, ('dp', 'seq'))
- new_up_bias: float32 [3072], P(('dp', 'seq'))
- copy_qkv: bfloat16 [768, 2304], P(('dp', 'seq'))
- copy_out: bfloat16 [768, 768], P(('dp', 'seq'))
- copy_up: bfloat16 [768, 3072], P(('dp', 'seq'))
- copy_down: bfloat16 [3072, 768], P(('dp', 'seq'))
Inputs may be any that keep to these rules, and one draw needn't show every extreme that they name: `segment_ids`: within each row of 1024 positions the ids never fall; no document has more than 512 positions.
All inputs are finite; a program needn't handle non-finite values.
Results may differ from a plain program's by a relative error of at most 0.012.
The roundings to bfloat16 on the way count: a program that leaves them out, or rounds other values in their place, can miss the bound.
Values may be sent and summed in bfloat16 or wider, within the bound.
A program may use at most 384 MiB of HBM per device.

v0:
```python
import jax
import jax.numpy as jnp
from jax import lax
from jax.sharding import PartitionSpec as P

HEADS = 12
HEAD_DIM = 64
MICRO = 2


BETA_ONE = 0.9
BETA_TWO = 0.999
ADAM_EPS = 1e-06
DECAY_RATE = 0.01
LEARN_RATE = 0.4
NORM_EPS = 1e-05
STEP_NUMBER = 10.0


def matmul(left_side, right_side):
    return jnp.dot(left_side, right_side, preferred_element_type=jnp.float32)


def inner_rows(left_side, right_side):
    return lax.dot_general(
        left_side, right_side, (((0,), (0,)), ((), ())), preferred_element_type=jnp.float32
    )


def times_transposed(left_side, right_side):
    return lax.dot_general(
        left_side, right_side, (((1,), (1,)), ((), ())), preferred_element_type=jnp.float32
    )


def gelu_tanh(values):
    return jax.nn.gelu(values, approximate=True)


def norm_forward(values, norm_gain, norm_shift):
    center = values - jnp.mean(values, axis=-1, keepdims=True)
    inverse = lax.rsqrt(jnp.mean(center * center, axis=-1, keepdims=True) + NORM_EPS)
    normed = center * inverse
    return (normed * norm_gain + norm_shift, normed, inverse)


def norm_backward(upstream, normed, inverse, norm_gain):
    scaled = upstream * norm_gain
    centered = scaled - jnp.mean(scaled, axis=-1, keepdims=True)
    return inverse * (centered - normed * jnp.mean(scaled * normed, axis=-1, keepdims=True))


def masked_scores(queries, key_rows, allowed):
    raw_scores = jnp.einsum(
        "sqhd,skhd->shqk", queries, key_rows, preferred_element_type=jnp.float32
    ) * HEAD_DIM ** (-0.5)
    return jnp.where(allowed[:, None], raw_scores, -1000000000.0)


def lamb_parts(weight, first, second, grad, decay, corr_one, corr_two, axis):
    first_new = BETA_ONE * first + (1.0 - BETA_ONE) * grad
    second_new = BETA_TWO * second + (1.0 - BETA_TWO) * grad * grad
    update = first_new / corr_one / (jnp.sqrt(second_new / corr_two) + ADAM_EPS) + decay * weight
    weight_sq = jnp.reshape(jnp.sum(weight * weight, axis=axis), (-1,))
    update_sq = jnp.reshape(jnp.sum(update * update, axis=axis), (-1,))
    return (first_new, second_new, update, weight_sq, update_sq)


def body(
    tokens,
    cotangent,
    segment_ids,
    w_qkv,
    m_qkv,
    v_qkv,
    w_out,
    m_out,
    v_out,
    w_up,
    m_up,
    v_up,
    w_down,
    m_down,
    v_down,
    vectors,
    m_vectors,
    v_vectors,
    up_bias,
    m_up_bias,
    v_up_bias,
):
    brain = jnp.bfloat16
    full_qkv, full_out, full_up, full_down, full_vectors, full_up_bias = (
        lax.all_gather(w_qkv.astype(brain), ("dp", "seq"), axis=0, tiled=True),
        lax.all_gather(w_out.astype(brain), ("dp", "seq"), axis=0, tiled=True),
        lax.all_gather(w_up.astype(brain), ("dp", "seq"), axis=0, tiled=True),
        lax.all_gather(w_down.astype(brain), ("dp", "seq"), axis=0, tiled=True),
        lax.all_gather(vectors.astype(brain), ("dp", "seq"), axis=1, tiled=True),
        lax.all_gather(up_bias.astype(brain), ("dp", "seq"), axis=0, tiled=True),
    )
    vector_rows = full_vectors.astype(jnp.float32)
    up_shift = full_up_bias.astype(jnp.float32)
    model_width = full_out.shape[0]
    row_count, pos_count, _ = tokens.shape
    seq_count = row_count // MICRO
    seq_length = segment_ids.shape[1]
    block = seq_count * pos_count
    score_scale = HEAD_DIM ** (-0.5)
    first_pos = lax.axis_index("seq") * pos_count
    query_places = first_pos + lax.iota(jnp.int32, pos_count)
    key_places = lax.iota(jnp.int32, seq_length)
    causal = key_places[None, None, :] <= query_places[None, :, None]
    grad_qkv = jnp.zeros(full_qkv.shape, jnp.float32)
    grad_out = jnp.zeros(full_out.shape, jnp.float32)
    grad_up = jnp.zeros(full_up.shape, jnp.float32)
    grad_down = jnp.zeros(full_down.shape, jnp.float32)
    grad_vectors = jnp.zeros(full_vectors.shape, jnp.float32)
    grad_up_bias = jnp.zeros(full_up_bias.shape, jnp.float32)
    mixed_parts = []
    input_parts = []
    local_heads = (seq_count, pos_count, HEADS, HEAD_DIM)
    whole_heads = (seq_count, seq_length, HEADS, HEAD_DIM)
    for micro_index in range(MICRO):
        lower = micro_index * seq_count
        token_part = (
            tokens[lower : lower + seq_count].astype(jnp.float32).reshape(block, model_width)
        )
        back_part = cotangent[lower : lower + seq_count].reshape(block, model_width)
        segment_part = segment_ids[lower : lower + seq_count]
        query_segments = lax.dynamic_slice_in_dim(segment_part, first_pos, pos_count, 1)
        allowed = (query_segments[:, :, None] == segment_part[:, None, :]) & causal
        normed_one, plain_one, inverse_one = norm_forward(
            token_part, vector_rows[0], vector_rows[1]
        )
        low_one = normed_one.astype(brain)
        projected = matmul(low_one, full_qkv)
        queries = (projected[:, :model_width] + vector_rows[4]).astype(brain)
        key_local = projected[:, model_width : 2 * model_width].astype(brain)
        value_local = (projected[:, 2 * model_width :] + vector_rows[5]).astype(brain)
        key_all, value_all = (
            lax.all_gather(
                key_local.reshape(seq_count, pos_count, model_width), "seq", axis=1, tiled=True
            ),
            lax.all_gather(
                value_local.reshape(seq_count, pos_count, model_width), "seq", axis=1, tiled=True
            ),
        )
        query_heads = queries.reshape(local_heads)
        key_heads = key_all.reshape(whole_heads)
        value_heads = value_all.reshape(whole_heads)
        scores = masked_scores(query_heads, key_heads, allowed)
        peak = jnp.max(scores, axis=-1, keepdims=True)
        log_total = peak + jnp.log(jnp.sum(jnp.exp(scores - peak), axis=-1, keepdims=True))
        attn_probs = jnp.exp(scores - log_total).astype(brain)
        context = jnp.einsum(
            "shqk,skhd->sqhd", attn_probs, value_heads, preferred_element_type=jnp.float32
        )
        context = context.astype(brain).reshape(block, model_width)
        attended = matmul(context, full_out) + vector_rows[6]
        resid_one = token_part + attended
        normed_two, plain_two, inverse_two = norm_forward(resid_one, vector_rows[2], vector_rows[3])
        low_two = normed_two.astype(brain)
        hidden_pre = matmul(low_two, full_up) + up_shift
        activated, gelu_pull = jax.vjp(gelu_tanh, hidden_pre)
        low_act = activated.astype(brain)
        result = resid_one + matmul(low_act, full_down) + vector_rows[7]
        mixed_parts.append(result.astype(brain).reshape(seq_count, pos_count, model_width))
        back_float = back_part.astype(jnp.float32)
        grad_down = grad_down + inner_rows(low_act, back_part)
        down_shift_grad = jnp.sum(back_float, axis=0)
        act_grad = times_transposed(back_part, full_down)
        hidden_grad = gelu_pull(act_grad)[0].astype(brain)
        grad_up = grad_up + inner_rows(low_two, hidden_grad)
        grad_up_bias = grad_up_bias + jnp.sum(hidden_grad.astype(jnp.float32), axis=0)
        two_grad = times_transposed(hidden_grad, full_up)
        resid_grad = back_float + norm_backward(two_grad, plain_two, inverse_two, vector_rows[2])
        gain_two = jnp.sum(two_grad * plain_two, axis=0)
        shift_two = jnp.sum(two_grad, axis=0)
        branch_grad = resid_grad.astype(brain)
        out_shift = jnp.sum(branch_grad.astype(jnp.float32), axis=0)
        grad_out = grad_out + inner_rows(context, branch_grad)
        context_grad = times_transposed(branch_grad, full_out).astype(brain).reshape(local_heads)
        again = masked_scores(query_heads, key_heads, allowed)
        attn_exact = jnp.exp(again - log_total)
        prob_grad = jnp.einsum(
            "sqhd,skhd->shqk", context_grad, value_heads, preferred_element_type=jnp.float32
        )
        row_dot = jnp.sum(attn_exact * prob_grad, axis=-1, keepdims=True)
        score_grad = jnp.where(allowed[:, None], attn_exact * (prob_grad - row_dot), 0.0).astype(
            brain
        )
        query_grad = (
            jnp.einsum("shqk,skhd->sqhd", score_grad, key_heads, preferred_element_type=jnp.float32)
            * score_scale
        )
        query_grad = query_grad.astype(brain).reshape(block, model_width)
        key_term = (
            jnp.einsum(
                "shqk,sqhd->skhd", score_grad, query_heads, preferred_element_type=jnp.float32
            )
            * score_scale
        )
        value_term = jnp.einsum(
            "shqk,sqhd->skhd", attn_probs, context_grad, preferred_element_type=jnp.float32
        )
        key_sum, value_sum = (
            lax.psum_scatter(
                key_term.reshape(seq_count, seq_length, model_width),
                "seq",
                scatter_dimension=1,
                tiled=True,
            ),
            lax.psum_scatter(
                value_term.reshape(seq_count, seq_length, model_width),
                "seq",
                scatter_dimension=1,
                tiled=True,
            ),
        )
        key_grad = key_sum.reshape(block, model_width).astype(brain)
        value_grad = value_sum.reshape(block, model_width).astype(brain)
        joined = jnp.concatenate([query_grad, key_grad, value_grad], axis=1)
        grad_qkv = grad_qkv + inner_rows(low_one, joined)
        one_grad = times_transposed(joined, full_qkv)
        input_rows = resid_grad + norm_backward(one_grad, plain_one, inverse_one, vector_rows[0])
        input_parts.append(input_rows.reshape(seq_count, pos_count, model_width))
        vector_terms = jnp.stack(
            [
                jnp.sum(one_grad * plain_one, axis=0),
                jnp.sum(one_grad, axis=0),
                gain_two,
                shift_two,
                jnp.sum(query_grad.astype(jnp.float32), axis=0),
                jnp.sum(value_grad.astype(jnp.float32), axis=0),
                out_shift,
                down_shift_grad,
            ]
        )
        grad_vectors = grad_vectors + vector_terms
    all_grads = (grad_qkv, grad_out, grad_up, grad_down, grad_vectors, grad_up_bias)
    summed = lax.psum(
        (all_grads[0], all_grads[1], all_grads[2], all_grads[3], all_grads[4], all_grads[5]),
        ("dp", "seq"),
    )
    place = lax.axis_index(("dp", "seq"))
    shares = (
        lax.dynamic_slice_in_dim(summed[0], place * w_qkv.shape[0], w_qkv.shape[0], 0),
        lax.dynamic_slice_in_dim(summed[1], place * w_out.shape[0], w_out.shape[0], 0),
        lax.dynamic_slice_in_dim(summed[2], place * w_up.shape[0], w_up.shape[0], 0),
        lax.dynamic_slice_in_dim(summed[3], place * w_down.shape[0], w_down.shape[0], 0),
        lax.dynamic_slice_in_dim(summed[4], place * vectors.shape[1], vectors.shape[1], 1),
        lax.dynamic_slice_in_dim(summed[5], place * up_bias.shape[0], up_bias.shape[0], 0),
    )
    count_float = jnp.asarray(STEP_NUMBER, jnp.float32)
    corr_one = 1.0 - jnp.power(jnp.asarray(BETA_ONE, jnp.float32), count_float)
    corr_two = 1.0 - jnp.power(jnp.asarray(BETA_TWO, jnp.float32), count_float)
    weights = (w_qkv, w_out, w_up, w_down, vectors, up_bias)
    firsts = (m_qkv, m_out, m_up, m_down, m_vectors, m_up_bias)
    seconds = (v_qkv, v_out, v_up, v_down, v_vectors, v_up_bias)
    decays = (DECAY_RATE, DECAY_RATE, DECAY_RATE, DECAY_RATE, 0.0, 0.0)
    axes_list = (None, None, None, None, 1, None)
    first_list = []
    second_list = []
    update_list = []
    weight_terms = []
    update_terms = []
    for tensor_index in range(6):
        first_new, second_new, update, weight_sq, update_sq = lamb_parts(
            weights[tensor_index],
            firsts[tensor_index],
            seconds[tensor_index],
            shares[tensor_index],
            decays[tensor_index],
            corr_one,
            corr_two,
            axes_list[tensor_index],
        )
        first_list.append(first_new)
        second_list.append(second_new)
        update_list.append(update)
        weight_terms.append(weight_sq)
        update_terms.append(update_sq)
    weight_total, update_total = lax.psum(
        (jnp.concatenate(weight_terms), jnp.concatenate(update_terms)), ("dp", "seq")
    )
    ratios = jnp.sqrt(weight_total) / (jnp.sqrt(update_total) + ADAM_EPS)
    new_list = []
    for tensor_index in range(4):
        new_list.append(
            weights[tensor_index] - LEARN_RATE * ratios[tensor_index] * update_list[tensor_index]
        )
    new_list.append(weights[4] - LEARN_RATE * ratios[4:12][:, None] * update_list[4])
    new_list.append(weights[5] - LEARN_RATE * ratios[12] * update_list[5])
    mixed = jnp.concatenate(mixed_parts, axis=0)
    input_grad = jnp.concatenate(input_parts, axis=0)
    return (
        mixed,
        input_grad,
        shares[0],
        shares[1],
        shares[2],
        shares[3],
        shares[4],
        shares[5],
        first_list[0],
        first_list[1],
        first_list[2],
        first_list[3],
        first_list[4],
        first_list[5],
        second_list[0],
        second_list[1],
        second_list[2],
        second_list[3],
        second_list[4],
        second_list[5],
        new_list[0],
        new_list[1],
        new_list[2],
        new_list[3],
        new_list[4],
        new_list[5],
        new_list[0].astype(brain),
        new_list[1].astype(brain),
        new_list[2].astype(brain),
        new_list[3].astype(brain),
    )


def solution(mesh):
    in_specs = (
        P("dp", "seq", None),
        P("dp", "seq", None),
        P("dp", None),
        P(("dp", "seq"), None),
        P(("dp", "seq"), None),
        P(("dp", "seq"), None),
        P(("dp", "seq"), None),
        P(("dp", "seq"), None),
        P(("dp", "seq"), None),
        P(("dp", "seq"), None),
        P(("dp", "seq"), None),
        P(("dp", "seq"), None),
        P(("dp", "seq"), None),
        P(("dp", "seq"), None),
        P(("dp", "seq"), None),
        P(None, ("dp", "seq")),
        P(None, ("dp", "seq")),
        P(None, ("dp", "seq")),
        P(("dp", "seq")),
        P(("dp", "seq")),
        P(("dp", "seq")),
    )
    out_specs = (
        P("dp", "seq", None),
        P("dp", "seq", None),
        P(("dp", "seq"), None),
        P(("dp", "seq"), None),
        P(("dp", "seq"), None),
        P(("dp", "seq"), None),
        P(None, ("dp", "seq")),
        P(("dp", "seq")),
        P(("dp", "seq"), None),
        P(("dp", "seq"), None),
        P(("dp", "seq"), None),
        P(("dp", "seq"), None),
        P(None, ("dp", "seq")),
        P(("dp", "seq")),
        P(("dp", "seq"), None),
        P(("dp", "seq"), None),
        P(("dp", "seq"), None),
        P(("dp", "seq"), None),
        P(None, ("dp", "seq")),
        P(("dp", "seq")),
        P(("dp", "seq"), None),
        P(("dp", "seq"), None),
        P(("dp", "seq"), None),
        P(("dp", "seq"), None),
        P(None, ("dp", "seq")),
        P(("dp", "seq")),
        P(("dp", "seq"), None),
        P(("dp", "seq"), None),
        P(("dp", "seq"), None),
        P(("dp", "seq"), None),
    )
    return jax.shard_map(body, mesh=mesh, in_specs=in_specs, out_specs=out_specs, check_vma=False)
```

profile of v0, /device:TPU:0, one launch (start us, length us, event | category | flops | bytes accessed | tf_op | source)
XLA Modules:
  0.0 1376.7 jit_solution(14741874597036236309)
XLA Ops:
  15.2 70.3 %all-gather = bf16[32,24,8]{1,2,0:T(8,128)(2,1)S(1)} all-gather(bf16[1,24,8]{1,2,0:T(8,128)(2,1)S(1)} %convert_bitcast_fusion), channel_id=1, replica_groups=mesh['dp'=8,'seq'=4] {'dp','seq'}, dimensions={0}, use_global_device_ids=true | all-gather | bytes 12672 | tf_op jit(solution)/shard_map/all_gather | solution.py:98
  87.1 4.5 fusion.178
  95.0 4.2 fusion.179
  102.8 2.4 slice.169
  109.0 38.6 %all-reduce = bf16[3072]{0:T(1024)(128)(2,1)S(1)} all-reduce(bf16[3072]{0:T(1024)(128)(2,1)S(1)} %dynamic-update-slice), channel_id=1, replica_groups=mesh['dp'=8,'seq'=4] {'dp','seq'}, use_global_device_ids=true, to_apply=%add | all-reduce | flops 3072 | bytes 12288
  155.6 6.8 fusion.180
  162.4 22.0 %all-gather.14.cloned.1.call-done = bf16[2,1024,768]{2,1,0:T(8,128)(2,1)} async-done(((bf16[2,256,768]{2,1,0:T(8,128)(2,1)}), bf16[2,1024,768]{2,1,0:T(8,128)(2,1)}) %all-gather.14.cloned.1.call-update) | async-done | bytes 3145744 | tf_op jit(solution)/shard_map/all_gather | solution.py:141
  184.4 3.2 copy.125
  187.6 13.2 fusion.4
  200.9 12.0 exponential_reduce_fusion.1
  212.9 17.1 %all-gather.12.cloned.1.call-done = bf16[2,1024,768]{2,1,0:T(8,128)(2,1)} async-done(((bf16[2,256,768]{2,1,0:T(8,128)(2,1)}), bf16[2,1024,768]{2,1,0:T(8,128)(2,1)}) %all-gather.12.cloned.1.call-update) | async-done | bytes 3145744 | tf_op jit(solution)/shard_map/all_gather | solution.py:144
  230.0 3.2 copy.123
  233.2 13.3 fusion.78
  248.4 27.7 %all-gather.22.cloned.1.call-done = bf16[2,1024,768]{2,1,0:T(8,128)(2,1)} async-done(((bf16[2,256,768]{2,1,0:T(8,128)(2,1)}), bf16[2,1024,768]{2,1,0:T(8,128)(2,1)}) %all-gather.22.cloned.1.call-update) | async-done | bytes 3145744 | tf_op jit(solution)/shard_map/all_gather | solution.py:144
  276.1 3.2 copy.128
  279.3 42.4 %all-gather.24.cloned.1.call-done = bf16[2,1024,768]{2,1,0:T(8,128)(2,1)} async-done(((bf16[2,256,768]{2,1,0:T(8,128)(2,1)}), bf16[2,1024,768]{2,1,0:T(8,128)(2,1)}) %all-gather.24.cloned.1.call-update) | async-done | bytes 3145744 | tf_op jit(solution)/shard_map/all_gather | solution.py:141
  321.7 4.6 copy.130
  326.3 15.0 %fusion.5 = (f32[2,12,256]{2,1,0:T(8,128)S(1)}, f32[2,12,256,1024]{3,2,1,0:T(8,128)}) fusion(pred[2,256,1024]{2,1,0:T(8,128)(4,1)} %get-tuple-element.133, bf16[2,1024,12,64]{1,3,2,0:T(8,128)(2,1)} %bitcast.204, bf16[2,256,12,64]{1,0,3,2:T(2,128)(2,1)} %reshape.385), kind=kOutput, calls=%fused_computation.15 | convolution fusion | flops 824174592 | bytes 29646848 | tf_op jit(solution)/shard_map/sqhd,skhd->shqk/dot_general | solution.py:54
  341.3 11.8 exponential_reduce_fusion
  353.1 11.4 fusion.79
  366.4 12.8 all-gather.16.cloned.1.call-done
  379.2 2.8 fusion.173
  385.6 59.5 %all-gather.18.cloned.1.call-done = bf16[768,3072]{1,0:T(8,128)(2,1)} async-done(((bf16[24,3072]{1,0:T(8,128)(2,1)}), bf16[768,3072]{1,0:T(8,128)(2,1)}) %all-gather.18.cloned.1.call-update) | async-done | bytes 4718608 | tf_op jit(solution)/shard_map/all_gather | solution.py:96
  445.1 8.2 fusion.153
  453.4 4.8 fusion.154
  458.2 15.6 %convert_reduce_fusion.1 = (f32[3072]{0:T(1024)}, bf16[512,3072]{1,0:T(8,128)(2,1)}, f32[3072]{0:T(1024)}, bf16[512,3072]{1,0:T(8,128)(2,1)S(1)}) fusion(f32[512,3072]{1,0:T(8,128)} %fusion.153, f32[3072]{0:T(1024)S(1)} %convert_element_type.214, f32[512,3072]{1,0:T(8,128)} %fusion.180, f32[512,3072]{1,0:T(8,128)} %fusion.154, ...), kind=kOutput, calls=%fused_computation.41 | convolution fusion | flops 2488264704 | bytes 30707712 | tf_op jit(solution)/shard_map/dot_general | solution.py:31
  473.8 8.1 multiply_reduce_fusion.3
  481.9 7.6 convert_reduce_fusion.9
  496.0 2.9 reshape.397
  498.9 13.4 fusion.89
  512.3 6.7 copy.148
  519.0 3.5 convolution_convert_fusion.1
  524.8 2.9 reshape.391
  527.7 13.9 %fusion.93 = f32[2,12,64,1024]{3,2,1,0:T(8,128)} fusion(bf16[2,256,12,64]{1,0,3,2:T(2,128)(2,1)} %reshape.391, f32[2,12,256]{2,1,0:T(8,128)S(1)} %log_add_fusion.1, f32[2,12,256,1024]{3,2,1,0:T(8,128)} %get-tuple-element.160, pred[2,256,1024]{2,1,0:T(8,128)(4,1)} %get-tuple-element.132), kind=kOutput, calls=%fused_computation.146 | convolution fusion | flops 830472192 | bytes 32792576 | tf_op jit(solution)/shard_map/shqk,sqhd->skhd/dot_general | solution.py:203
  541.6 6.7 copy.139
  548.5 14.2 %fusion.95 = f32[2,12,256,1024]{3,2,1,0:T(8,128)} fusion(bf16[2,1024,12,64]{1,3,2,0:T(8,128)(2,1)} %bitcast.201, bf16[2,256,12,64]{1,0,3,2:T(2,128)(2,1)} %reshape.391), kind=kOutput, calls=%fused_computation.148 | convolution fusion | flops 805306368 | bytes 29097984 | tf_op jit(solution)/shard_map/sqhd,skhd->shqk/dot_general | solution.py:185
  562.7 54.6 %broadcast_multiply_fusion.1 = f32[2,12,64,1024]{3,2,1,0:T(8,128)} fusion(f32[2,12,256,1024]{3,2,1,0:T(8,128)} %fusion.95, pred[2,256,1024]{2,1,0:T(8,128)(4,1)} %get-tuple-element.132, f32[2,12,256]{2,1,0:T(8,128)S(1)} %log_add_fusion.1, f32[2,12,256,1024]{3,2,1,0:T(8,128)} %get-tuple-element.160, bf16[2,256,12,64]{1,0,3,2:T(2,128)(2,1)} %reshape.377), kind=kOutput, calls=%fused_computation.49 | convolution fusion | flops 876092416 | bytes 57958400 | tf_op jit(solution)/shard_map/shqk,sqhd->skhd/dot_general | solution.py:198
  617.2 6.9 copy.137
  624.2 11.8 fusion.91
  636.0 54.1 %broadcast_multiply_fusion = f32[2,12,64,1024]{3,2,1,0:T(8,128)} fusion(f32[2,12,256,1024]{3,2,1,0:T(8,128)} %fusion.91, pred[2,256,1024]{2,1,0:T(8,128)(4,1)} %get-tuple-element.133, f32[2,12,256]{2,1,0:T(8,128)S(1)} %log_add_fusion, f32[2,12,256,1024]{3,2,1,0:T(8,128)} %get-tuple-element.156, bf16[2,256,12,64]{1,0,3,2:T(2,128)(2,1)} %reshape.385), kind=kOutput, calls=%fused_computation.48 | convolution fusion | flops 876092416 | bytes 57958400 | tf_op jit(solution)/shard_map/shqk,sqhd->skhd/dot_general | solution.py:198
  690.0 6.8 copy.146
  698.8 52.6 %convert_reduce_fusion.11 = (f32[12,64]{1,0:T(8,128)S(1)}, bf16[2,256,12,64]{1,3,2,0:T(8,128)(2,1)}) fusion(bf16[2,1024,12,64]{1,3,2,0:T(8,128)(2,1)S(1)} %bitcast.203, f32[2,12,256,1024]{3,2,1,0:T(8,128)} %fusion.95, pred[2,256,1024]{2,1,0:T(8,128)(4,1)} %get-tuple-element.132, f32[2,12,256]{2,1,0:T(8,128)S(1)} %log_add_fusion.1, ...), kind=kOutput, calls=%fused_computation.110 | convolution fusion | flops 876091648 | bytes 54815744 | tf_op jit(solution)/shard_map/shqk,skhd->sqhd/dot_general | solution.py:193
  754.5 53.2 %convert_reduce_fusion.7 = (f32[12,64]{1,0:T(8,128)S(1)}, bf16[2,256,12,64]{1,3,2,0:T(8,128)(2,1)}) fusion(bf16[2,1024,12,64]{1,3,2,0:T(8,128)(2,1)} %bitcast.205, f32[2,12,256,1024]{3,2,1,0:T(8,128)} %fusion.91, pred[2,256,1024]{2,1,0:T(8,128)(4,1)} %get-tuple-element.133, f32[2,12,256]{2,1,0:T(8,128)S(1)} %log_add_fusion, ...), kind=kOutput, calls=%fused_computation.105 | convolution fusion | flops 876091648 | bytes 54815744 | tf_op jit(solution)/shard_map/shqk,skhd->sqhd/dot_general | solution.py:193
  815.3 2.9 fusion.152
  818.4 6.7 fusion.155
  825.2 5.8 convolution_add_fusion.2
  831.0 8.7 convolution_add_fusion.1
  839.7 2.4 convert_reduce_fusion.6
  844.4 2.4 convert_reduce_fusion.10
  849.0 2.4 convert_element_type.235
  858.4 4.0 fusion.87
  862.5 5.0 convolution_add_fusion
  869.5 9.3 add_convert_fusion.2
  878.9 8.8 add_convert_fusion
  891.4 4.4 fusion.73
  895.9 41.1 %all-reduce.2 = (f32[8,768]{1,0:T(8,128)S(1)}, f32[3072]{0:T(1024)S(1)}) all-reduce(f32[8,768]{1,0:T(8,128)S(1)} %add.415, f32[3072]{0:T(1024)S(1)} %add.416), channel_id=1, replica_groups=mesh['dp'=8,'seq'=4] {'dp','seq'}, use_global_device_ids=true, to_apply=%region_46.47 | all-reduce | flops 9216 | bytes 73728 | tf_op jit(solution)/shard_map/psum | solution.py:241
  939.2 4.3 fusion.72
  943.5 354.4 %all-reduce.6.cloned.1.call-done = (f32[768,2304]{1,0:T(8,128)}, f32[768,768]{1,0:T(8,128)}, f32[768,3072]{1,0:T(8,128)}, f32[3072,768]{1,0:T(8,128)}) async-done(((f32[768,2304]{1,0:T(8,128)}, f32[768,768]{1,0:T(8,128)}, f32[768,3072]{1,0:T(8,128)}, f32[3072,768]{1,0:T(8,128)}), (f32[768,2304]{1,0:T(8,128)}, f32[768,768]{1,0:T(8,128)}, f32[768,3072]{1,0:T(8,128)}, ...) | async-done | bytes 28311568 | tf_op jit(solution)/shard_map/psum | solution.py:241
  1297.9 2.7 multiply_reduce_fusion.17
  1300.6 2.8 multiply_reduce_fusion.15
  1305.7 2.7 multiply_reduce_fusion.14
  1308.4 3.3 concatenate.22
  1311.7 3.3 concatenate.23
  1317.0 40.2 %all-reduce.1 = (f32[13]{0:T(128)S(1)}, f32[13]{0:T(128)S(1)}) all-reduce(f32[13]{0:T(128)S(1)} %concatenate.23, f32[13]{0:T(128)S(1)} %concatenate.22), channel_id=1, replica_groups=mesh['dp'=8,'seq'=4] {'dp','seq'}, use_global_device_ids=true, to_apply=%region_63.64 | all-reduce | flops 26 | bytes 208 | tf_op jit(solution)/shard_map/psum | solution.py:283
  (353 shorter events, 89.8 us)
Async XLA Ops:
  7.2 79.2 %copy-start = (bf16[4,256,768]{2,1,0:T(8,128)(2,1)S(1)}, bf16[4,256,768]{2,1,0:T(8,128)(2,1)}, u32[]{:S(2)}) copy-start(bf16[4,256,768]{2,1,0:T(8,128)(2,1)} %param.21) | copy-start | bytes 4718596
  7.2 79.9 %all-gather.10.cloned.1.call-start = ((), (), s32[]{:S(2)}) async-start(), calls=%async_computation.4 | async-start | bytes 3649536 | tf_op jit(solution)/shard_map/all_gather | solution.py:94
  9.0 146.6 %all-gather.20.cloned.1.call-start = ((), (), s32[]{:S(2)}) async-start(), calls=%async_computation.9 | async-start | bytes 4866048 | tf_op jit(solution)/shard_map/all_gather | solution.py:97
  10.7 173.7 %all-gather.14.cloned.1.call-start = ((), (), s32[]{:S(2)}) async-start(), calls=%async_computation.6 | async-start | bytes 3932160 | tf_op jit(solution)/shard_map/all_gather | solution.py:141
  12.4 79.2 %copy-start.60 = (f32[1,2,2,128]{3,1,2,0:T(2,128)}, f32[1,2,2,128]{3,1,2,0:T(2,128)S(1)}, u32[]{:S(2)}) copy-start(f32[1,2,2,128]{3,1,2,0:T(2,128)S(1)} %copy.151) | copy-start | bytes 6148
  12.4 79.2 %copy-start.62 = (f32[1,2,2,128]{3,1,2,0:T(2,128)}, f32[1,2,2,128]{3,1,2,0:T(2,128)S(1)}, u32[]{:S(2)}) copy-start(f32[1,2,2,128]{3,1,2,0:T(2,128)S(1)} %copy.154) | copy-start | bytes 6148
  14.4 77.2 %copy-start.64 = (f32[1,2,2,128]{3,1,2,0:T(2,128)}, f32[1,2,2,128]{3,1,2,0:T(2,128)S(1)}, u32[]{:S(2)}) copy-start(f32[1,2,2,128]{3,1,2,0:T(2,128)S(1)} %copy.152) | copy-start | bytes 6148
  14.5 77.2 %copy-start.66 = (f32[1,2,2,128]{3,1,2,0:T(2,128)}, f32[1,2,2,128]{3,1,2,0:T(2,128)S(1)}, u32[]{:S(2)}) copy-start(f32[1,2,2,128]{3,1,2,0:T(2,128)S(1)} %copy.155) | copy-start | bytes 6148
  86.4 366.9 %copy-start.51 = (f32[768]{0:T(1024)}, f32[768]{0:T(1024)S(1)}, u32[]{:S(2)}) copy-start(f32[768]{0:T(1024)S(1)} %get-tuple-element.64) | copy-start | bytes 9220
  86.4 403.1 %copy-start.49 = (f32[768]{0:T(1024)}, f32[768]{0:T(1024)S(1)}, u32[]{:S(2)}) copy-start(f32[768]{0:T(1024)S(1)} %get-tuple-element.62) | copy-start | bytes 9220
  87.1 7.9 copy-start.25
  94.9 135.1 %all-gather.12.cloned.1.call-start = ((), (), s32[]{:S(2)}) async-start(), calls=%async_computation.5 | async-start | bytes 3932160 | tf_op jit(solution)/shard_map/all_gather | solution.py:144
  99.1 6.9 copy-start.35
  102.2 45.4 %copy-start.68 = (s32[4,1024]{1,0:T(4,128)S(1)}, s32[4,1024]{1,0:T(4,128)}, u32[]{:S(2)}) copy-start(s32[4,1024]{1,0:T(4,128)} %param.23) | copy-start | bytes 49156
  102.2 45.6 %copy-start.10 = (bf16[4,256,768]{2,1,0:T(8,128)(2,1)S(1)}, bf16[4,256,768]{2,1,0:T(8,128)(2,1)}, u32[]{:S(2)}) copy-start(bf16[4,256,768]{2,1,0:T(8,128)(2,1)} %param.22) | copy-start | bytes 4718596
  102.2 173.9 %all-gather.22.cloned.1.call-start = ((), (), s32[]{:S(2)}) async-start(), calls=%async_computation.10 | async-start | bytes 3932160 | tf_op jit(solution)/shard_map/all_gather | solution.py:144
  102.8 218.9 %all-gather.24.cloned.1.call-start = ((), (), s32[]{:S(2)}) async-start(), calls=%async_computation.11 | async-start | bytes 3932160 | tf_op jit(solution)/shard_map/all_gather | solution.py:141
  105.3 273.9 %all-gather.16.cloned.1.call-start = ((), (), s32[]{:S(2)}) async-start(), calls=%async_computation.7 | async-start | bytes 1216512 | tf_op jit(solution)/shard_map/all_gather | solution.py:95
  106.0 339.1 %all-gather.18.cloned.1.call-start = ((), (), s32[]{:S(2)}) async-start(), calls=%async_computation.8 | async-start | bytes 4866048 | tf_op jit(solution)/shard_map/all_gather | solution.py:96
  106.8 732.9 %reduce-scatter.11.cloned.1.call-start = ((), (), s32[]{:S(2)}) async-start(), calls=%async_computation.15 | async-start | bytes 7864320 | tf_op jit(solution)/shard_map/reduce_scatter | solution.py:213
  147.5 310.6 %copy-start.72 = (f32[3072]{0:T(1024)}, f32[3072]{0:T(1024)S(1)}, u32[]{:S(2)}) copy-start(f32[3072]{0:T(1024)S(1)} %convert_element_type.214) | copy-start | bytes 36868
  148.8 13.5 copy-start.31
  187.6 13.3 copy-start.8
  187.6 13.2 copy-start.15
  233.2 13.3 copy-start.2
  326.3 15.0 %copy-start.14 = (pred[2,256,1024]{2,1,0:T(8,128)(4,1)S(1)}, pred[2,256,1024]{2,1,0:T(8,128)(4,1)}, u32[]{:S(2)}) copy-start(pred[2,256,1024]{2,1,0:T(8,128)(4,1)} %get-tuple-element.133) | copy-start | bytes 1572868
  382.0 99.8 %copy-start.76 = (f32[512]{0:T(512)}, f32[512]{0:T(512)S(1)}, u32[]{:S(2)}) copy-start(f32[512]{0:T(512)S(1)} %broadcast_multiply_fusion.11) | copy-start | bytes 6148
  384.1 105.4 %copy-start.53 = (f32[512]{0:T(512)}, f32[512]{0:T(512)S(1)}, u32[]{:S(2)}) copy-start(f32[512]{0:T(512)S(1)} %broadcast_multiply_fusion.10) | copy-start | bytes 6148
  385.6 96.3 %copy-start.86 = (f32[512]{0:T(512)}, f32[512]{0:T(512)S(1)}, u32[]{:S(2)}) copy-start(f32[512]{0:T(512)S(1)} %add_rsqrt_fusion.1) | copy-start | bytes 6148
  385.6 103.9 %copy-start.58 = (f32[512]{0:T(512)}, f32[512]{0:T(512)S(1)}, u32[]{:S(2)}) copy-start(f32[512]{0:T(512)S(1)} %add_rsqrt_fusion) | copy-start | bytes 6148
  445.1 8.3 copy-start.4
  445.1 8.3 copy-start.94
  445.1 13.1 slice-start
  458.2 15.6 %copy-start.38 = (f32[512,768]{1,0:T(8,128)S(1)}, f32[512,768]{1,0:T(8,128)}, u32[]{:S(2)}) copy-start(f32[512,768]{1,0:T(8,128)} %copy-done.37) | copy-start | bytes 4718596
  473.8 8.1 copy-start.27
  481.9 7.7 copy-start.32
  519.0 325.4 %reduce-scatter.7.cloned.1.call-start = ((), (), s32[]{:S(2)}) async-start(), calls=%async_computation.13 | async-start | bytes 7864320 | tf_op jit(solution)/shard_map/reduce_scatter | solution.py:213
  548.4 300.6 %reduce-scatter.5.cloned.1.call-start = ((), (), s32[]{:S(2)}) async-start(), calls=%async_computation.12 | async-start | bytes 7864320 | tf_op jit(solution)/shard_map/reduce_scatter | solution.py:207
  624.1 229.6 %reduce-scatter.9.cloned.1.call-start = ((), (), s32[]{:S(2)}) async-start(), calls=%async_computation.14 | async-start | bytes 7864320 | tf_op jit(solution)/shard_map/reduce_scatter | solution.py:207
  696.9 601.0 %all-reduce.6.cloned.1.call-start = ((), (), s32[]{:S(2)}) async-start(), calls=%async_computation.16 | async-start | bytes 56623104 | tf_op jit(solution)/shard_map/psum | solution.py:241
  754.5 56.5 %copy-start.11 = (f32[512,768]{1,0:T(8,128)S(1)}, f32[512,768]{1,0:T(8,128)}, u32[]{:S(2)}) copy-start(f32[512,768]{1,0:T(8,128)} %get-tuple-element.117) | copy-start | bytes 4718596
  818.3 6.8 copy-start.5
  818.3 6.8 copy-start.28
  818.4 6.8 copy-start.54
  818.4 6.8 copy-start.59
  818.4 12.6 slice-start.2
  878.9 10.1 copy-start.20
  878.9 10.1 copy-start.22
  878.9 10.1 copy-start.24
  878.9 10.1 copy-start.95
  891.3 45.7 %copy-start.89 = (f32[96]{0:T(128)S(1)}, f32[96]{0:T(128)}, u32[]{:S(2)}) copy-start(f32[96]{0:T(128)} %param.39) | copy-start | bytes 1156
  891.3 45.7 %copy-start.92 = (f32[96]{0:T(128)S(1)}, f32[96]{0:T(128)}, u32[]{:S(2)}) copy-start(f32[96]{0:T(128)} %param.41) | copy-start | bytes 1156
  891.3 45.7 %copy-start.93 = (f32[96]{0:T(128)S(1)}, f32[96]{0:T(128)}, u32[]{:S(2)}) copy-start(f32[96]{0:T(128)} %param.40) | copy-start | bytes 1156
  891.3 46.9 %copy-start.57 = (f32[8,24]{1,0:T(8,128)S(1)}, f32[8,24]{1,0:T(8,128)}, u32[]{:S(2)}) copy-start(f32[8,24]{1,0:T(8,128)} %param.36) | copy-start | bytes 2308
  891.4 46.9 %copy-start.84 = (f32[8,24]{1,0:T(8,128)S(1)}, f32[8,24]{1,0:T(8,128)}, u32[]{:S(2)}) copy-start(f32[8,24]{1,0:T(8,128)} %param.38) | copy-start | bytes 2308
  891.4 46.9 %copy-start.85 = (f32[8,24]{1,0:T(8,128)S(1)}, f32[8,24]{1,0:T(8,128)}, u32[]{:S(2)}) copy-start(f32[8,24]{1,0:T(8,128)} %param.37) | copy-start | bytes 2308
  939.1 422.5 %copy-start.69 = (f32[8,24]{1,0:T(8,128)}, f32[8,24]{1,0:T(8,128)S(1)}, u32[]{:S(2)}) copy-start(f32[8,24]{1,0:T(8,128)S(1)} %get-tuple-element.93) | copy-start | bytes 2308
  939.1 422.5 %copy-start.70 = (f32[8,24]{1,0:T(8,128)}, f32[8,24]{1,0:T(8,128)S(1)}, u32[]{:S(2)}) copy-start(f32[8,24]{1,0:T(8,128)S(1)} %get-tuple-element.94) | copy-start | bytes 2308
  939.1 364.3 %copy-start.48 = (f32[24,768]{1,0:T(8,128)S(1)}, f32[24,768]{1,0:T(8,128)}, u32[]{:S(2)}) copy-start(f32[24,768]{1,0:T(8,128)} %param.27) | copy-start | bytes 221188
  939.2 366.5 %copy-start.34 = (f32[96,768]{1,0:T(8,128)S(1)}, f32[96,768]{1,0:T(8,128)}, u32[]{:S(2)}) copy-start(f32[96,768]{1,0:T(8,128)} %param.33) | copy-start | bytes 884740
  943.5 371.6 %copy-start.12 = (f32[512,768]{1,0:T(8,128)S(1)}, f32[512,768]{1,0:T(8,128)}, u32[]{:S(2)}) copy-start(f32[512,768]{1,0:T(8,128)} %get-tuple-element.126) | copy-start | bytes 4718596
  943.5 371.6 %copy-start.13 = (f32[512,768]{1,0:T(8,128)S(1)}, f32[512,768]{1,0:T(8,128)}, u32[]{:S(2)}) copy-start(f32[512,768]{1,0:T(8,128)} %get-tuple-element.127) | copy-start | bytes 4718596
  1303.4 57.7 %copy-start.90 = (f32[96]{0:T(128)S(1)}, f32[96]{0:T(128)}, u32[]{:S(2)}) copy-start(f32[96]{0:T(128)} %param.39) | copy-start | bytes 1156
  1303.4 57.7 %copy-start.91 = (f32[96]{0:T(128)S(1)}, f32[96]{0:T(128)}, u32[]{:S(2)}) copy-start(f32[96]{0:T(128)} %get-tuple-element.89) | copy-start | bytes 1156
  (54 other events, 170.4 us)
Sparse Core Ops, SparseCore 0:
  11.5 62.8 all-gather.9
  77.8 62.6 all-gather.19
  142.4 41.9 all-gather.13
  186.1 43.8 all-gather.11
  232.3 43.8 all-gather.21
  277.8 43.8 all-gather.23
  325.2 53.9 all-gather.15
  382.7 62.3 all-gather.17
  519.1 68.3 reduce-scatter.10
  590.3 70.1 reduce-scatter.6
  663.5 70.0 reduce-scatter.4
  736.4 70.1 reduce-scatter.8
  867.7 430.1 all-reduce.5
where the time goes:
time: 1380 us
  waiting for transfers between devices  537 us (39%)
  matrix products  451 us (33%)
  blocking collectives  190 us (14%)
  local copies, waits for them, and re-layouts  99.2 us (7%)
  other arithmetic  79.9 us (6%)
  between operations  18.9 us (1%)
    psum x1, waiting for transfers between devices, body(): lax.psum((all_grads[0], all_grads[1], all_grads[2], all_grads[3], all_gra...  354 us
    dot_general x2, matrix products, body(): jnp.einsum('shqk,sqhd->skhd', score_grad, query_heads, preferred_element_...  109 us
    dot_general x2, matrix products, body(): jnp.einsum('shqk,skhd->sqhd', score_grad, key_heads, preferred_element_ty...  106 us
    all_gather x1, blocking collectives, body(): lax.all_gather(vectors.astype(brain), ('dp', 'seq'), axis=1, tiled=True)  70.3 us
    all_gather x2, waiting for transfers between devices, body(): lax.all_gather(key_local.reshape(seq_count, pos_count, model_width), 'seq...  64.4 us
    all_gather x1, waiting for transfers between devices, body(): lax.all_gather(w_up.astype(brain), ('dp', 'seq'), axis=0, tiled=True)  59.5 us
    dot_general x8, matrix products, times_transposed(): lax.dot_general(left_side, right_side, (((1,), (1,)), ((), ())), preferre...  49.7 us
    all_gather x2, waiting for transfers between devices, body(): lax.all_gather(value_local.reshape(seq_count, pos_count, model_width), 's...  44.8 us
  transfers between devices with their start and end apart: 13, of which 7 were waited for; matrix products, arithmetic and copies ran while one was open for 37% of the time, Pallas kernels for 0%

commit v1 on v0

v1 whole, which is shorter than its diff:
```python
import jax
import jax.numpy as jnp
from jax import lax
from jax.experimental import pallas as pl
from jax.experimental.pallas import tpu as pltpu
from jax.sharding import PartitionSpec as P

HEADS = 12
HEAD_DIM = 64
LONGEST = 512
QUERY_BLOCK = 256


BETA_ONE = 0.9
BETA_TWO = 0.999
ADAM_EPS = 1e-06
DECAY_RATE = 0.01
LEARN_RATE = 0.4
NORM_EPS = 1e-05
STEP_NUMBER = 10.0

BRAIN = jnp.bfloat16
FLOAT = jnp.float32


def matmul(left_side, right_side):
    return jnp.dot(left_side, right_side, preferred_element_type=FLOAT)


def inner_rows(left_side, right_side):
    return lax.dot_general(
        left_side, right_side, (((0,), (0,)), ((), ())), preferred_element_type=FLOAT
    )


def times_transposed(left_side, right_side):
    return lax.dot_general(
        left_side, right_side, (((1,), (1,)), ((), ())), preferred_element_type=FLOAT
    )


def gelu_tanh(values):
    return jax.nn.gelu(values, approximate=True)


def norm_forward(values, norm_gain, norm_shift):
    center = values - jnp.mean(values, axis=-1, keepdims=True)
    inverse = lax.rsqrt(jnp.mean(center * center, axis=-1, keepdims=True) + NORM_EPS)
    normed = center * inverse
    return (normed * norm_gain + norm_shift, normed, inverse)


def norm_backward(upstream, normed, inverse, norm_gain):
    scaled = upstream * norm_gain
    centered = scaled - jnp.mean(scaled, axis=-1, keepdims=True)
    return inverse * (centered - normed * jnp.mean(scaled * normed, axis=-1, keepdims=True))


def windows(length):
    return [
        (max(0, first - LONGEST), first + QUERY_BLOCK) for first in range(0, length, QUERY_BLOCK)
    ]


def fill_bias(seg_col, seg_row, bias, length):
    place = 0
    for index, (low, high) in enumerate(windows(length)):
        first = index * QUERY_BLOCK
        size = high - low
        keys = seg_col[0, low:high, :]
        queries = seg_row[0, :, first : first + QUERY_BLOCK]
        key_place = low + lax.broadcasted_iota(jnp.int32, (size, QUERY_BLOCK), 0)
        query_place = first + lax.broadcasted_iota(jnp.int32, (size, QUERY_BLOCK), 1)
        allowed = (keys == queries) & (key_place <= query_place)
        bias[place : place + size, :] = jnp.where(allowed, 0.0, -1000000000.0)
        place += size


def split_heads(pair):
    lane = lax.broadcasted_iota(jnp.int32, pair.shape, 1)
    zero = jnp.zeros_like(pair)
    return (jnp.where(lane < HEAD_DIM, pair, zero), jnp.where(lane < HEAD_DIM, zero, pair))


def attend_forward(seg_col, seg_row, q_ref, k_ref, v_ref, c_ref, lse_ref, bias):
    length = q_ref.shape[0]

    @pl.when(pl.program_id(1) == 0)
    def _():
        fill_bias(seg_col, seg_row, bias, length)

    v_turned = v_ref[...].T
    place = 0
    for index, (low, high) in enumerate(windows(length)):
        first = index * QUERY_BLOCK
        size = high - low
        queries = split_heads(q_ref[first : first + QUERY_BLOCK, :] * HEAD_DIM ** (-0.5))
        keys = k_ref[low:high, :]
        blocked = bias[place : place + size, :]
        parts = []
        for head in range(2):
            scores = times_transposed(keys, queries[head]) + blocked
            peak = jnp.max(scores, axis=0, keepdims=True)
            probs = jnp.exp(scores - peak)
            total = jnp.sum(probs, axis=0, keepdims=True)
            probs = (probs * (1.0 / total)).astype(BRAIN)
            lse_ref[0, 0, head : head + 1, first : first + QUERY_BLOCK] = peak + jnp.log(total)
            turned = v_turned[head * HEAD_DIM : (head + 1) * HEAD_DIM, low:high]
            parts.append(matmul(turned, probs))
        context = jnp.concatenate(parts, axis=0).T
        c_ref[first : first + QUERY_BLOCK, :] = context.astype(BRAIN)
        place += size


def attend_backward(
    seg_col, seg_row, q_ref, k_ref, v_ref, g_ref, lse_ref, out_ref, bias, key_sum, value_sum
):
    length = q_ref.shape[0]
    pair = pl.program_id(1)

    @pl.when(pair == 0)
    def _():
        fill_bias(seg_col, seg_row, bias, length)

    key_sum[...] = jnp.zeros_like(key_sum)
    value_sum[...] = jnp.zeros_like(value_sum)
    width = HEADS * HEAD_DIM
    k_turned = k_ref[...].T
    lanes = 2 * HEAD_DIM
    column = pl.multiple_of(pair * lanes, lanes)
    place = 0
    for index, (low, high) in enumerate(windows(length)):
        first = index * QUERY_BLOCK
        size = high - low
        rows = slice(first, first + QUERY_BLOCK)
        queries = split_heads(q_ref[rows, :] * HEAD_DIM ** (-0.5))
        grads = split_heads(g_ref[rows, :])
        keys = k_ref[low:high, :]
        values = v_ref[low:high, :]
        blocked = bias[place : place + size, :]
        all_probs = []
        all_scores = []
        parts = []
        for head in range(2):
            scores = times_transposed(keys, queries[head]) + blocked
            probs = jnp.exp(scores - lse_ref[0, 0, head : head + 1, rows])
            prob_grad = times_transposed(values, grads[head])
            row_dot = jnp.sum(probs * prob_grad, axis=0, keepdims=True)
            score_grad = (probs * (prob_grad - row_dot)).astype(BRAIN)
            all_probs.append(probs.astype(BRAIN))
            all_scores.append(score_grad)
            turned = k_turned[head * HEAD_DIM : (head + 1) * HEAD_DIM, low:high]
            parts.append(matmul(turned, score_grad))
        query_grad = jnp.concatenate(parts, axis=0).T * HEAD_DIM ** (-0.5)
        out_ref[rows, pl.ds(column, lanes)] = query_grad.astype(BRAIN)
        value_sum[low:high, :] += matmul(
            jnp.concatenate(all_probs, axis=1), jnp.concatenate(grads, axis=0)
        )
        key_sum[low:high, :] += matmul(
            jnp.concatenate(all_scores, axis=1), jnp.concatenate(queries, axis=0)
        )
        place += size
    out_ref[:, pl.ds(width + column, lanes)] = key_sum[...].astype(BRAIN)
    out_ref[:, pl.ds(2 * width + column, lanes)] = value_sum[...].astype(BRAIN)


def attention_specs(length):
    lanes = 2 * HEAD_DIM
    pairs = HEADS // 2
    spec = lambda shift: pl.BlockSpec((length, lanes), lambda r, j: (r, shift * pairs + j))
    segs = [
        pl.BlockSpec((1, length, 1), lambda r, j: (r, 0, 0)),
        pl.BlockSpec((1, 1, length), lambda r, j: (r, 0, 0)),
    ]
    lse = pl.BlockSpec((1, 1, 8, length), lambda r, j: (r, j, 0, 0))
    plain = pl.BlockSpec((length, lanes), lambda r, j: (r, j))
    bias = pltpu.VMEM((sum(high - low for low, high in windows(length)), QUERY_BLOCK), FLOAT)
    return segs, [spec(0), spec(1), spec(2)], plain, lse, bias


def attention_forward(segments, qkv, length):
    rows = segments.shape[0]
    segs, qkv_specs, plain, lse, bias = attention_specs(length)
    width = HEADS * HEAD_DIM
    return pl.pallas_call(
        attend_forward,
        grid=(rows, HEADS // 2),
        in_specs=segs + qkv_specs,
        out_specs=[plain, lse],
        out_shape=[
            jax.ShapeDtypeStruct((rows * length, width), BRAIN),
            jax.ShapeDtypeStruct((rows, HEADS // 2, 8, length), FLOAT),
        ],
        scratch_shapes=[bias],
        name="attend_forward",
        compiler_params=pltpu.CompilerParams(vmem_limit_bytes=48 * 1024 * 1024),
    )(segments[:, :, None], segments[:, None, :], qkv, qkv, qkv)


def attention_backward(segments, qkv, grads, lse_rows, length):
    rows = segments.shape[0]
    segs, qkv_specs, plain, lse, bias = attention_specs(length)
    width = HEADS * HEAD_DIM
    return pl.pallas_call(
        attend_backward,
        grid=(rows, HEADS // 2),
        in_specs=segs + qkv_specs + [plain, lse],
        out_specs=pl.BlockSpec((length, 3 * width), lambda r, j: (r, 0)),
        out_shape=jax.ShapeDtypeStruct((rows * length, 3 * width), BRAIN),
        scratch_shapes=[
            bias,
            pltpu.VMEM((length, 2 * HEAD_DIM), FLOAT),
            pltpu.VMEM((length, 2 * HEAD_DIM), FLOAT),
        ],
        name="attend_backward",
        compiler_params=pltpu.CompilerParams(vmem_limit_bytes=56 * 1024 * 1024),
    )(segments[:, :, None], segments[:, None, :], qkv, qkv, qkv, grads, lse_rows)


def lamb_parts(weight, first, second, grad, decay, corr_one, corr_two, axis):
    first_new = BETA_ONE * first + (1.0 - BETA_ONE) * grad
    second_new = BETA_TWO * second + (1.0 - BETA_TWO) * grad * grad
    update = first_new / corr_one / (jnp.sqrt(second_new / corr_two) + ADAM_EPS) + decay * weight
    weight_sq = jnp.reshape(jnp.sum(weight * weight, axis=axis), (-1,))
    update_sq = jnp.reshape(jnp.sum(update * update, axis=axis), (-1,))
    return (first_new, second_new, update, weight_sq, update_sq)


def body(
    tokens,
    cotangent,
    segment_ids,
    w_qkv,
    m_qkv,
    v_qkv,
    w_out,
    m_out,
    v_out,
    w_up,
    m_up,
    v_up,
    w_down,
    m_down,
    v_down,
    vectors,
    m_vectors,
    v_vectors,
    up_bias,
    m_up_bias,
    v_up_bias,
):
    both = ("dp", "seq")
    small = jnp.concatenate([vectors.reshape(-1), up_bias]).astype(BRAIN)
    small = lax.all_gather(small[None], both, axis=0, tiled=True)
    cut = vectors.size
    full_vectors = small[:, :cut].reshape(-1, vectors.shape[0], vectors.shape[1])
    vector_rows = full_vectors.transpose(1, 0, 2).reshape(vectors.shape[0], -1).astype(FLOAT)
    up_shift = small[:, cut:].reshape(-1).astype(FLOAT)
    full_qkv = lax.all_gather(w_qkv.astype(BRAIN), both, axis=0, tiled=True)
    full_out = lax.all_gather(w_out.astype(BRAIN), both, axis=0, tiled=True)
    full_up = lax.all_gather(w_up.astype(BRAIN), both, axis=0, tiled=True)
    full_down = lax.all_gather(w_down.astype(BRAIN), both, axis=0, tiled=True)

    width = tokens.shape[2]
    length = segment_ids.shape[1]
    token_rows = lax.all_to_all(tokens, "seq", split_axis=0, concat_axis=1, tiled=True)
    back_rows = lax.all_to_all(cotangent, "seq", split_axis=0, concat_axis=1, tiled=True)
    rows = token_rows.shape[0]
    segments = lax.dynamic_slice_in_dim(segment_ids, lax.axis_index("seq") * rows, rows, 0)
    count = rows * length
    token_part = token_rows.reshape(count, width).astype(FLOAT)
    back_part = back_rows.reshape(count, width)

    normed_one, plain_one, inverse_one = norm_forward(token_part, vector_rows[0], vector_rows[1])
    low_one = normed_one.astype(BRAIN)
    shifts = jnp.concatenate([vector_rows[4], jnp.zeros_like(vector_rows[4]), vector_rows[5]])
    qkv = (matmul(low_one, full_qkv) + shifts).astype(BRAIN)
    context, lse_rows = attention_forward(segments, qkv, length)
    resid_one = token_part + matmul(context, full_out) + vector_rows[6]
    normed_two, plain_two, inverse_two = norm_forward(resid_one, vector_rows[2], vector_rows[3])
    low_two = normed_two.astype(BRAIN)
    hidden_pre = matmul(low_two, full_up) + up_shift
    activated, gelu_pull = jax.vjp(gelu_tanh, hidden_pre)
    low_act = activated.astype(BRAIN)
    result = resid_one + matmul(low_act, full_down) + vector_rows[7]
    mixed = result.astype(BRAIN).reshape(rows, length, width)
    mixed = lax.all_to_all(mixed, "seq", split_axis=1, concat_axis=0, tiled=True)

    back_float = back_part.astype(FLOAT)
    grad_down = inner_rows(low_act, back_part)
    act_grad = times_transposed(back_part, full_down)
    hidden_grad = gelu_pull(act_grad)[0].astype(BRAIN)
    grad_up = inner_rows(low_two, hidden_grad)
    grad_up_bias = jnp.sum(hidden_grad.astype(FLOAT), axis=0)
    two_grad = times_transposed(hidden_grad, full_up)
    resid_grad = back_float + norm_backward(two_grad, plain_two, inverse_two, vector_rows[2])
    branch_grad = resid_grad.astype(BRAIN)
    grad_out = inner_rows(context, branch_grad)
    context_grad = times_transposed(branch_grad, full_out).astype(BRAIN)
    joined = attention_backward(segments, qkv, context_grad, lse_rows, length)
    grad_qkv = inner_rows(low_one, joined)
    one_grad = times_transposed(joined, full_qkv)
    input_rows = resid_grad + norm_backward(one_grad, plain_one, inverse_one, vector_rows[0])
    input_grad = input_rows.astype(BRAIN).reshape(rows, length, width)
    input_grad = lax.all_to_all(input_grad, "seq", split_axis=1, concat_axis=0, tiled=True)
    input_grad = input_grad.astype(FLOAT)
    joined_sum = jnp.sum(joined.astype(FLOAT), axis=0)
    grad_vectors = jnp.stack(
        [
            jnp.sum(one_grad * plain_one, axis=0),
            jnp.sum(one_grad, axis=0),
            jnp.sum(two_grad * plain_two, axis=0),
            jnp.sum(two_grad, axis=0),
            joined_sum[:width],
            joined_sum[2 * width :],
            jnp.sum(branch_grad.astype(FLOAT), axis=0),
            jnp.sum(back_float, axis=0),
        ]
    )
    devices = width // vectors.shape[1]
    small_grad = jnp.concatenate(
        [
            grad_vectors.reshape(vectors.shape[0], devices, -1).transpose(1, 0, 2).reshape(devices, -1),
            grad_up_bias.reshape(devices, -1),
        ],
        axis=1,
    )
    scatter = lambda value: lax.psum_scatter(value, both, scatter_dimension=0, tiled=True)
    small_share = scatter(small_grad)[0]
    shares = (
        scatter(grad_qkv),
        scatter(grad_out),
        scatter(grad_up),
        scatter(grad_down),
        small_share[:cut].reshape(vectors.shape),
        small_share[cut:],
    )
    count_float = jnp.asarray(STEP_NUMBER, FLOAT)
    corr_one = 1.0 - jnp.power(jnp.asarray(BETA_ONE, FLOAT), count_float)
    corr_two = 1.0 - jnp.power(jnp.asarray(BETA_TWO, FLOAT), count_float)
    weights = (w_qkv, w_out, w_up, w_down, vectors, up_bias)
    firsts = (m_qkv, m_out, m_up, m_down, m_vectors, m_up_bias)
    seconds = (v_qkv, v_out, v_up, v_down, v_vectors, v_up_bias)
    decays = (DECAY_RATE, DECAY_RATE, DECAY_RATE, DECAY_RATE, 0.0, 0.0)
    axes_list = (None, None, None, None, 1, None)
    parts = [
        lamb_parts(*each, corr_one, corr_two, axis)
        for *each, axis in zip(weights, firsts, seconds, shares, decays, axes_list)
    ]
    totals = lax.psum(
        jnp.stack(
            [
                jnp.concatenate([part[3] for part in parts]),
                jnp.concatenate([part[4] for part in parts]),
            ]
        ),
        both,
    )
    ratios = jnp.sqrt(totals[0]) / (jnp.sqrt(totals[1]) + ADAM_EPS)
    scales = [ratios[0], ratios[1], ratios[2], ratios[3], ratios[4:12][:, None], ratios[12]]
    news = [
        weight - LEARN_RATE * scale * part[2] for weight, scale, part in zip(weights, scales, parts)
    ]
    return (
        mixed,
        input_grad,
        *shares,
        *[part[0] for part in parts],
        *[part[1] for part in parts],
        *news,
        *[new.astype(BRAIN) for new in news[:4]],
    )


def solution(mesh):
    matrix = P(("dp", "seq"), None)
    rows = P("dp", "seq", None)
    vector = P(None, ("dp", "seq"))
    bias = P(("dp", "seq"))
    six = (matrix, matrix, matrix, matrix, vector, bias)
    in_specs = (rows, rows, P("dp", None)) + tuple(spec for spec in six for _ in range(3))
    out_specs = (rows, rows) + six * 4 + (matrix,) * 4
    return jax.shard_map(body, mesh=mesh, in_specs=in_specs, out_specs=out_specs, check_vma=False)
```

time: 1380 us -> 928 us (0.67)
  matrix products: 451 us -> 113 us
  waiting for transfers between devices: 537 us -> 394 us
  Pallas kernels: 0 us -> 62.6 us
  local copies, waits for them, and re-layouts: 99.2 us -> 61.8 us
  starting transfers between devices: 0.54 us -> 18.8 us
  other arithmetic: 79.9 us -> 65.8 us
    psum x1 -> x0, waiting for transfers between devices: 354 us -> none  [body(): lax.psum((all_grads[0], all_grads[1], all_grads[2], all_grads[3], all_gra...]
    dot_general x20 -> x4, matrix products: 364 us -> 36.2 us  [matmul(): return jnp.dot(left_side, right_side, preferred_element_type=FLOAT)]
    reduce_scatter x4, waiting for transfers between devices: 0.01 us -> 283 us  [body(): lax.psum_scatter(value, both, scatter_dimension=0, tiled=True)]
    all_gather x8 -> x4, waiting for transfers between devices: 182 us -> 110 us  [the longest x1 60.9 us: body(): full_down = lax.all_gather(w_down.astype(BRAIN), both, axis=0, tiled=True)]
    pallas_call x0 -> x2, Pallas kernels: none -> 62.6 us  [the longest x1 34.2 us: attention_backward(): pl.pallas_call(attend_backward, grid=(rows, HEADS // 2), in_specs=segs +...]
    psum x2 -> x1, blocking collectives: 81.3 us -> 39.6 us  [body(): lax.psum(jnp.stack([jnp.concatenate([part[3] for part in parts]), jnp.con...]
    unnamed x1, blocking collectives: 38.6 us -> 64.8 us
    unnamed x7 -> x5, other arithmetic: 0.71 us -> 22.9 us
  transfers between devices with their start and end apart: 13 -> 12, of which waited for: 7 -> 5; matrix products, arithmetic and copies ran while one was open for 37% -> 17% of each run, Pallas kernels for 0% -> 7%
where the time goes in v1:
time: 928 us; the launch traced here: 917 us
  waiting for transfers between devices  394 us (42%)
  blocking collectives  184 us (20%)
  matrix products  113 us (12%)
  other arithmetic  65.8 us (7%)
  Pallas kernels  62.6 us (7%)
  local copies, waits for them, and re-layouts  61.8 us (7%)
  starting transfers between devices  18.8 us (2%)
  between operations  18.3 us (2%)
    reduce_scatter x4, waiting for transfers between devices, body(): lax.psum_scatter(value, both, scatter_dimension=0, tiled=True)  283 us
    all_gather x1, blocking collectives, body(): small = lax.all_gather(small[None], both, axis=0, tiled=True)  79.1 us
    unnamed x1, blocking collectives  64.8 us
    all_gather x1, waiting for transfers between devices, body(): full_down = lax.all_gather(w_down.astype(BRAIN), both, axis=0, tiled=True)  60.9 us
    all_gather x1, waiting for transfers between devices, body(): full_up = lax.all_gather(w_up.astype(BRAIN), both, axis=0, tiled=True)  49.3 us
    dot_general x4, matrix products, times_transposed(): lax.dot_general(left_side, right_side, (((1,), (1,)), ((), ())), preferre...  41 us
    psum x1, blocking collectives, body(): lax.psum(jnp.stack([jnp.concatenate([part[3] for part in parts]), jnp.con...  39.6 us
    dot_general x4, matrix products, matmul(): return jnp.dot(left_side, right_side, preferred_element_type=FLOAT)  36.2 us
  transfers between devices with their start and end apart: 12, of which 5 were waited for; matrix products, arithmetic and copies ran while one was open for 17% of the time, Pallas kernels for 7%

profile of v1, /device:TPU:0, one launch (start us, length us, event | category | flops | bytes accessed | tf_op | source)
XLA Modules:
  0.0 917.3 jit_solution(4124774945958802811)
XLA Ops:
  7.3 1.6 convert_element_type.118
  8.9 1.5 convert_element_type.120
  10.5 1.6 convert_element_type.122
  12.2 5.2 all-to-all-start
  18.2 79.1 %all-gather = bf16[32,1,288]{2,1,0:T(2,128)(2,1)S(1)} all-gather(bf16[1,1,288]{2,1,0:T(2,128)(2,1)S(1)} %maximum_bitcast_fusion), channel_id=1, replica_groups=mesh['dp'=8,'seq'=4] {'dp','seq'}, dimensions={0}, use_global_device_ids=true | all-gather | bytes 19008 | tf_op jit(solution)/shard_map/all_gather | solution.py:254
  99.5 4.4 all-to-all-start.2
  103.9 2.1 copy.97
  107.0 9.2 %add_convert_fusion.q_ref.k_ref.v_ref = bf16[1024,2304]{1,0:T(8,128)(2,1)} fusion(bf16[768,2304]{1,0:T(8,128)(2,1)} %all-gather.6.cloned.1.call-done, f32[2304]{0:T(1024)S(1)} %pad_maximum_fusion.1, f32[1024,768]{0,1:T(8,128)} %copy.97, f32[768]{0:T(1024)S(1)} %add.203, f32[768]{0:T(1024)S(1)} %mul.457, f32[1024]{0:T(1024)S(1)} %bitcast.81, ...), kind=kOutput, calls=%fused_computation.12 | convolution fusion | flops 3632529408 | bytes 11426816 | tf_op jit(solution)/shard_map/dot_general | solution.py:27
  116.2 28.4 %attend_forward.1 = (bf16[1024,768]{1,0:T(8,128)(2,1)S(1)}, f32[1,6,8,1024]{3,2,1,0:T(8,128)S(1)}) custom-call(s32[1,1024,1]{2,1,0:T(8,128)S(1)} %copy.85.seg_col, s32[1,1,1024]{2,1,0:T(1,128)S(1)} %get-tuple-element.144.seg_row, bf16[1024,2304]{1,0:T(8,128)(2,1)} %add_convert_fusion.q_ref.k_ref.v_ref, bf16[1024,2304]{1,0:T(8,128)(2,1)} %add_convert_fusion.q_ref.k_ref.v_ref, ...), custom_call_target="tpu_custom_call" | custom-call | tf_op jit(solution)/shard_map/attend_forward/pallas_call | solution.py:185
  145.3 3.9 fusion.35
  149.2 1.7 copy-done.3
  151.3 49.3 %all-gather.10.cloned.1.call-done = bf16[768,3072]{1,0:T(8,128)(2,1)} async-done(((bf16[24,3072]{1,0:T(8,128)(2,1)}), bf16[768,3072]{1,0:T(8,128)(2,1)}) %all-gather.10.cloned.1.call-update) | async-done | bytes 4718608 | tf_op jit(solution)/shard_map/all_gather | solution.py:261
  200.7 11.3 %fusion.21 = f32[1024,3072]{1,0:T(8,128)} fusion(bf16[768,3072]{1,0:T(8,128)(2,1)} %all-gather.10.cloned.1.call-done, f32[1024,768]{0,1:T(8,128)} %copy-done.3, f32[768]{0:T(1024)S(1)} %add.213, f32[768]{0:T(1024)S(1)} %mul.463, f32[1024]{0:T(1024)S(1)} %add_rsqrt_fusion, f32[1024]{0:T(1024)S(1)} %broadcast_multiply_fusion.4), kind=kOutput, calls=%fused_computation.121 | convolution fusion | flops 4835770368 | bytes 20461568 | tf_op jit(solution)/shard_map/dot_general | solution.py:27
  212.0 13.3 %fusion.22 = f32[3072,768]{1,0:T(8,128)} fusion(bf16[1024,768]{1,0:T(8,128)(2,1)} %bitcast.7, f32[1024,3072]{1,0:T(8,128)} %fusion.21, f32[3072]{0:T(1024)S(1)} %reshape.350), kind=kOutput, calls=%fused_computation.122 | convolution fusion | flops 4863295488 | bytes 23605248 | tf_op jit(solution)/shard_map/dot_general | solution.py:31
  225.3 134.6 %reduce-scatter.11.cloned.1.call-done = f32[96,768]{1,0:T(8,128)} async-done(((f32[3072,768]{1,0:T(8,128)}), f32[96,768]{1,0:T(8,128)}) %reduce-scatter.11.cloned.1.call-update) | async-done | bytes 294928 | tf_op jit(solution)/shard_map/reduce_scatter | solution.py:328
  360.0 2.6 multiply_reduce_fusion.10
  362.6 2.2 copy.98
  364.9 60.9 %all-gather.12.cloned.1.call-done = bf16[3072,768]{1,0:T(8,128)(2,1)} async-done(((bf16[96,768]{1,0:T(8,128)(2,1)}), bf16[3072,768]{1,0:T(8,128)(2,1)}) %all-gather.12.cloned.1.call-update) | async-done | bytes 4718608 | tf_op jit(solution)/shard_map/all_gather | solution.py:262
  425.8 16.2 %convert_reduce_fusion = (f32[3072]{0:T(1024)S(1)}, bf16[1024,3072]{1,0:T(8,128)(2,1)S(1)}) fusion(f32[1024,3072]{1,0:T(8,128)} %fusion.21, f32[3072]{0:T(1024)S(1)} %reshape.350, bf16[1024,768]{1,0:T(8,128)(2,1)} %bitcast.7, bf16[3072,768]{1,0:T(8,128)(2,1)} %all-gather.12.cloned.1.call-done), kind=kOutput, calls=%fused_computation.9 | convolution fusion | flops 4904186880 | bytes 25190400 | tf_op jit(solution)/shard_map/dot_general | solution.py:37
  442.0 11.3 %fusion.37 = (f32[768]{0:T(1024)S(1)}, f32[1024,768]{1,0:T(8,128)}) fusion(bf16[1024,3072]{1,0:T(8,128)(2,1)S(1)} %get-tuple-element.160, bf16[768,3072]{1,0:T(8,128)(2,1)} %all-gather.10.cloned.1.call-done), kind=kOutput, calls=%fused_computation.131 | convolution fusion | flops 4832623616 | bytes 14158848 | tf_op jit(solution)/shard_map/dot_general | solution.py:37
  453.3 3.7 copy.89
  457.1 4.0 multiply_reduce_fusion
  461.8 1.4 convert_reduce_fusion.3
  463.2 1.6 copy-done.10
  464.8 2.9 fusion.15
  467.8 4.5 convolution_convert_fusion.g_ref
  472.3 34.2 %attend_backward.1 = bf16[1024,2304]{1,0:T(8,128)(2,1)} custom-call(s32[1,1024,1]{2,1,0:T(8,128)} %copy-done, s32[1,1,1024]{2,1,0:T(1,128)} %copy-done.2, bf16[1024,2304]{1,0:T(8,128)(2,1)} %add_convert_fusion.q_ref.k_ref.v_ref, bf16[1024,2304]{1,0:T(8,128)(2,1)} %add_convert_fusion.q_ref.k_ref.v_ref, bf16[1024,2304]{1,0:T(8,128)(2,1)} %add_convert_fusion.q_ref.k_ref.v_ref, ...), custom_call_target="tpu_custom_call" | custom-call | tf_op jit(solution)/shard_map/attend_backward/pallas_call | solution.py:204
  506.5 8.5 fusion.19
  515.1 1.8 copy-done.5
  516.9 10.9 %fusion.20 = f32[768,3072]{1,0:T(8,128)} fusion(bf16[1024,3072]{1,0:T(8,128)(2,1)} %copy-done.29, f32[1024,768]{0,1:T(8,128)S(1)} %copy-done.5, f32[768]{0:T(1024)S(1)} %add.213, f32[768]{0:T(1024)S(1)} %mul.463, f32[1024]{0:T(1024)S(1)} %add_rsqrt_fusion, f32[1024]{0:T(1024)S(1)} %broadcast_multiply_fusion.4), kind=kOutput, calls=%fused_computation.120 | convolution fusion | flops 4835770368 | bytes 18888704 | tf_op jit(solution)/shard_map/dot_general | solution.py:31
  527.9 1.7 convert_reduce_fusion.2
  529.7 11.8 %fusion.8 = bf16[1,1024,768]{1,2,0:T(8,128)(2,1)} fusion(f32[768]{0:T(1024)S(1)} %add.221, f32[1024,768]{0,1:T(8,128)S(1)} %copy-done.5, bf16[3072,768]{1,0:T(8,128)(2,1)} %all-gather.12.cloned.1.call-done, f32[1024,3072]{1,0:T(8,128)} %fusion.21, f32[3072]{0:T(1024)S(1)} %reshape.350), kind=kOutput, calls=%fused_computation.34 | convolution fusion | flops 4865654784 | bytes 22035456 | tf_op jit(solution)/shard_map/dot_general | solution.py:27
  541.5 7.2 copy.87
  549.2 11.4 %reduce.45 = bf16[1024,768]{1,0:T(8,128)(2,1)} reduce(bf16[1024,1,768]{2,1,0:T(2,128)(2,1)S(1)} %bitcast.72, bf16[]{:T(256)} %broadcast.177), dimensions={1}, to_apply=%bitcast.50.reduce_sub_computation | reduce | bytes 3145730
  560.6 3.7 reshape.404
  564.3 4.5 all-to-all-start.1
  568.9 9.0 fusion.36
  577.9 3.8 copy.91
  581.6 3.2 multiply_reduce_fusion.1
  584.8 0.9 copy-done.11
  585.7 2.1 fusion.7
  587.9 7.3 copy.92
  595.1 11.4 %reduce.46 = bf16[1024,768]{1,0:T(8,128)(2,1)} reduce(bf16[1024,1,768]{2,1,0:T(2,128)(2,1)S(1)} %bitcast.73, bf16[]{:T(256)} %broadcast.177), dimensions={1}, to_apply=%bitcast.48.reduce_sub_computation | reduce | bytes 3145730
  606.5 3.7 reshape.402
  610.5 3.1 convert_reduce_fusion.1
  613.8 4.4 all-to-all-start.3
  618.9 64.8 %all-reduce = f32[32,288]{1,0:T(8,128)S(1)} all-reduce(f32[32,288]{1,0:T(8,128)S(1)} %pad_maximum_fusion), channel_id=6, replica_groups=mesh['dp'=8,'seq'=4] {'dp','seq'}, use_global_device_ids=true, to_apply=%region_20.0.clone | all-reduce | flops 9216 | bytes 73728
  683.9 1.2 multiply_reduce_fusion.18
  685.2 3.1 reshape.405
  688.3 1.4 copy.100
  689.7 3.1 reshape.403
  692.9 2.3 multiply_reduce_fusion.15
  695.1 9.6 %reduce-scatter.5.cloned.1.call-done = f32[24,2304]{1,0:T(8,128)} async-done(((f32[768,2304]{1,0:T(8,128)}), f32[24,2304]{1,0:T(8,128)}) %reduce-scatter.5.cloned.1.call-update) | async-done | bytes 221200 | tf_op jit(solution)/shard_map/reduce_scatter | solution.py:328
  704.8 2.8 multiply_reduce_fusion.13
  707.6 139.0 %reduce-scatter.9.cloned.1.call-done = f32[24,3072]{1,0:T(8,128)} async-done(((f32[768,3072]{1,0:T(8,128)}), f32[24,3072]{1,0:T(8,128)}) %reduce-scatter.9.cloned.1.call-update) | async-done | bytes 294928 | tf_op jit(solution)/shard_map/reduce_scatter | solution.py:328
  846.5 2.8 multiply_reduce_fusion.11
  849.3 3.3 concatenate.34
  852.6 3.3 concatenate.33
  856.0 1.9 copy.101
  857.8 39.6 %psum.7 = f32[2,13]{1,0:T(2,128)S(1)} all-reduce(f32[2,13]{1,0:T(2,128)S(1)} %pad_maximum_fusion.2), channel_id=1, replica_groups=mesh['dp'=8,'seq'=4] {'dp','seq'}, use_global_device_ids=true, to_apply=%region_33.0 | all-reduce | flops 26 | bytes 208 | tf_op jit(solution)/shard_map/psum | solution.py:350
  901.9 2.0 fusion.26
  903.9 1.6 fusion.25
  905.5 2.0 fusion.24
  907.5 2.1 fusion.23
  (144 shorter events, 10.0 us)
Async XLA Ops:
  7.2 10.2 %copy-start.17 = (f32[8,24]{1,0:T(8,128)S(1)}, f32[8,24]{1,0:T(8,128)}, u32[]{:S(2)}) copy-start(f32[8,24]{1,0:T(8,128)} %param.36) | copy-start | bytes 2308
  7.2 10.3 %copy-start.24 = (f32[96]{0:T(128)S(1)}, f32[96]{0:T(128)}, u32[]{:S(2)}) copy-start(f32[96]{0:T(128)} %param.39) | copy-start | bytes 1156
  7.2 99.7 %all-gather.6.cloned.1.call-start = ((), (), s32[]{:S(2)}) async-start(), calls=%async_computation.8 | async-start | bytes 3649536 | tf_op jit(solution)/shard_map/all_gather | solution.py:259
  8.9 136.4 %all-gather.8.cloned.1.call-start = ((), (), s32[]{:S(2)}) async-start(), calls=%async_computation.9 | async-start | bytes 1216512 | tf_op jit(solution)/shard_map/all_gather | solution.py:260
  10.5 190.2 %all-gather.10.cloned.1.call-start = ((), (), s32[]{:S(2)}) async-start(), calls=%async_computation.10 | async-start | bytes 4866048 | tf_op jit(solution)/shard_map/all_gather | solution.py:261
  12.2 87.3 %all-to-all-start = ((bf16[4,256,768]{2,1,0:T(8,128)(2,1)}), bf16[4,256,768]{2,1,0:T(8,128)(2,1)S(1)}, u32[]{:S(2)}, u32[]{:S(2)}) async-start(bf16[4,256,768]{2,1,0:T(8,128)(2,1)} %param.21), calls=%async_computation | async-start | bytes 3145728 | tf_op jit(solution)/shard_map/all_to_all | solution.py:266
  98.6 17.6 %copy-start.2 = (s32[1,1,1024]{2,1,0:T(1,128)}, s32[1,1,1024]{2,1,0:T(1,128)S(1)}, u32[]{:S(2)}) copy-start(s32[1,1,1024]{2,1,0:T(1,128)S(1)} %get-tuple-element.144.seg_row) | copy-start | bytes 12292
  98.8 17.4 %copy-start = (s32[1,1024,1]{2,1,0:T(8,128)}, s32[1,1024,1]{2,1,0:T(8,128)S(1)}, u32[]{:S(2)}) copy-start(s32[1,1024,1]{2,1,0:T(8,128)S(1)} %copy.85.seg_col) | copy-start | bytes 12292
  99.5 112.5 %all-to-all-start.2 = ((bf16[4,256,768]{2,1,0:T(8,128)(2,1)}), bf16[4,256,768]{2,1,0:T(8,128)(2,1)}, u32[]{:S(2)}, u32[]{:S(2)}) async-start(bf16[4,256,768]{2,1,0:T(8,128)(2,1)} %param.22), calls=%async_computation.2 | async-start | bytes 3145728 | tf_op jit(solution)/shard_map/all_to_all | solution.py:267
  103.9 256.1 %reduce-scatter.11.cloned.1.call-start = ((), (), s32[]{:S(2)}) async-start(), calls=%async_computation.15 | async-start | bytes 9732096 | tf_op jit(solution)/shard_map/reduce_scatter | solution.py:328
  144.6 0.7 copy-start.1
  149.2 1.8 copy-start.3
  225.2 134.7 %copy-start.13 = (f32[96,768]{1,0:T(8,128)S(1)}, f32[96,768]{1,0:T(8,128)}, u32[]{:S(2)}) copy-start(f32[96,768]{1,0:T(8,128)} %param.33) | copy-start | bytes 884740
  225.2 134.7 %copy-start.15 = (f32[96,768]{1,0:T(8,128)S(1)}, f32[96,768]{1,0:T(8,128)}, u32[]{:S(2)}) copy-start(f32[96,768]{1,0:T(8,128)} %param.35) | copy-start | bytes 884740
  225.2 134.7 %copy-start.16 = (f32[96,768]{1,0:T(8,128)S(1)}, f32[96,768]{1,0:T(8,128)}, u32[]{:S(2)}) copy-start(f32[96,768]{1,0:T(8,128)} %param.34) | copy-start | bytes 884740
  225.3 200.5 %all-gather.12.cloned.1.call-start = ((), (), s32[]{:S(2)}) async-start(), calls=%async_computation.11 | async-start | bytes 4866048 | tf_op jit(solution)/shard_map/all_gather | solution.py:262
  362.6 330.3 %reduce-scatter.7.cloned.1.call-start = ((), (), s32[]{:S(2)}) async-start(), calls=%async_computation.13 | async-start | bytes 2433024 | tf_op jit(solution)/shard_map/reduce_scatter | solution.py:328
  442.0 11.3 %copy-start.29 = (bf16[1024,3072]{1,0:T(8,128)(2,1)}, bf16[1024,3072]{1,0:T(8,128)(2,1)S(1)}, u32[]{:S(2)}) copy-start(bf16[1024,3072]{1,0:T(8,128)(2,1)S(1)} %get-tuple-element.160) | copy-start | bytes 18874372
  457.1 4.0 copy-start.4
  457.1 4.7 copy-start.8
  463.2 1.6 copy-start.10
  464.8 3.0 copy-start.28
  467.8 237.0 %reduce-scatter.5.cloned.1.call-start = ((), (), s32[]{:S(2)}) async-start(), calls=%async_computation.12 | async-start | bytes 7299072 | tf_op jit(solution)/shard_map/reduce_scatter | solution.py:328
  472.3 34.2 %copy-start.6 = (f32[1024,768]{0,1:T(8,128)S(1)}, f32[1024,768]{0,1:T(8,128)}, u32[]{:S(2)}) copy-start(f32[1024,768]{0,1:T(8,128)} %copy.97) | copy-start | bytes 9437188
  515.1 1.9 copy-start.5
  515.1 331.4 %reduce-scatter.9.cloned.1.call-start = ((), (), s32[]{:S(2)}) async-start(), calls=%async_computation.14 | async-start | bytes 9732096 | tf_op jit(solution)/shard_map/reduce_scatter | solution.py:328
  564.3 49.4 %all-to-all-start.1 = ((bf16[4,2,98304]{2,1,0:T(2,128)(2,1)}), bf16[4,2,98304]{2,1,0:T(2,128)(2,1)}, u32[]{:S(2)}, u32[]{:S(2)}) async-start(bf16[4,2,98304]{2,1,0:T(2,128)(2,1)} %reshape.404), calls=%async_computation.1 | async-start | bytes 3145728 | tf_op jit(solution)/shard_map/all_to_all | solution.py:287
  577.9 3.8 copy-start.7
  581.6 3.2 copy-start.9
  581.6 4.1 copy-start.11
  613.7 70.2 %copy-start.25 = (f32[96]{0:T(128)S(1)}, f32[96]{0:T(128)}, u32[]{:S(2)}) copy-start(f32[96]{0:T(128)} %param.39) | copy-start | bytes 1156
  613.7 70.2 %copy-start.26 = (f32[96]{0:T(128)S(1)}, f32[96]{0:T(128)}, u32[]{:S(2)}) copy-start(f32[96]{0:T(128)} %param.41) | copy-start | bytes 1156
  613.7 70.2 %copy-start.27 = (f32[96]{0:T(128)S(1)}, f32[96]{0:T(128)}, u32[]{:S(2)}) copy-start(f32[96]{0:T(128)} %param.40) | copy-start | bytes 1156
  613.7 71.4 %copy-start.18 = (f32[8,24]{1,0:T(8,128)S(1)}, f32[8,24]{1,0:T(8,128)}, u32[]{:S(2)}) copy-start(f32[8,24]{1,0:T(8,128)} %param.36) | copy-start | bytes 2308
  613.7 71.4 %copy-start.22 = (f32[8,24]{1,0:T(8,128)S(1)}, f32[8,24]{1,0:T(8,128)}, u32[]{:S(2)}) copy-start(f32[8,24]{1,0:T(8,128)} %param.38) | copy-start | bytes 2308
  613.7 71.3 %copy-start.23 = (f32[8,24]{1,0:T(8,128)S(1)}, f32[8,24]{1,0:T(8,128)}, u32[]{:S(2)}) copy-start(f32[8,24]{1,0:T(8,128)} %param.37) | copy-start | bytes 2308
  613.8 75.9 %all-to-all-start.3 = ((bf16[4,2,98304]{2,1,0:T(2,128)(2,1)}), bf16[4,2,98304]{2,1,0:T(2,128)(2,1)}, u32[]{:S(2)}, u32[]{:S(2)}) async-start(bf16[4,2,98304]{2,1,0:T(2,128)(2,1)} %reshape.402), calls=%async_computation.3 | async-start | bytes 3145728 | tf_op jit(solution)/shard_map/all_to_all | solution.py:305
  683.9 5.8 copy-start.19
  685.2 224.3 %copy-start.20 = (f32[8,24]{1,0:T(8,128)}, f32[8,24]{1,0:T(8,128)S(1)}, u32[]{:S(2)}) copy-start(f32[8,24]{1,0:T(8,128)S(1)} %get-tuple-element.131) | copy-start | bytes 2308
  685.2 224.3 %copy-start.21 = (f32[8,24]{1,0:T(8,128)}, f32[8,24]{1,0:T(8,128)S(1)}, u32[]{:S(2)}) copy-start(f32[8,24]{1,0:T(8,128)S(1)} %get-tuple-element.132) | copy-start | bytes 2308
  689.7 3.2 copy-start.14
  689.7 156.8 %copy-start.12 = (f32[24,3072]{1,0:T(8,128)S(1)}, f32[24,3072]{1,0:T(8,128)}, u32[]{:S(2)}) copy-start(f32[24,3072]{1,0:T(8,128)} %param.30) | copy-start | bytes 884740
Sparse Core Ops, SparseCore 0:
  11.5 65.8 all-gather.5
  80.8 53.8 all-gather.7
  138.2 62.4 all-gather.9
  225.4 134.5 reduce-scatter.10
  363.3 62.4 all-gather.11
  467.9 97.8 reduce-scatter.6
  572.0 132.7 reduce-scatter.4
  711.2 135.2 reduce-scatter.8

commit v2 on v1

--- a/solution.py
+++ b/solution.py
@@ -1,3 +1,5 @@
+import functools
+
 import jax
 import jax.numpy as jnp
 from jax import lax
@@ -18,6 +20,8 @@
 LEARN_RATE = 0.4
 NORM_EPS = 1e-05
 STEP_NUMBER = 10.0
+CORR_ONE = 1.0 - BETA_ONE**STEP_NUMBER
+CORR_TWO = 1.0 - BETA_TWO**STEP_NUMBER
 
 BRAIN = jnp.bfloat16
 FLOAT = jnp.float32
@@ -217,13 +221,503 @@
     )(segments[:, :, None], segments[:, None, :], qkv, qkv, qkv, grads, lse_rows)
 
 
-def lamb_parts(weight, first, second, grad, decay, corr_one, corr_two, axis):
+MESH = pl.DeviceIdType.MESH
+
+
+def bits_of(count):
+    return count.bit_length() - 1
+
+
+def flipped(value, bit):
+    step = 1 << bit
+    return value + step * (1 - 2 * lax.rem(lax.div(value, step), 2))
+
+
+def rounded_down(value, bit):
+    return lax.div(value, 1 << bit) * (1 << bit)
+
+
+def spread(value, bit, total):
+    step = 1 << (bit + 1)
+    return [lax.rem(value, step) + step * turn for turn in range(1 << (total - 1 - bit))]
+
+
+def greet(peers):
+    barrier = pltpu.get_barrier_semaphore()
+    for peer in peers:
+        pl.semaphore_signal(barrier, inc=1, device_id=peer, device_id_type=MESH)
+    pl.semaphore_wait(barrier, len(peers))
+
+
+def cube_peers(place, line, seq_count, half_count):
+    peers = [{"dp": flipped(place, 0)}]
+    peers += [{"dp": flipped(place, bit + 1)} for bit in range(bits_of(half_count))]
+    peers += [{"seq": flipped(line, bit)} for bit in range(bits_of(seq_count))]
+    return peers
+
+
+def column_halves(width):
+    if width % 256:
+        return [slice(0, width)]
+    return [slice(0, width // 2), slice(width // 2, width)]
+
+
+def gather_stages(full, columns, backwards):
+    half_count, _, seq_count = full.shape[:3]
+    place, line = lax.axis_index("dp"), lax.axis_index("seq")
+    chip, core = lax.div(place, 2), lax.rem(place, 2)
+    stages = []
+    for bit in range(bits_of(half_count)):
+        block = pl.ds(rounded_down(chip, bit), 1 << bit)
+        stages.append(([full.at[block, core, line, :, columns]], {"dp": flipped(place, bit + 1)}))
+    total = bits_of(seq_count)
+    for bit in reversed(range(total)) if backwards else range(total):
+        if backwards:
+            held = [full.at[:, core, at, :, columns] for at in spread(line, bit, total)]
+        else:
+            block = pl.ds(rounded_down(line, bit), 1 << bit)
+            held = [full.at[:, core, block, :, columns]]
+        stages.append((held, {"seq": flipped(line, bit)}))
+    stages.append(([full.at[:, core, :, :, columns]], {"dp": flipped(place, 0)}))
+    return stages
+
+
+def gather_kernel(count, *refs):
+    shards, fulls = refs[:count], refs[count : 2 * count]
+    send_sem, recv_sem, own_sem = refs[2 * count :]
+    half_count, _, seq_count = fulls[0].shape[:3]
+    place, line = lax.axis_index("dp"), lax.axis_index("seq")
+    chip, core = lax.div(place, 2), lax.rem(place, 2)
+    owns = [
+        pltpu.make_async_copy(shard, full.at[chip, core, line], own_sem.at[index])
+        for index, (shard, full) in enumerate(zip(shards, fulls))
+    ]
+    for own in owns:
+        own.start()
+    greet(cube_peers(place, line, seq_count, half_count))
+    slot = 0
+    chunks = []
+    for full in fulls:
+        chunk = []
+        for turn, columns in enumerate(column_halves(full.shape[-1])):
+            stages = []
+            for slices, peer in gather_stages(full, columns, turn == 1):
+                copies = []
+                for part in slices:
+                    copies.append(
+                        pltpu.make_async_remote_copy(
+                            part,
+                            part,
+                            send_sem.at[slot],
+                            recv_sem.at[slot],
+                            device_id=peer,
+                            device_id_type=MESH,
+                        )
+                    )
+                    slot += 1
+                stages.append(copies)
+            chunk.append(stages)
+        chunks.append(chunk)
+    steps = len(chunks[0][0])
+    for wave in range(count + steps):
+        for index, chunk in enumerate(chunks):
+            step = wave - index
+            if step == 0:
+                owns[index].wait()
+            for stages in chunk:
+                if 1 <= step <= steps:
+                    for copy in stages[step - 1]:
+                        copy.wait_recv()
+                if 0 <= step < steps:
+                    for copy in stages[step]:
+                        copy.start()
+    for chunk in chunks:
+        for stages in chunk:
+            for copies in stages:
+                for copy in copies:
+                    copy.wait_send()
+
+
+def copies_in_all(widths, half_count, seq_count):
+    single = bits_of(half_count) + bits_of(seq_count) + 1
+    double = single + bits_of(half_count) + 1 + seq_count - 1
+    return sum(double if len(column_halves(width)) == 2 else single for width in widths)
+
+
+def gather_all(shards, dp_count, seq_count):
+    half_count = dp_count // 2
+    slots = copies_in_all([shard.shape[1] for shard in shards], half_count, seq_count)
+    fulls = pl.pallas_call(
+        functools.partial(gather_kernel, len(shards)),
+        out_shape=[
+            jax.ShapeDtypeStruct((half_count, 2, seq_count) + shard.shape, shard.dtype)
+            for shard in shards
+        ],
+        in_specs=[pl.BlockSpec(memory_space=pltpu.VMEM)] * len(shards),
+        out_specs=[pl.BlockSpec(memory_space=pl.ANY)] * len(shards),
+        scratch_shapes=[
+            pltpu.SemaphoreType.DMA((slots,)),
+            pltpu.SemaphoreType.DMA((slots,)),
+            pltpu.SemaphoreType.DMA((len(shards),)),
+        ],
+        name="gather_weights",
+        compiler_params=pltpu.CompilerParams(collective_id=0, has_side_effects=True),
+    )(*shards)
+    return fulls
+
+
+def lamb_pieces(weight, first, second, grad, decay):
     first_new = BETA_ONE * first + (1.0 - BETA_ONE) * grad
     second_new = BETA_TWO * second + (1.0 - BETA_TWO) * grad * grad
-    update = first_new / corr_one / (jnp.sqrt(second_new / corr_two) + ADAM_EPS) + decay * weight
-    weight_sq = jnp.reshape(jnp.sum(weight * weight, axis=axis), (-1,))
-    update_sq = jnp.reshape(jnp.sum(update * update, axis=axis), (-1,))
-    return (first_new, second_new, update, weight_sq, update_sq)
+    spread_out = jnp.sqrt(second_new / CORR_TWO) + ADAM_EPS
+    update = first_new / CORR_ONE / spread_out + decay * weight
+    return (first_new, second_new, update)
+
+
+def square_sum(values):
+    return jnp.sum(jnp.sum(values * values, axis=1, keepdims=True), axis=0, keepdims=True)
+
+
+def picked(small, rank, vector_size, bias_size):
+    width = small.shape[1]
+    row = lax.broadcasted_iota(jnp.int32, (width, 128), 0)
+    lane = lax.broadcasted_iota(jnp.int32, (width, 128), 1)
+    dot = functools.partial(jnp.dot, precision=lax.Precision.HIGHEST, preferred_element_type=FLOAT)
+    chosen = (row == lane + rank * vector_size) & (lane < vector_size)
+    vector_grad = dot(small[0:8, :], jnp.where(chosen, 1.0, 0.0))[:, :vector_size]
+    start = rank * bias_size
+    chosen = (row == lane + lax.rem(start, width)) & (lane < bias_size)
+    tail = dot(small[8:16, :], jnp.where(chosen, 1.0, 0.0))
+    tail_row = lax.broadcasted_iota(jnp.int32, tail.shape, 0)
+    tail = jnp.sum(jnp.where(tail_row == lax.div(start, width), tail, 0.0), axis=0, keepdims=True)
+    return vector_grad, tail[:, :bias_size]
+
+
+def scatter_kernel(*refs):
+    grads, small = refs[0:4], refs[4]
+    weights, firsts, seconds = refs[5:11], refs[11:17], refs[17:23]
+    shares, norm_out = refs[23:29], refs[29]
+    owns, cores, lines = refs[30:34], refs[34:38], refs[38:46]
+    chips = refs[46:54]
+    small_sum, small_in, norm_mine, norm_dp, norm_line, norm_seq = refs[54:60]
+    send_sem, recv_sem, own_sem, small_send, small_recv, norm_send, norm_recv = refs[60:67]
+
+    half_count, _, seq_count = grads[0].shape[:3]
+    dp_count = 2 * half_count
+    place, line = lax.axis_index("dp"), lax.axis_index("seq")
+    chip, core = lax.div(place, 2), lax.rem(place, 2)
+    seq_bits, half_bits = bits_of(seq_count), bits_of(half_count)
+
+    loads = [
+        pltpu.make_async_copy(grad.at[:, core], own, own_sem.at[index])
+        for index, (grad, own) in enumerate(zip(grads, owns))
+    ]
+    for load in loads:
+        load.start()
+    dp_peers = [{"dp": lax.rem(place + turn, dp_count)} for turn in range(1, dp_count)]
+    seq_peers = [{"seq": lax.rem(line + turn, seq_count)} for turn in range(1, seq_count)]
+    greet(dp_peers + seq_peers)
+
+    slots = iter(range(send_sem.shape[0]))
+
+    def remote(source, target, peer):
+        slot = next(slots)
+        return pltpu.make_async_remote_copy(
+            source, target, send_sem.at[slot], recv_sem.at[slot], device_id=peer, device_id_type=MESH
+        )
+
+    def add_loop(own, held, columns, trips, where):
+        def step(turn, carry):
+            mine, theirs = where(turn)
+            own[mine[0], mine[1], :, columns] = (
+                own[mine[0], mine[1], :, columns] + held[theirs]
+            )
+            return carry
+
+        lax.fori_loop(0, trips, step, 0)
+
+    chunks = []
+    for index, (grad, own, from_core) in enumerate(zip(grads, owns, cores)):
+        for turn, columns in enumerate(column_halves(grad.shape[-1])):
+            backwards = turn == 1
+            from_line, from_chip = lines[2 * index + turn], chips[2 * index + turn]
+            stages = []
+            copies = [
+                remote(
+                    grad.at[:, 1 - core, :, :, columns],
+                    from_core.at[:, :, :, columns],
+                    {"dp": flipped(place, 0)},
+                )
+            ]
+
+            def core_add(own=own, from_core=from_core, columns=columns):
+                def step(at, carry):
+                    one, two = lax.div(at, seq_count), lax.rem(at, seq_count)
+                    own[one, two, :, columns] = (
+                        own[one, two, :, columns] + from_core[one, two, :, columns]
+                    )
+                    return carry
+
+                lax.fori_loop(0, half_count * seq_count, step, 0)
+
+            stages.append((copies, core_add))
+            base = 0
+            for bit in range(seq_bits) if backwards else reversed(range(seq_bits)):
+                peer_line = flipped(line, bit)
+                if backwards:
+                    away, kept = spread(peer_line, bit, seq_bits), spread(line, bit, seq_bits)
+                else:
+                    size = 1 << bit
+                    away = [rounded_down(peer_line, bit) + at for at in range(size)]
+                    kept = [rounded_down(line, bit) + at for at in range(size)]
+                copies = [
+                    remote(
+                        own.at[:, at, :, columns],
+                        from_line.at[base + order],
+                        {"seq": peer_line},
+                    )
+                    for order, at in enumerate(away)
+                ]
+
+                def line_add(own=own, from_line=from_line, columns=columns, kept=kept, base=base):
+                    for order, at in enumerate(kept):
+
+                        def step(one, carry, at=at, order=order):
+                            own[one, at, :, columns] = (
+                                own[one, at, :, columns] + from_line[base + order, one]
+                            )
+                            return carry
+
+                        lax.fori_loop(0, half_count, step, 0)
+
+                stages.append((copies, line_add))
+                base += len(away)
+            base = 0
+            for bit in reversed(range(half_bits)):
+                size = 1 << bit
+                peer_chip = flipped(chip, bit)
+                away, kept = rounded_down(peer_chip, bit), rounded_down(chip, bit)
+                copies = [
+                    remote(
+                        own.at[pl.ds(away, size), line, :, columns],
+                        from_chip.at[pl.ds(base, size)],
+                        {"dp": flipped(place, bit + 1)},
+                    )
+                ]
+                if bit:
+
+                    def chip_add(
+                        own=own, from_chip=from_chip, columns=columns, kept=kept, base=base, size=size
+                    ):
+                        for at in range(size):
+                            own[kept + at, line, :, columns] = (
+                                own[kept + at, line, :, columns] + from_chip[base + at]
+                            )
+                else:
+
+                    def chip_add(
+                        own=own, from_chip=from_chip, columns=columns, base=base, share=shares[index]
+                    ):
+                        share[:, columns] = own[chip, line, :, columns].astype(FLOAT) + from_chip[
+                            base
+                        ].astype(FLOAT)
+
+                stages.append((copies, chip_add))
+                base += size
+            chunks.append((index, stages))
+
+    small_peers = cube_peers(place, line, seq_count, half_count)
+    small_copies = [
+        pltpu.make_async_remote_copy(
+            small if step == 0 else small_sum.at[step - 1],
+            small_in.at[step],
+            small_send.at[step],
+            small_recv.at[step],
+            device_id=peer,
+            device_id_type=MESH,
+        )
+        for step, peer in enumerate(small_peers)
+    ]
+
+    def start_small(step):
+        if 1 <= step <= len(small_copies):
+            small_copies[step - 1].wait_recv()
+            before = small[...] if step == 1 else small_sum[step - 2]
+            small_sum[step - 1] = before + small_in[step - 1]
+        if 0 <= step < len(small_copies):
+            small_copies[step].start()
+
+    steps = len(chunks[0][1])
+    order = [3, 2, 1, 0]
+    for wave in range(len(order) + steps):
+        start_small(wave)
+        for at, index in enumerate(order):
+            step = wave - at
+            if step == 1:
+                loads[index].wait()
+            for owner, stages in chunks:
+                if owner != index:
+                    continue
+                if 1 <= step <= steps:
+                    copies, add = stages[step - 1]
+                    for copy in copies:
+                        copy.wait_recv()
+                    add()
+                if 0 <= step < steps:
+                    for copy in stages[step][0]:
+                        copy.start()
+
+    rank = place * seq_count + line
+    vector_grad, bias_grad = picked(
+        small_sum[len(small_copies) - 1], rank, shares[4].shape[1], shares[5].shape[1]
+    )
+    shares[4][...] = vector_grad
+    shares[5][...] = bias_grad
+
+    lane = lax.broadcasted_iota(jnp.int32, (8, 128), 1)
+    row = lax.broadcasted_iota(jnp.int32, (8, 128), 0)
+    tile = jnp.zeros((8, 128), FLOAT)
+    for index in (0, 1, 2, 3, 5):
+        decay = DECAY_RATE if index < 4 else 0.0
+        weight = weights[index][...]
+        update = lamb_pieces(
+            weight, firsts[index][...], seconds[index][...], shares[index][...], decay
+        )[2]
+        here = row == (index if index < 4 else 4)
+        tile = jnp.where(here & (lane == 0), square_sum(weight), tile)
+        tile = jnp.where(here & (lane == 1), square_sum(update), tile)
+    norm_mine[0:8, :] = tile
+    weight = weights[4][...]
+    update = lamb_pieces(weight, firsts[4][...], seconds[4][...], vector_grad, 0.0)[2]
+    weight_sq = jnp.sum(weight * weight, axis=1, keepdims=True)
+    update_sq = jnp.sum(update * update, axis=1, keepdims=True)
+    norm_mine[8:16, :] = jnp.where(lane == 0, weight_sq, jnp.where(lane == 1, update_sq, 0.0))
+
+    def exchange(source, held, peers, at, base):
+        copies = [
+            pltpu.make_async_remote_copy(
+                source,
+                held.at[at],
+                norm_send.at[base + turn],
+                norm_recv.at[base + turn],
+                device_id=peer,
+                device_id_type=MESH,
+            )
+            for turn, peer in enumerate(peers)
+        ]
+        for copy in copies:
+            copy.start()
+        held[at] = source[...]
+        for copy in copies:
+            copy.wait_recv()
+        total = held[0]
+        for turn in range(1, held.shape[0]):
+            total = total + held[turn]
+        return copies, total
+
+    sent, total = exchange(norm_mine, norm_dp, dp_peers, place, 0)
+    norm_line[...] = total
+    more, total = exchange(norm_line, norm_seq, seq_peers, line, len(dp_peers))
+    norm_out[...] = total
+    for copy in sent + more + small_copies:
+        copy.wait_send()
+    for _, stages in chunks:
+        for copies, _ in stages:
+            for copy in copies:
+                copy.wait_send()
+
+
+def scatter_all(grads, small, weights, firsts, seconds, dp_count, seq_count):
+    half_count = dp_count // 2
+    shapes = [weight.shape for weight in weights]
+    views = [
+        grad.reshape(half_count, 2, seq_count, shape[0], shape[1])
+        for grad, shape in zip(grads, shapes)
+    ]
+    vmem = pl.BlockSpec(memory_space=pltpu.VMEM)
+    halves = [(shape[0], shape[1] // 2) for shape in shapes[:4] for _ in range(2)]
+    slots = copies_in_all([shape[1] for shape in shapes[:4]], half_count, seq_count)
+    slots += 4 * (seq_count - 1 - bits_of(seq_count))
+    stages = bits_of(dp_count) + bits_of(seq_count)
+    return pl.pallas_call(
+        scatter_kernel,
+        out_shape=[jax.ShapeDtypeStruct(shape, FLOAT) for shape in shapes]
+        + [jax.ShapeDtypeStruct((16, 128), FLOAT)],
+        in_specs=[pl.BlockSpec(memory_space=pl.ANY)] * 4 + [vmem] * 19,
+        out_specs=[vmem] * 7,
+        scratch_shapes=[
+            pltpu.VMEM((half_count, seq_count) + shape, BRAIN) for shape in shapes[:4]
+        ]
+        + [pltpu.VMEM((half_count, seq_count) + shape, BRAIN) for shape in shapes[:4]]
+        + [pltpu.VMEM((seq_count - 1, half_count) + half, BRAIN) for half in halves]
+        + [pltpu.VMEM((half_count - 1,) + half, BRAIN) for half in halves]
+        + [
+            pltpu.VMEM((stages,) + small.shape, FLOAT),
+            pltpu.VMEM((stages,) + small.shape, FLOAT),
+            pltpu.VMEM((16, 128), FLOAT),
+            pltpu.VMEM((dp_count, 16, 128), FLOAT),
+            pltpu.VMEM((16, 128), FLOAT),
+            pltpu.VMEM((seq_count, 16, 128), FLOAT),
+            pltpu.SemaphoreType.DMA((slots,)),
+            pltpu.SemaphoreType.DMA((slots,)),
+            pltpu.SemaphoreType.DMA((4,)),
+            pltpu.SemaphoreType.DMA((stages,)),
+            pltpu.SemaphoreType.DMA((stages,)),
+            pltpu.SemaphoreType.DMA((dp_count + seq_count,)),
+            pltpu.SemaphoreType.DMA((dp_count + seq_count,)),
+        ],
+        name="scatter_gradients",
+        compiler_params=pltpu.CompilerParams(
+            collective_id=1, has_side_effects=True, vmem_limit_bytes=60 * 1024 * 1024
+        ),
+    )(*views, small, *weights, *firsts, *seconds)
+
+
+def lamb_kernel(*refs):
+    grads, norms = refs[0:6], refs[6]
+    weights, firsts, seconds = refs[7:13], refs[13:19], refs[19:25]
+    grad_out, first_out, second_out, new_out = refs[25:31], refs[31:37], refs[37:43], refs[43:49]
+    copy_out = refs[49:53]
+    weight_norm = jnp.sqrt(norms[:, 0:1])
+    scales = weight_norm / (jnp.sqrt(norms[:, 1:2]) + ADAM_EPS)
+    for index in range(6):
+        grad = grads[index][...]
+        weight = weights[index][...]
+        decay = DECAY_RATE if index < 4 else 0.0
+        first_new, second_new, update = lamb_pieces(
+            weight, firsts[index][...], seconds[index][...], grad, decay
+        )
+        scale = scales[8:16] if index == 4 else scales[min(index, 4) : min(index, 4) + 1]
+        new = weight - LEARN_RATE * scale * update
+        grad_out[index][...] = grad
+        first_out[index][...] = first_new
+        second_out[index][...] = second_new
+        new_out[index][...] = new
+        if index < 4:
+            copy_out[index][...] = new.astype(BRAIN)
+
+
+def lamb_all(grads, norms, weights, firsts, seconds):
+    vmem = pl.BlockSpec(memory_space=pltpu.VMEM)
+    shapes = [jax.ShapeDtypeStruct(weight.shape, FLOAT) for weight in weights]
+    copies = [jax.ShapeDtypeStruct(weight.shape, BRAIN) for weight in weights[:4]]
+    return pl.pallas_call(
+        lamb_kernel,
+        out_shape=shapes * 4 + copies,
+        in_specs=[vmem] * 25,
+        out_specs=[vmem] * 28,
+        name="lamb_update",
+        compiler_params=pltpu.CompilerParams(vmem_limit_bytes=48 * 1024 * 1024),
+    )(*grads, norms, *weights, *firsts, *seconds)
+
+
+def back_to_positions(values, shape):
+    row_count, pos_count, width = shape
+    seq_count = lax.axis_size("seq")
+    parts = values.reshape(row_count // seq_count, seq_count, pos_count, width)
+    parts = parts.transpose(1, 0, 2, 3)
+    parts = lax.all_to_all(parts, "seq", split_axis=0, concat_axis=0, tiled=True)
+    return parts.reshape(shape)
 
 
 def body(
@@ -249,17 +743,23 @@
     m_up_bias,
     v_up_bias,
 ):
-    both = ("dp", "seq")
-    small = jnp.concatenate([vectors.reshape(-1), up_bias]).astype(BRAIN)
-    small = lax.all_gather(small[None], both, axis=0, tiled=True)
-    cut = vectors.size
-    full_vectors = small[:, :cut].reshape(-1, vectors.shape[0], vectors.shape[1])
-    vector_rows = full_vectors.transpose(1, 0, 2).reshape(vectors.shape[0], -1).astype(FLOAT)
-    up_shift = small[:, cut:].reshape(-1).astype(FLOAT)
-    full_qkv = lax.all_gather(w_qkv.astype(BRAIN), both, axis=0, tiled=True)
-    full_out = lax.all_gather(w_out.astype(BRAIN), both, axis=0, tiled=True)
-    full_up = lax.all_gather(w_up.astype(BRAIN), both, axis=0, tiled=True)
-    full_down = lax.all_gather(w_down.astype(BRAIN), both, axis=0, tiled=True)
+    dp_count, seq_count = lax.axis_size("dp"), lax.axis_size("seq")
+    vector_size, bias_size = vectors.shape[1], up_bias.shape[0]
+    small = jnp.concatenate(
+        [
+            jnp.pad(vectors, ((0, 0), (0, 128 - vector_size))),
+            jnp.pad(up_bias[None], ((0, 7), (0, 128 - bias_size))),
+        ]
+    )
+    shards = [part.astype(BRAIN) for part in (small, w_qkv, w_out, w_up, w_down)]
+    fulls = gather_all(shards, dp_count, seq_count)
+    small = fulls[0].reshape(dp_count * seq_count, 16, 128)
+    full_vectors = small[:, :8, :vector_size].transpose(1, 0, 2)
+    vector_rows = full_vectors.reshape(8, -1).astype(FLOAT)
+    up_shift = small[:, 8, :bias_size].reshape(-1).astype(FLOAT)
+    full_qkv, full_out, full_up, full_down = [
+        full.reshape(-1, full.shape[-1]) for full in fulls[1:]
+    ]
 
     width = tokens.shape[2]
     length = segment_ids.shape[1]
@@ -283,8 +783,7 @@
     activated, gelu_pull = jax.vjp(gelu_tanh, hidden_pre)
     low_act = activated.astype(BRAIN)
     result = resid_one + matmul(low_act, full_down) + vector_rows[7]
-    mixed = result.astype(BRAIN).reshape(rows, length, width)
-    mixed = lax.all_to_all(mixed, "seq", split_axis=1, concat_axis=0, tiled=True)
+    mixed = back_to_positions(result.astype(BRAIN), tokens.shape)
 
     back_float = back_part.astype(FLOAT)
     grad_down = inner_rows(low_act, back_part)
@@ -301,9 +800,7 @@
     grad_qkv = inner_rows(low_one, joined)
     one_grad = times_transposed(joined, full_qkv)
     input_rows = resid_grad + norm_backward(one_grad, plain_one, inverse_one, vector_rows[0])
-    input_grad = input_rows.astype(BRAIN).reshape(rows, length, width)
-    input_grad = lax.all_to_all(input_grad, "seq", split_axis=1, concat_axis=0, tiled=True)
-    input_grad = input_grad.astype(FLOAT)
+    input_grad = back_to_positions(input_rows.astype(BRAIN), tokens.shape).astype(FLOAT)
     joined_sum = jnp.sum(joined.astype(FLOAT), axis=0)
     grad_vectors = jnp.stack(
         [
@@ -317,59 +814,20 @@
             jnp.sum(back_float, axis=0),
         ]
     )
-    devices = width // vectors.shape[1]
-    small_grad = jnp.concatenate(
-        [
-            grad_vectors.reshape(vectors.shape[0], devices, -1).transpose(1, 0, 2).reshape(devices, -1),
-            grad_up_bias.reshape(devices, -1),
-        ],
-        axis=1,
+    small_grad = jnp.concatenate([grad_vectors, grad_up_bias.reshape(-1, width)])
+    small_grad = jnp.pad(small_grad, ((0, 16 - small_grad.shape[0]), (0, 0)))
+    as_row = lambda value: value.reshape(1, -1)
+    weights = (w_qkv, w_out, w_up, w_down, vectors, as_row(up_bias))
+    firsts = (m_qkv, m_out, m_up, m_down, m_vectors, as_row(m_up_bias))
+    seconds = (v_qkv, v_out, v_up, v_down, v_vectors, as_row(v_up_bias))
+    matrix_grads = [grad.astype(BRAIN) for grad in (grad_qkv, grad_out, grad_up, grad_down)]
+    *shares, norms = scatter_all(
+        matrix_grads, small_grad, weights, firsts, seconds, dp_count, seq_count
     )
-    scatter = lambda value: lax.psum_scatter(value, both, scatter_dimension=0, tiled=True)
-    small_share = scatter(small_grad)[0]
-    shares = (
-        scatter(grad_qkv),
-        scatter(grad_out),
-        scatter(grad_up),
-        scatter(grad_down),
-        small_share[:cut].reshape(vectors.shape),
-        small_share[cut:],
-    )
-    count_float = jnp.asarray(STEP_NUMBER, FLOAT)
-    corr_one = 1.0 - jnp.power(jnp.asarray(BETA_ONE, FLOAT), count_float)
-    corr_two = 1.0 - jnp.power(jnp.asarray(BETA_TWO, FLOAT), count_float)
-    weights = (w_qkv, w_out, w_up, w_down, vectors, up_bias)
-    firsts = (m_qkv, m_out, m_up, m_down, m_vectors, m_up_bias)
-    seconds = (v_qkv, v_out, v_up, v_down, v_vectors, v_up_bias)
-    decays = (DECAY_RATE, DECAY_RATE, DECAY_RATE, DECAY_RATE, 0.0, 0.0)
-    axes_list = (None, None, None, None, 1, None)
-    parts = [
-        lamb_parts(*each, corr_one, corr_two, axis)
-        for *each, axis in zip(weights, firsts, seconds, shares, decays, axes_list)
-    ]
-    totals = lax.psum(
-        jnp.stack(
-            [
-                jnp.concatenate([part[3] for part in parts]),
-                jnp.concatenate([part[4] for part in parts]),
-            ]
-        ),
-        both,
-    )
-    ratios = jnp.sqrt(totals[0]) / (jnp.sqrt(totals[1]) + ADAM_EPS)
-    scales = [ratios[0], ratios[1], ratios[2], ratios[3], ratios[4:12][:, None], ratios[12]]
-    news = [
-        weight - LEARN_RATE * scale * part[2] for weight, scale, part in zip(weights, scales, parts)
-    ]
-    return (
-        mixed,
-        input_grad,
-        *shares,
-        *[part[0] for part in parts],
-        *[part[1] for part in parts],
-        *news,
-        *[new.astype(BRAIN) for new in news[:4]],
-    )
+    results = list(lamb_all(shares, norms, weights, firsts, seconds))
+    for index in (5, 11, 17, 23):
+        results[index] = results[index].reshape(-1)
+    return (mixed, input_grad, *results)
 
 
 def solution(mesh):

time: 928 us -> 418 us (0.45)
  waiting for transfers between devices: 394 us -> 0.01 us
  Pallas kernels: 62.6 us -> 248 us
  blocking collectives: 184 us -> 0 us
  local copies, waits for them, and re-layouts: 61.8 us -> 12.1 us
  other arithmetic: 65.8 us -> 26.5 us
  between operations: 18.3 us -> 1.64 us
    reduce_scatter x4 -> x0, waiting for transfers between devices: 283 us -> none  [body(): lax.psum_scatter(value, both, scatter_dimension=0, tiled=True)]
    pallas_call x0 -> x3, Pallas kernels: none -> 186 us  [the longest x1 94.9 us: scatter_all(): pl.pallas_call(scatter_kernel, out_shape=[jax.ShapeDtypeStruct(shape, FLO...]
    all_gather x4 -> x0, waiting for transfers between devices: 110 us -> none  [the longest x1 60.9 us: body(): full_down = lax.all_gather(w_down.astype(BRAIN), both, axis=0, tiled=True)]
    all_gather x1 -> x0, blocking collectives: 79.1 us -> none  [body(): small = lax.all_gather(small[None], both, axis=0, tiled=True)]
    unnamed x1 -> x0, blocking collectives: 64.8 us -> none
    psum x1 -> x0, blocking collectives: 39.6 us -> none  [body(): lax.psum(jnp.stack([jnp.concatenate([part[3] for part in parts]), jnp.con...]
    unnamed x5 -> x4, other arithmetic: 22.9 us -> 0.02 us
    reduce_sum x9 -> x0, other arithmetic: 19.5 us -> none  [the longest x6 11.2 us: lamb_parts(): weight_sq = jnp.reshape(jnp.sum(weight * weight, axis=axis), (-1,))]
  transfers between devices with their start and end apart: 12 -> 4, of which waited for: 5 -> 0; matrix products, arithmetic and copies ran while one was open for 17% -> 21% of each run, Pallas kernels for 7% -> 60%
where the time goes in v2:
time: 418 us; the launch traced here: 413 us
  Pallas kernels  248 us (59%)
  matrix products  106 us (25%)
  other arithmetic  26.5 us (6%)
  starting transfers between devices  18.7 us (4%)
  local copies, waits for them, and re-layouts  12.1 us (3%)
    pallas_call x1, Pallas kernels, scatter_all(): pl.pallas_call(scatter_kernel, out_shape=[jax.ShapeDtypeStruct(shape, FLO...  94.9 us
    pallas_call x1, Pallas kernels, gather_all(): pl.pallas_call(functools.partial(gather_kernel, len(shards)), out_shape=[...  88 us
    dot_general x4, matrix products, inner_rows(): lax.dot_general(left_side, right_side, (((0,), (0,)), ((), ())), preferre...  44.1 us
    dot_general x4, matrix products, times_transposed(): lax.dot_general(left_side, right_side, (((1,), (1,)), ((), ())), preferre...  36 us
    pallas_call x1, Pallas kernels, attention_backward(): pl.pallas_call(attend_backward, grid=(rows, HEADS // 2), in_specs=segs +...  34.2 us
    pallas_call x1, Pallas kernels, attention_forward(): pl.pallas_call(attend_forward, grid=(rows, HEADS // 2), in_specs=segs + q...  28.5 us
    dot_general x4, matrix products, matmul(): return jnp.dot(left_side, right_side, preferred_element_type=FLOAT)  25.6 us
    all_to_all x2, starting transfers between devices, back_to_positions(): lax.all_to_all(parts, 'seq', split_axis=0, concat_axis=0, tiled=True)  9 us
  transfers between devices with their start and end apart: 4, of which 0 were waited for; matrix products, arithmetic and copies ran while one was open for 21% of the time, Pallas kernels for 60%

profile of v2, /device:TPU:0, one launch (start us, length us, event | category | flops | bytes accessed | tf_op | source)
XLA Modules:
  0.0 412.9 jit_solution(16168659734000783006)
XLA Ops:
  0.7 0.0 copy-start.5
  0.7 0.0 copy-start.13
  0.7 0.0 copy-start.3
  0.7 0.0 copy-start.29
  0.7 5.3 %all-to-all-start = ((bf16[4,256,768]{2,1,0:T(8,128)(2,1)}), bf16[4,256,768]{2,1,0:T(8,128)(2,1)}, u32[]{:S(2)}, u32[]{:S(2)}) async-start(bf16[4,256,768]{2,1,0:T(8,128)(2,1)} %param.21), calls=%async_computation | async-start | bytes 3145728 | tf_op jit(solution)/shard_map/all_to_all | solution.py:766
  6.1 0.7 convert_element_type.117.refs_1_
  6.8 0.6 convert_element_type.118.refs_2_
  7.4 0.7 convert_element_type.119.refs_3_
  8.1 0.7 convert_element_type.120.refs_4_
  8.7 0.6 fusion.33.refs_0_
  9.3 88.0 %gather_weights.1 = (bf16[4,2,4,16,128]{4,3,2,1,0:T(8,128)(2,1)}, bf16[4,2,4,24,2304]{4,3,2,1,0:T(8,128)(2,1)}, bf16[4,2,4,24,768]{4,3,2,1,0:T(8,128)(2,1)}, bf1...) custom-call(bf16[16,128]{1,0:T(8,128)(2,1)} %fusion.33.refs_0_, ...), custom_call_target="tpu_custom_call" | custom-call | tf_op jit(solution)/shard_map/gather_weights/pallas_call | solution.py:350
  97.4 0.8 slice.58
  98.2 0.1 add.116
  98.3 0.7 dynamic-slice_bitcast_fusion
  99.1 0.2 copy.55.seg_col
  99.3 0.1 add.110
  99.4 0.1 mul.155
  99.5 0.1 squeeze.7
  99.6 0.1 squeeze.6
  99.6 0.1 add.128
  99.7 0.1 add.120
  99.8 0.1 mul.161
  99.9 0.9 fusion.30
  100.8 0.1 reshape.275
  100.9 4.4 %all-to-all-start.2 = ((bf16[4,256,768]{2,1,0:T(8,128)(2,1)}), bf16[4,256,768]{2,1,0:T(8,128)(2,1)}, u32[]{:S(2)}, u32[]{:S(2)}) async-start(bf16[4,256,768]{2,1,0:T(8,128)(2,1)} %param.22), calls=%async_computation.2 | async-start | bytes 3145728 | tf_op jit(solution)/shard_map/all_to_all | solution.py:767
  105.3 1.8 convert_reduce_fusion.2
  107.2 2.0 fusion.12
  109.2 2.0 fusion.15
  111.2 5.4 %add_convert_fusion.q_ref.k_ref.v_ref = bf16[1024,2304]{1,0:T(8,128)(2,1)} fusion(bf16[1024,768]{1,0:T(8,128)(2,1)S(1)} %bitcast.117, bf16[768,2304]{1,0:T(8,128)(2,1)S(1)} %bitcast.133, f32[2304]{0:T(1024)S(1)} %pad_maximum_fusion), kind=kOutput, calls=%fused_computation.17 | convolution fusion | flops 3628597248 | bytes 9839616 | tf_op jit(solution)/shard_map/dot_general | solution.py:31
  116.6 28.5 %attend_forward.1 = (bf16[1024,768]{1,0:T(8,128)(2,1)S(1)}, f32[1,6,8,1024]{3,2,1,0:T(8,128)S(1)}) custom-call(s32[1,1024,1]{2,1,0:T(8,128)S(1)} %copy.55.seg_col, s32[1,1,1024]{2,1,0:T(1,128)S(1)} %get-tuple-element.133.seg_row, bf16[1024,2304]{1,0:T(8,128)(2,1)} %add_convert_fusion.q_ref.k_ref.v_ref, bf16[1024,2304]{1,0:T(8,128)(2,1)} %add_convert_fusion.q_ref.k_ref.v_ref, ...), custom_call_target="tpu_custom_call" | custom-call | tf_op jit(solution)/shard_map/attend_forward/pallas_call | solution.py:189
  145.2 3.1 fusion.41
  148.3 0.5 multiply_reduce_fusion.2
  148.9 1.1 copy-done.35
  150.0 8.2 %fusion.38 = f32[1024,3072]{1,0:T(8,128)} fusion(bf16[768,3072]{1,0:T(8,128)(2,1)S(1)} %bitcast.128, f32[1024,768]{1,0:T(8,128)S(1)} %get-tuple-element.142, f32[768]{0:T(1024)S(1)} %add.120, f32[768]{0:T(1024)S(1)} %mul.161, f32[1024]{0:T(1024)S(1)} %add_rsqrt_fusion, f32[1024]{0:T(1024)S(1)} %broadcast_multiply_fusion.4), kind=kOutput, calls=%fused_computation.83 | convolution fusion | flops 4835770368 | bytes 20461568 | tf_op jit(solution)/shard_map/dot_general | solution.py:31
  158.2 22.1 %convolution_convert_fusion = bf16[3072,768]{1,0:T(8,128)(2,1)} fusion(bf16[1024,768]{1,0:T(8,128)(2,1)} %bitcast.14, f32[1024,3072]{1,0:T(8,128)} %fusion.38, f32[3072]{0:T(1024)S(1)} %reshape.275), kind=kOutput, calls=%fused_computation.18 | convolution fusion | flops 4865654784 | bytes 18886656 | tf_op jit(solution)/shard_map/dot_general | solution.py:35
  180.3 16.3 %convert_reduce_fusion = (f32[3072]{0:T(1024)S(1)}, bf16[1024,3072]{1,0:T(8,128)(2,1)}) fusion(f32[1024,3072]{1,0:T(8,128)S(1)} %copy-done.46, f32[3072]{0:T(1024)S(1)} %reshape.275, bf16[3072,768]{1,0:T(8,128)(2,1)} %bitcast.129, bf16[1024,768]{1,0:T(8,128)(2,1)} %bitcast.14), kind=kOutput, calls=%fused_computation.14 | convolution fusion | flops 4904186880 | bytes 25190400 | tf_op jit(solution)/shard_map/dot_general | solution.py:41
  196.6 8.9 %add_convert_fusion.1 = bf16[1024,768]{1,0:T(8,128)(2,1)} fusion(f32[1024,768]{1,0:T(8,128)S(1)} %copy-done.36, bf16[3072,768]{1,0:T(8,128)(2,1)S(1)} %bitcast.132, f32[768]{0:T(1024)S(1)} %add.128, f32[1024,3072]{1,0:T(8,128)S(1)} %copy-done.46, f32[3072]{0:T(1024)S(1)} %reshape.275), kind=kOutput, calls=%fused_computation.50 | convolution fusion | flops 4865654784 | bytes 22035456 | tf_op jit(solution)/shard_map/dot_general | solution.py:31
  205.5 4.7 %all-to-all-start.1 = ((bf16[4,1,256,768]{3,2,1,0:T(8,128)(2,1)}), bf16[4,1,256,768]{3,2,1,0:T(8,128)(2,1)S(1)}, u32[]{:S(2)}, u32[]{:S(2)}) async-start(bf16[4,1,256,768]{3,2,1,0:T(8,128)(2,1)} %bitcast.116), calls=%async_computation.1 | async-start | bytes 3145728 | tf_op jit(solution)/shard_map/all_to_all | solution.py:719
  210.2 9.9 %multiply_reduce_fusion = (f32[768]{0:T(1024)S(1)}, f32[1024]{0:T(1024)S(1)}, f32[1024]{0:T(1024)S(1)}, f32[768]{0:T(1024)S(1)}, f32[1024,768]{1,0:T(8,128)S(1)}) fusion(f32[1024,768]{1,0:T(8,128)} %copy-done.35, f32[1024]{0:T(1024)S(1)} %add_rsqrt_fusion, f32[1024]{0:T(1024)S(1)} %broadcast_multiply_fusion.4, f32[768]{0:T(1024)S(1)} %mul.161, ...), kind=kOutput, calls=%fused_computation.47 | convolution fusion | flops 4838912000 | bytes 17327104 | tf_op jit(solution)/shard_map/dot_general | solution.py:41
  220.1 2.5 convert_reduce_fusion.4
  222.6 2.6 convolution_convert_fusion.3.g_ref
  225.3 34.2 %attend_backward.1 = bf16[1024,2304]{1,0:T(8,128)(2,1)} custom-call(s32[1,1024,1]{2,1,0:T(8,128)} %copy-done, s32[1,1,1024]{2,1,0:T(1,128)} %copy-done.24, bf16[1024,2304]{1,0:T(8,128)(2,1)} %add_convert_fusion.q_ref.k_ref.v_ref, bf16[1024,2304]{1,0:T(8,128)(2,1)} %add_convert_fusion.q_ref.k_ref.v_ref, bf16[1024,2304]{1,0:T(8,128)(2,1)} %add_convert_fusion.q_ref.k_ref.v_ref, ...), custom_call_target="tpu_custom_call" | custom-call | tf_op jit(solution)/shard_map/attend_backward/pallas_call | solution.py:208
  259.4 3.2 convert_reduce_fusion.1
  262.6 0.6 copy-done.34
  263.2 7.2 %fusion.29 = (f32[768]{0:T(1024)S(1)}, f32[1024]{0:T(1024)S(1)}, f32[1024]{0:T(1024)S(1)}, f32[768]{0:T(1024)S(1)}, bf16[1024,768]{1,0:T(8,128)(2,1)}, /*index=5*/f32[1024,768]{1,0:T(8,128)}) fusion(bf16[4,256,768]{2,1,0:T(8,128)(2,1)} %all-to-all-done, f32[1024]{0:T(1024)S(1)} %bitcast.121, f32[1024]{0:T(1024)S(1)} %bitcast.123, f32[768]{0:T(1024)S(1)} %mul.155, ...), kind=kOutput, calls=%fused_computation.44 | convolution fusion | flops 3634098688 | bytes 14577664 | tf_op jit(solution)/shard_map/dot_general | solution.py:41
  270.5 1.7 convert_reduce_fusion.3
  272.2 0.1 concatenate.12
  272.3 0.6 pad.16.refs_4_
  272.9 5.1 %fusion.26 = bf16[1024,768]{1,0:T(8,128)(2,1)} fusion(f32[1024,768]{1,0:T(8,128)} %copy-done.39, bf16[4,256,768]{2,1,0:T(8,128)(2,1)} %all-to-all-done, f32[1024,768]{1,0:T(8,128)} %get-tuple-element.144, f32[1024]{0:T(1024)S(1)} %broadcast_multiply_fusion, f32[1024]{0:T(1024)S(1)} %bitcast.122, f32[1024]{0:T(1024)S(1)} %broadcast_multiply_fusion.1, ...), kind=kLoop, calls=%fused_computation.41 | loop fusion | flops 7864320 | bytes 9456640 | tf_op jit(solution)/shard_map/convert_element_type | solution.py:803
  278.0 10.0 %convolution_convert_fusion.1 = bf16[768,3072]{1,0:T(8,128)(2,1)} fusion(bf16[1024,3072]{1,0:T(8,128)(2,1)} %get-tuple-element.146, f32[1024,768]{1,0:T(8,128)S(1)} %copy-done.38, f32[768]{0:T(1024)S(1)} %add.120, f32[768]{0:T(1024)S(1)} %mul.161, f32[1024]{0:T(1024)S(1)} %add_rsqrt_fusion, f32[1024]{0:T(1024)S(1)} %broadcast_multiply_fusion.4), kind=kOutput, calls=%fused_computation.19 | convolution fusion | flops 4838129664 | bytes 14170112 | tf_op jit(solution)/shard_map/dot_general | solution.py:35
  288.0 4.3 %all-to-all-start.3 = ((bf16[4,1,256,768]{3,2,1,0:T(8,128)(2,1)}), bf16[4,1,256,768]{3,2,1,0:T(8,128)(2,1)}, u32[]{:S(2)}, u32[]{:S(2)}) async-start(bf16[4,1,256,768]{3,2,1,0:T(8,128)(2,1)} %bitcast.112), calls=%async_computation.3 | async-start | bytes 3145728 | tf_op jit(solution)/shard_map/all_to_all | solution.py:719
  292.3 4.5 %convolution_convert_fusion.4 = bf16[768,768]{1,0:T(8,128)(2,1)} fusion(bf16[1024,768]{1,0:T(8,128)(2,1)S(1)} %get-tuple-element.74, f32[1024,768]{1,0:T(8,128)} %copy-done.39), kind=kOutput, calls=%fused_computation.58 | convolution fusion | flops 1209335808 | bytes 5898240 | tf_op jit(solution)/shard_map/dot_general | solution.py:35
  296.8 7.6 %convolution_convert_fusion.2 = bf16[768,2304]{1,0:T(8,128)(2,1)} fusion(bf16[1024,768]{1,0:T(8,128)(2,1)S(1)} %copy-done.47, bf16[1024,2304]{1,0:T(8,128)(2,1)} %attend_backward.1), kind=kOutput, calls=%fused_computation.20 | convolution fusion | flops 3625648128 | bytes 9830400 | tf_op jit(solution)/shard_map/dot_general | solution.py:35
  304.6 94.9 %scatter_gradients.1 = (f32[24,2304]{1,0:T(8,128)}, f32[24,768]{1,0:T(8,128)}, f32[24,3072]{1,0:T(8,128)}, f32[96,768]{1,0:T(8,128)}, f32[8,24]{1,0:T(8,128)}, /*index=5*/f32[1,96]{1,0:T(1,128)}, f32[16,128]{1,0:T(8,128)}) custom-call(bf16[4,2,4,24,2304]{4,3,2,1,0:T(8,128)(2,1)} %bitcast.115, bf16[4,2,4,24,768]{4,3,2,1,0:T(8,128)(2,1)} %bitcast.118, ...), custom_call_target="tpu_custom_call" | custom-call | tf_op jit(solution)/shard_map/scatter_gradients/pallas_call | solution.py:642
  399.7 1.0 copy-done.17
  400.7 1.0 copy-done.18
  401.6 0.9 copy-done.19
  402.6 0.9 copy-done.21
  403.4 0.7 copy-done.27
  404.1 0.7 copy-done.28
  404.8 0.7 copy-done.33
  405.5 2.6 lamb_update.1
  408.2 3.5 bitcast_convert_fusion
  411.6 1.1 copy.64
  (122 shorter events, 0.4 us)
Async XLA Ops:
  0.7 5.4 %copy-start.22 = (f32[8,24]{1,0:T(8,128)S(1)}, f32[8,24]{1,0:T(8,128)}, u32[]{:S(2)}) copy-start(f32[8,24]{1,0:T(8,128)} %refs_11_.3) | copy-start | bytes 2308
  0.7 5.4 %copy-start.5 = (f32[24,2304]{1,0:T(8,128)S(1)}, f32[24,2304]{1,0:T(8,128)}, u32[]{:S(2)}) copy-start(f32[24,2304]{1,0:T(8,128)} %refs_7_.3) | copy-start | bytes 663556
  0.7 6.1 %copy-start.13 = (f32[24,768]{1,0:T(8,128)S(1)}, f32[24,768]{1,0:T(8,128)}, u32[]{:S(2)}) copy-start(f32[24,768]{1,0:T(8,128)} %refs_8_.3) | copy-start | bytes 221188
  0.7 6.7 %copy-start.1 = (f32[24,3072]{1,0:T(8,128)S(1)}, f32[24,3072]{1,0:T(8,128)}, u32[]{:S(2)}) copy-start(f32[24,3072]{1,0:T(8,128)} %refs_9_.3) | copy-start | bytes 884740
  0.7 7.3 %copy-start.3 = (f32[96,768]{1,0:T(8,128)S(1)}, f32[96,768]{1,0:T(8,128)}, u32[]{:S(2)}) copy-start(f32[96,768]{1,0:T(8,128)} %refs_10_.1) | copy-start | bytes 884740
  0.7 8.0 %copy-start.29 = (f32[96]{0:T(128)S(1)}, f32[96]{0:T(128)}, u32[]{:S(2)}) copy-start(f32[96]{0:T(128)} %param.39) | copy-start | bytes 1156
  0.7 100.1 %all-to-all-start = ((bf16[4,256,768]{2,1,0:T(8,128)(2,1)}), bf16[4,256,768]{2,1,0:T(8,128)(2,1)}, u32[]{:S(2)}, u32[]{:S(2)}) async-start(bf16[4,256,768]{2,1,0:T(8,128)(2,1)} %param.21), calls=%async_computation | async-start | bytes 3145728 | tf_op jit(solution)/shard_map/all_to_all | solution.py:766
  99.1 17.6 %copy-start.24 = (s32[1,1,1024]{2,1,0:T(1,128)}, s32[1,1,1024]{2,1,0:T(1,128)S(1)}, u32[]{:S(2)}) copy-start(s32[1,1,1024]{2,1,0:T(1,128)S(1)} %get-tuple-element.133.seg_row) | copy-start | bytes 12292
  99.3 17.4 %copy-start = (s32[1,1024,1]{2,1,0:T(8,128)}, s32[1,1024,1]{2,1,0:T(8,128)S(1)}, u32[]{:S(2)}) copy-start(s32[1,1024,1]{2,1,0:T(8,128)S(1)} %copy.55.seg_col) | copy-start | bytes 12292
  100.9 57.3 %all-to-all-start.2 = ((bf16[4,256,768]{2,1,0:T(8,128)(2,1)}), bf16[4,256,768]{2,1,0:T(8,128)(2,1)}, u32[]{:S(2)}, u32[]{:S(2)}) async-start(bf16[4,256,768]{2,1,0:T(8,128)(2,1)} %param.22), calls=%async_computation.2 | async-start | bytes 3145728 | tf_op jit(solution)/shard_map/all_to_all | solution.py:767
  105.3 5.9 %copy-start.42 = (bf16[4,2,4,24,2304]{4,3,2,1,0:T(8,128)(2,1)S(1)}, bf16[4,2,4,24,2304]{4,3,2,1,0:T(8,128)(2,1)}, u32[]{:S(2)}) copy-start(bf16[4,2,4,24,2304]{4,3,2,1,0:T(8,128)(2,1)} %get-tuple-element.73) | copy-start | bytes 10616836
  116.6 28.5 %copy-start.44 = (bf16[4,2,4,24,768]{4,3,2,1,0:T(8,128)(2,1)S(1)}, bf16[4,2,4,24,768]{4,3,2,1,0:T(8,128)(2,1)}, u32[]{:S(2)}) copy-start(bf16[4,2,4,24,768]{4,3,2,1,0:T(8,128)(2,1)} %get-tuple-element.75) | copy-start | bytes 3538948
  145.1 3.1 copy-start.20
  145.2 4.8 %slice-start = ((s8[4718592]{0:T(1024)(128)(4,1)}), s8[4194304]{0:T(1024)(128)(4,1)S(1)}, s32[]{:S(2)}) async-start(s8[4718592]{0:T(1024)(128)(4,1)} %bitcast.126), calls=%async_computation.4 | async-start | bytes 8388608
  145.2 4.8 %slice-start.1 = ((s8[4718592]{0:T(1024)(128)(4,1)}), s8[524288]{0:T(1024)(128)(4,1)S(1)}, s32[]{:S(2)}) async-start(s8[4718592]{0:T(1024)(128)(4,1)} %bitcast.126), calls=%async_computation.5 | async-start | bytes 1048576
  148.3 1.7 copy-start.35
  158.2 22.1 %copy-start.46 = (f32[1024,3072]{1,0:T(8,128)S(1)}, f32[1024,3072]{1,0:T(8,128)}, u32[]{:S(2)}) copy-start(f32[1024,3072]{1,0:T(8,128)} %fusion.38) | copy-start | bytes 37748740
  158.2 38.4 %slice-start.2 = ((s8[4718592]{0:T(1024)(128)(4,1)}), s8[4194304]{0:T(1024)(128)(4,1)S(1)}, s32[]{:S(2)}) async-start(s8[4718592]{0:T(1024)(128)(4,1)} %bitcast.130), calls=%async_computation.6 | async-start | bytes 8388608
  180.3 16.3 %copy-start.36 = (f32[1024,768]{1,0:T(8,128)S(1)}, f32[1024,768]{1,0:T(8,128)}, u32[]{:S(2)}) copy-start(f32[1024,768]{1,0:T(8,128)} %copy-done.35) | copy-start | bytes 9437188
  180.3 16.3 %slice-start.3 = ((s8[4718592]{0:T(1024)(128)(4,1)}), s8[524288]{0:T(1024)(128)(4,1)S(1)}, s32[]{:S(2)}) async-start(s8[4718592]{0:T(1024)(128)(4,1)} %bitcast.130), calls=%async_computation.7 | async-start | bytes 1048576
  205.5 82.5 %all-to-all-start.1 = ((bf16[4,1,256,768]{3,2,1,0:T(8,128)(2,1)}), bf16[4,1,256,768]{3,2,1,0:T(8,128)(2,1)S(1)}, u32[]{:S(2)}, u32[]{:S(2)}) async-start(bf16[4,1,256,768]{3,2,1,0:T(8,128)(2,1)} %bitcast.116), calls=%async_computation.1 | async-start | bytes 3145728 | tf_op jit(solution)/shard_map/all_to_all | solution.py:719
  210.1 9.9 %copy-start.37 = (f32[1024,768]{1,0:T(8,128)S(1)}, f32[1024,768]{1,0:T(8,128)}, u32[]{:S(2)}) copy-start(f32[1024,768]{1,0:T(8,128)} %copy-done.35) | copy-start | bytes 9437188
  220.1 2.6 copy-start.45
  222.6 2.7 copy-start.39
  225.3 37.4 %copy-start.43 = (bf16[4,2,4,24,2304]{4,3,2,1,0:T(8,128)(2,1)S(1)}, bf16[4,2,4,24,2304]{4,3,2,1,0:T(8,128)(2,1)}, u32[]{:S(2)}) copy-start(bf16[4,2,4,24,2304]{4,3,2,1,0:T(8,128)(2,1)} %get-tuple-element.73) | copy-start | bytes 10616836
  259.4 3.8 copy-start.34
  272.9 5.1 %copy-start.38 = (f32[1024,768]{1,0:T(8,128)S(1)}, f32[1024,768]{1,0:T(8,128)}, u32[]{:S(2)}) copy-start(f32[1024,768]{1,0:T(8,128)} %copy-done.35) | copy-start | bytes 9437188
  288.0 8.8 %copy-start.40 = (bf16[4,1,256,768]{3,2,1,0:T(8,128)(2,1)}, bf16[4,1,256,768]{3,2,1,0:T(8,128)(2,1)S(1)}, u32[]{:S(2)}) copy-start(bf16[4,1,256,768]{3,2,1,0:T(8,128)(2,1)S(1)} %all-to-all-done.1) | copy-start | bytes 4718596
  288.0 120.2 %all-to-all-start.3 = ((bf16[4,1,256,768]{3,2,1,0:T(8,128)(2,1)}), bf16[4,1,256,768]{3,2,1,0:T(8,128)(2,1)}, u32[]{:S(2)}, u32[]{:S(2)}) async-start(bf16[4,1,256,768]{3,2,1,0:T(8,128)(2,1)} %bitcast.112), calls=%async_computation.3 | async-start | bytes 3145728 | tf_op jit(solution)/shard_map/all_to_all | solution.py:719
  292.3 4.5 %copy-start.47 = (bf16[1024,768]{1,0:T(8,128)(2,1)S(1)}, bf16[1024,768]{1,0:T(8,128)(2,1)}, u32[]{:S(2)}) copy-start(bf16[1024,768]{1,0:T(8,128)(2,1)} %get-tuple-element.124) | copy-start | bytes 4718596
  304.4 95.1 %copy-start.2 = (f32[24,3072]{1,0:T(8,128)S(1)}, f32[24,3072]{1,0:T(8,128)}, u32[]{:S(2)}) copy-start(f32[24,3072]{1,0:T(8,128)} %refs_9_.3) | copy-start | bytes 884740
  304.4 95.1 %copy-start.4 = (f32[96,768]{1,0:T(8,128)S(1)}, f32[96,768]{1,0:T(8,128)}, u32[]{:S(2)}) copy-start(f32[96,768]{1,0:T(8,128)} %refs_10_.1) | copy-start | bytes 884740
  304.4 95.1 %copy-start.6 = (f32[24,2304]{1,0:T(8,128)S(1)}, f32[24,2304]{1,0:T(8,128)}, u32[]{:S(2)}) copy-start(f32[24,2304]{1,0:T(8,128)} %refs_7_.3) | copy-start | bytes 663556
  304.4 95.1 %copy-start.7 = (f32[24,3072]{1,0:T(8,128)S(1)}, f32[24,3072]{1,0:T(8,128)}, u32[]{:S(2)}) copy-start(f32[24,3072]{1,0:T(8,128)} %refs_15_.3) | copy-start | bytes 884740
  304.5 95.1 %copy-start.8 = (f32[96,768]{1,0:T(8,128)S(1)}, f32[96,768]{1,0:T(8,128)}, u32[]{:S(2)}) copy-start(f32[96,768]{1,0:T(8,128)} %refs_16_.1) | copy-start | bytes 884740
  304.5 95.1 %copy-start.9 = (f32[24,3072]{1,0:T(8,128)S(1)}, f32[24,3072]{1,0:T(8,128)}, u32[]{:S(2)}) copy-start(f32[24,3072]{1,0:T(8,128)} %refs_21_.3) | copy-start | bytes 884740
  304.5 95.1 %copy-start.10 = (f32[96,768]{1,0:T(8,128)S(1)}, f32[96,768]{1,0:T(8,128)}, u32[]{:S(2)}) copy-start(f32[96,768]{1,0:T(8,128)} %refs_22_.1) | copy-start | bytes 884740
  304.5 95.1 %copy-start.11 = (f32[24,2304]{1,0:T(8,128)S(1)}, f32[24,2304]{1,0:T(8,128)}, u32[]{:S(2)}) copy-start(f32[24,2304]{1,0:T(8,128)} %refs_13_.3) | copy-start | bytes 663556
  304.5 95.1 %copy-start.12 = (f32[24,2304]{1,0:T(8,128)S(1)}, f32[24,2304]{1,0:T(8,128)}, u32[]{:S(2)}) copy-start(f32[24,2304]{1,0:T(8,128)} %refs_19_.3) | copy-start | bytes 663556
  304.5 95.1 %copy-start.14 = (f32[24,768]{1,0:T(8,128)S(1)}, f32[24,768]{1,0:T(8,128)}, u32[]{:S(2)}) copy-start(f32[24,768]{1,0:T(8,128)} %refs_8_.3) | copy-start | bytes 221188
  304.5 95.1 %copy-start.15 = (f32[24,768]{1,0:T(8,128)S(1)}, f32[24,768]{1,0:T(8,128)}, u32[]{:S(2)}) copy-start(f32[24,768]{1,0:T(8,128)} %refs_14_.3) | copy-start | bytes 221188
  304.5 95.1 %copy-start.16 = (f32[24,768]{1,0:T(8,128)S(1)}, f32[24,768]{1,0:T(8,128)}, u32[]{:S(2)}) copy-start(f32[24,768]{1,0:T(8,128)} %refs_20_.3) | copy-start | bytes 221188
  304.5 95.1 %copy-start.23 = (f32[8,24]{1,0:T(8,128)S(1)}, f32[8,24]{1,0:T(8,128)}, u32[]{:S(2)}) copy-start(f32[8,24]{1,0:T(8,128)} %refs_11_.3) | copy-start | bytes 2308
  304.6 95.1 %copy-start.25 = (f32[8,24]{1,0:T(8,128)S(1)}, f32[8,24]{1,0:T(8,128)}, u32[]{:S(2)}) copy-start(f32[8,24]{1,0:T(8,128)} %refs_17_.3) | copy-start | bytes 2308
  304.6 95.1 %copy-start.26 = (f32[8,24]{1,0:T(8,128)S(1)}, f32[8,24]{1,0:T(8,128)}, u32[]{:S(2)}) copy-start(f32[8,24]{1,0:T(8,128)} %refs_23_.1) | copy-start | bytes 2308
  304.6 95.1 %copy-start.30 = (f32[96]{0:T(128)S(1)}, f32[96]{0:T(128)}, u32[]{:S(2)}) copy-start(f32[96]{0:T(128)} %param.39) | copy-start | bytes 1156
  304.6 95.1 %copy-start.31 = (f32[96]{0:T(128)S(1)}, f32[96]{0:T(128)}, u32[]{:S(2)}) copy-start(f32[96]{0:T(128)} %param.40) | copy-start | bytes 1156
  304.6 95.1 %copy-start.32 = (f32[96]{0:T(128)S(1)}, f32[96]{0:T(128)}, u32[]{:S(2)}) copy-start(f32[96]{0:T(128)} %param.41) | copy-start | bytes 1156
  399.7 1.0 copy-start.17
  400.6 1.0 copy-start.18
  401.6 0.9 copy-start.19
  402.5 0.9 copy-start.21
  403.4 0.7 copy-start.27
  404.1 0.7 copy-start.28
  404.8 0.7 copy-start.33
  408.1 3.5 copy-start.41

commit v3 on v1

--- a/solution.py
+++ b/solution.py
@@ -1,3 +1,5 @@
+import functools
+
 import jax
 import jax.numpy as jnp
 from jax import lax
@@ -18,6 +20,8 @@
 LEARN_RATE = 0.4
 NORM_EPS = 1e-05
 STEP_NUMBER = 10.0
+CORR_ONE = 1.0 - BETA_ONE**STEP_NUMBER
+CORR_TWO = 1.0 - BETA_TWO**STEP_NUMBER
 
 BRAIN = jnp.bfloat16
 FLOAT = jnp.float32
@@ -82,8 +86,19 @@
     return (jnp.where(lane < HEAD_DIM, pair, zero), jnp.where(lane < HEAD_DIM, zero, pair))
 
 
-def attend_forward(seg_col, seg_row, q_ref, k_ref, v_ref, c_ref, lse_ref, bias):
+def attend_forward(counts, splits, *refs):
+    seg_col, seg_row, q_ref, k_ref, v_ref = refs[0:5]
+    cotangent, shards = refs[5], refs[6:8]
+    c_ref, lse_ref, back_rows, fulls = refs[8], refs[9], refs[10], refs[11:13]
+    bias, bounces, bounce, send_sem, recv_sem, own_sem, move_sem = refs[13], refs[14:16], *refs[16:]
     length = q_ref.shape[0]
+    here = Here(*counts)
+    slots = Slots(send_sem, recv_sem)
+    gathers = gathers_of(here, slots, shards, fulls, bounces, own_sem, splits)
+    move = Exchange(here, slots, cotangent, back_rows, True, bounce, move_sem)
+    waves = led_by(lambda: greet(here.near_peers()), waves_of(gathers))
+    blocks = windows(length)
+    beside = Beside(waves, HEADS // 2 * len(blocks), extra=(lambda: move.start(0), 5))
 
     @pl.when(pl.program_id(1) == 0)
     def _():
@@ -91,7 +106,8 @@
 
     v_turned = v_ref[...].T
     place = 0
-    for index, (low, high) in enumerate(windows(length)):
+    for index, (low, high) in enumerate(blocks):
+        beside.point(index, len(blocks))
         first = index * QUERY_BLOCK
         size = high - low
         queries = split_heads(q_ref[first : first + QUERY_BLOCK, :] * HEAD_DIM ** (-0.5))
@@ -111,12 +127,67 @@
         c_ref[first : first + QUERY_BLOCK, :] = context.astype(BRAIN)
         place += size
 
-
-def attend_backward(
-    seg_col, seg_row, q_ref, k_ref, v_ref, g_ref, lse_ref, out_ref, bias, key_sum, value_sum
-):
+    @pl.when((pl.program_id(0) == pl.num_programs(0) - 1) & (pl.program_id(1) == HEADS // 2 - 1))
+    def _():
+        beside.rest()
+        move.finish(0)
+        drain_all(gathers + [move])
+
+
+def led_by(ahead, waves):
+    def both():
+        ahead()
+        waves[0]()
+
+    return [both] + waves[1:]
+
+
+class Beside:
+    def __init__(self, waves, points, extra=None):
+        self.waves, self.points = waves, points
+        self.at = {}
+        early = len(waves) - 1
+        for index in range(early):
+            self.at.setdefault(index * points // early, []).append(waves[index])
+        if extra:
+            self.at.setdefault(extra[1], []).append(extra[0])
+        self.late = waves[early:]
+
+    def point(self, index, per_step):
+        for point, calls in self.at.items():
+            if point % per_step == index:
+
+                @pl.when((pl.program_id(0) == 0) & (pl.program_id(1) == point // per_step))
+                def _(calls=calls):
+                    for call in calls:
+                        call()
+
+    def rest(self):
+        for call in self.late:
+            call()
+
+
+def attend_backward(counts, splits, *refs):
+    seg_col, seg_row, q_ref, k_ref, v_ref, g_ref, lse_ref = refs[0:7]
+    mixed_rows, grads = refs[7], refs[8:10]
+    out_ref, mixed, shares = refs[10], refs[11], refs[12:14]
+    bias, key_sum, value_sum = refs[14:17]
+    buffers, bounce, send_sem, recv_sem, own_sem, move_sem = refs[17:25], *refs[25:]
     length = q_ref.shape[0]
     pair = pl.program_id(1)
+    here = Here(*counts)
+    slots = Slots(send_sem, recv_sem)
+    scatters, loads = scatters_of(here, slots, grads, buffers, shares, own_sem, splits)
+    move = Exchange(here, slots, mixed_rows, mixed, False, bounce, move_sem)
+
+    def begin():
+        for load in loads:
+            load().start()
+        greet(here.near_peers())
+
+    waves = led_by(begin, waves_of(scatters))
+    blocks = windows(length)
+    beside = Beside(waves, HEADS // 2 * len(blocks), extra=(lambda: move.start(0), 5))
 
     @pl.when(pair == 0)
     def _():
@@ -129,7 +200,8 @@
     lanes = 2 * HEAD_DIM
     column = pl.multiple_of(pair * lanes, lanes)
     place = 0
-    for index, (low, high) in enumerate(windows(length)):
+    for index, (low, high) in enumerate(blocks):
+        beside.point(index, len(blocks))
         first = index * QUERY_BLOCK
         size = high - low
         rows = slice(first, first + QUERY_BLOCK)
@@ -163,6 +235,12 @@
     out_ref[:, pl.ds(width + column, lanes)] = key_sum[...].astype(BRAIN)
     out_ref[:, pl.ds(2 * width + column, lanes)] = value_sum[...].astype(BRAIN)
 
+    @pl.when((pl.program_id(0) == pl.num_programs(0) - 1) & (pair == HEADS // 2 - 1))
+    def _():
+        beside.rest()
+        move.finish(0)
+        drain_all(scatters + [move])
+
 
 def attention_specs(length):
     lanes = 2 * HEAD_DIM
@@ -178,52 +256,712 @@
     return segs, [spec(0), spec(1), spec(2)], plain, lse, bias
 
 
-def attention_forward(segments, qkv, length):
+def attention_forward(segments, qkv, length, cotangent, shards, counts):
     rows = segments.shape[0]
     segs, qkv_specs, plain, lse, bias = attention_specs(length)
     width = HEADS * HEAD_DIM
+    row_count, pos_count, _ = cotangent.shape
+    splits = [True] * len(shards)
+    slots = slot_count(counts, [shard.shape for shard in shards], splits, 1)
     return pl.pallas_call(
-        attend_forward,
+        functools.partial(attend_forward, counts, splits),
         grid=(rows, HEADS // 2),
-        in_specs=segs + qkv_specs,
-        out_specs=[plain, lse],
+        in_specs=segs + qkv_specs + [ANYWHERE] * 3,
+        out_specs=[plain, lse] + [ANYWHERE] * 3,
         out_shape=[
             jax.ShapeDtypeStruct((rows * length, width), BRAIN),
             jax.ShapeDtypeStruct((rows, HEADS // 2, 8, length), FLOAT),
+            jax.ShapeDtypeStruct((rows, counts[1], pos_count, width), BRAIN),
+        ]
+        + [full_shape(shard, *counts) for shard in shards],
+        scratch_shapes=[bias]
+        + [pltpu.VMEM(shard.shape, shard.dtype) for shard in shards]
+        + [
+            pltpu.VMEM((rows, pos_count, width), BRAIN),
+            pltpu.SemaphoreType.DMA((slots,)),
+            pltpu.SemaphoreType.DMA((slots,)),
+            pltpu.SemaphoreType.DMA((2 * len(shards),)),
+            pltpu.SemaphoreType.DMA((2,)),
         ],
-        scratch_shapes=[bias],
         name="attend_forward",
-        compiler_params=pltpu.CompilerParams(vmem_limit_bytes=48 * 1024 * 1024),
-    )(segments[:, :, None], segments[:, None, :], qkv, qkv, qkv)
-
-
-def attention_backward(segments, qkv, grads, lse_rows, length):
+        compiler_params=pltpu.CompilerParams(
+            collective_id=1, has_side_effects=True, vmem_limit_bytes=48 * 1024 * 1024
+        ),
+    )(segments[:, :, None], segments[:, None, :], qkv, qkv, qkv, cotangent, *shards)
+
+
+def attention_backward(segments, qkv, context_grad, lse_rows, length, result, grads, shapes, counts):
     rows = segments.shape[0]
     segs, qkv_specs, plain, lse, bias = attention_specs(length)
     width = HEADS * HEAD_DIM
+    seq_count = counts[1]
+    pos_count = length // seq_count
+    splits = [True] * len(shapes)
+    slots = slot_count(counts, shapes, splits, 1)
     return pl.pallas_call(
-        attend_backward,
+        functools.partial(attend_backward, counts, splits),
         grid=(rows, HEADS // 2),
-        in_specs=segs + qkv_specs + [plain, lse],
-        out_specs=pl.BlockSpec((length, 3 * width), lambda r, j: (r, 0)),
-        out_shape=jax.ShapeDtypeStruct((rows * length, 3 * width), BRAIN),
+        in_specs=segs + qkv_specs + [plain, lse] + [ANYWHERE] * 3,
+        out_specs=[pl.BlockSpec((length, 3 * width), lambda r, j: (r, 0)), ANYWHERE] + [WHOLE] * 2,
+        out_shape=[
+            jax.ShapeDtypeStruct((rows * length, 3 * width), BRAIN),
+            jax.ShapeDtypeStruct((seq_count, rows, pos_count, width), BRAIN),
+        ]
+        + [jax.ShapeDtypeStruct(shape, FLOAT) for shape in shapes],
         scratch_shapes=[
             bias,
             pltpu.VMEM((length, 2 * HEAD_DIM), FLOAT),
             pltpu.VMEM((length, 2 * HEAD_DIM), FLOAT),
+        ]
+        + scatter_buffers(shapes, counts)
+        + [
+            pltpu.VMEM((rows, pos_count, width), BRAIN),
+            pltpu.SemaphoreType.DMA((slots,)),
+            pltpu.SemaphoreType.DMA((slots,)),
+            pltpu.SemaphoreType.DMA((len(shapes),)),
+            pltpu.SemaphoreType.DMA((2,)),
         ],
         name="attend_backward",
-        compiler_params=pltpu.CompilerParams(vmem_limit_bytes=56 * 1024 * 1024),
-    )(segments[:, :, None], segments[:, None, :], qkv, qkv, qkv, grads, lse_rows)
-
-
-def lamb_parts(weight, first, second, grad, decay, corr_one, corr_two, axis):
+        compiler_params=pltpu.CompilerParams(
+            collective_id=2, has_side_effects=True, vmem_limit_bytes=62 * 1024 * 1024
+        ),
+    )(
+        segments[:, :, None],
+        segments[:, None, :],
+        qkv,
+        qkv,
+        qkv,
+        context_grad,
+        lse_rows,
+        result.reshape(rows, seq_count, pos_count, width),
+        *scatter_views(grads, shapes, counts),
+    )
+
+
+MESH = pl.DeviceIdType.MESH
+ANYWHERE = pl.BlockSpec(memory_space=pl.ANY)
+WHOLE = pl.BlockSpec(memory_space=pltpu.VMEM)
+
+
+def bits_of(count):
+    return count.bit_length() - 1
+
+
+def flipped(value, bit):
+    step = 1 << bit
+    return value + step * (1 - 2 * lax.rem(lax.div(value, step), 2))
+
+
+def rounded_down(value, bit):
+    return lax.div(value, 1 << bit) * (1 << bit)
+
+
+def spread(value, bit, total):
+    step = 1 << (bit + 1)
+    return [lax.rem(value, step) + step * turn for turn in range(1 << (total - 1 - bit))]
+
+
+class Here:
+    def __init__(self, dp_count, seq_count):
+        self.dp_count, self.seq_count = dp_count, seq_count
+        self.half_count = dp_count // 2
+        self.seq_bits = bits_of(seq_count)
+        self.place, self.line = lax.axis_index("dp"), lax.axis_index("seq")
+        self.chip, self.core = lax.div(self.place, 2), lax.rem(self.place, 2)
+
+    def core_peer(self):
+        return {"dp": flipped(self.place, 0)}
+
+    def line_peer(self, bit):
+        return {"seq": flipped(self.line, bit)}
+
+    def other_lines(self):
+        return [lax.rem(self.line + turn, self.seq_count) for turn in range(1, self.seq_count)]
+
+    def other_chips(self):
+        return [lax.rem(self.chip + turn, self.half_count) for turn in range(1, self.half_count)]
+
+    def chip_peers(self):
+        return [{"dp": 2 * chip + self.core} for chip in self.other_chips()]
+
+    def near_peers(self):
+        peers = [self.core_peer()] + self.chip_peers()
+        return peers + [{"seq": line} for line in self.other_lines()]
+
+    def all_peers(self):
+        peers = [{"dp": lax.rem(self.place + turn, self.dp_count)} for turn in range(1, self.dp_count)]
+        return peers + [{"seq": line} for line in self.other_lines()]
+
+
+def greet(peers):
+    barrier = pltpu.get_barrier_semaphore()
+    for peer in peers:
+        pl.semaphore_signal(barrier, inc=1, device_id=peer, device_id_type=MESH)
+    pl.semaphore_wait(barrier, len(peers))
+
+
+class Slots:
+    def __init__(self, send_sem, recv_sem):
+        self.send_sem, self.recv_sem, self.used = send_sem, recv_sem, 0
+
+    def take(self, count):
+        first = self.used
+        self.used += count
+        return first
+
+    def copy(self, slot, source, target, peer):
+        return pltpu.make_async_remote_copy(
+            source,
+            target,
+            self.send_sem.at[slot],
+            self.recv_sem.at[slot],
+            device_id=peer,
+            device_id_type=MESH,
+        )
+
+
+def parts_of(shape, split):
+    rows, width = shape
+    tiles = width // 128
+    if width % 128 or tiles < 2:
+        return [[(slice(0, rows), slice(0, width), False)]]
+    middle = tiles // 2 * 128
+    first, second = (0, middle), (middle, width)
+    every = slice(0, rows)
+    if split and rows % 32 == 0:
+        return [
+            [(part, slice(*first), False), (part, slice(*second), True)]
+            for part in (slice(0, rows // 2), slice(rows // 2, rows))
+        ]
+    if split and tiles >= 4:
+        lists = [[], []]
+        for (low, high), backwards in ((first, False), (second, True)):
+            cut = low + (high - low) // 256 * 128
+            lists[0].append((every, slice(low, cut), backwards))
+            lists[1].append((every, slice(cut, high), backwards))
+        return lists
+    return [[(every, slice(*first), False), (every, slice(*second), True)]]
+
+
+class Transfer:
+    def start(self, stage):
+        for copy in self.copies(stage):
+            copy.start()
+
+    def finish(self, stage):
+        for copy in self.copies(stage):
+            copy.wait_recv()
+        self.use(stage)
+
+    def use(self, stage):
+        pass
+
+    def drain(self):
+        for stage in range(self.stages):
+            for copy in self.copies(stage):
+                copy.wait_send()
+
+
+class Gather(Transfer):
+    def __init__(self, here, slots, shard, full, pieces, own_done):
+        self.here, self.slots, self.shard, self.full = here, slots, shard, full
+        self.pieces, self.own_done = pieces, own_done
+        self.stages = here.seq_bits + 2
+        self.each = here.half_count + here.seq_count
+        self.first = slots.take(self.each * len(pieces))
+
+    def copies(self, stage):
+        here, full = self.here, self.full
+        found = []
+        for index, (rows, columns, backwards) in enumerate(self.pieces):
+            slot = self.first + self.each * index
+            if stage == 0:
+                target = full.at[here.chip, here.core, here.line, rows, columns]
+                for turn, peer in enumerate(here.chip_peers()):
+                    source = self.shard.at[rows, columns]
+                    found.append(self.slots.copy(slot + turn, source, target, peer))
+                continue
+            slot += here.half_count - 1
+            if stage == self.stages - 1:
+                part = full.at[:, here.core, :, rows, columns]
+                slot += here.seq_count - 1
+                found.append(self.slots.copy(slot, part, part, here.core_peer()))
+                continue
+            if backwards:
+                bit = here.seq_bits - stage
+                slot += (1 << (stage - 1)) - 1
+                parts = [
+                    full.at[:, here.core, at, rows, columns]
+                    for at in spread(here.line, bit, here.seq_bits)
+                ]
+            else:
+                bit = stage - 1
+                slot += bit
+                block = pl.ds(rounded_down(here.line, bit), 1 << bit)
+                parts = [full.at[:, here.core, block, rows, columns]]
+            for turn, part in enumerate(parts):
+                found.append(self.slots.copy(slot + turn, part, part, here.line_peer(bit)))
+        return found
+
+    def start(self, stage):
+        if stage == 1:
+            self.own_done()
+        super().start(stage)
+
+
+class Scatter(Transfer):
+    def __init__(self, here, slots, grad, own, from_core, from_line, from_chip, share, pieces, load):
+        self.here, self.slots, self.grad, self.own = here, slots, grad, own
+        self.from_core, self.from_line, self.from_chip = from_core, from_line, from_chip
+        self.share, self.pieces, self.load = share, pieces, load
+        self.stages = here.seq_bits + 2
+        self.each = here.half_count + here.seq_count
+        self.first = slots.take(self.each * len(pieces))
+
+    def line_stage(self, stage, backwards):
+        here = self.here
+        if backwards:
+            bit = stage - 1
+            away = spread(flipped(here.line, bit), bit, here.seq_bits)
+            kept = spread(here.line, bit, here.seq_bits)
+        else:
+            bit = here.seq_bits - stage
+            away = [rounded_down(flipped(here.line, bit), bit) + at for at in range(1 << bit)]
+            kept = [rounded_down(here.line, bit) + at for at in range(1 << bit)]
+        base = sum(1 << (here.seq_bits - past) for past in range(1, stage))
+        return bit, away, kept, base
+
+    def copies(self, stage):
+        here = self.here
+        found = []
+        for index, (rows, columns, backwards) in enumerate(self.pieces):
+            slot = self.first + self.each * index
+            if stage == 0:
+                found.append(
+                    self.slots.copy(
+                        slot,
+                        self.grad.at[:, 1 - here.core, :, rows, columns],
+                        self.from_core.at[:, :, rows, columns],
+                        here.core_peer(),
+                    )
+                )
+            elif stage == self.stages - 1:
+                slot += here.seq_count
+                for turn, chip in enumerate(here.other_chips()):
+                    found.append(
+                        self.slots.copy(
+                            slot + turn,
+                            self.own.at[chip, here.line, rows, columns],
+                            self.from_chip.at[turn, rows, columns],
+                            {"dp": 2 * chip + here.core},
+                        )
+                    )
+            else:
+                bit, away, _, base = self.line_stage(stage, backwards)
+                for turn, at in enumerate(away):
+                    found.append(
+                        self.slots.copy(
+                            slot + 1 + base + turn,
+                            self.own.at[:, at, rows, columns],
+                            self.from_line.at[base + turn, :, rows, columns],
+                            here.line_peer(bit),
+                        )
+                    )
+        return found
+
+    def use(self, stage):
+        here, own = self.here, self.own
+        if stage == 0:
+            self.load()
+        for rows, columns, backwards in self.pieces:
+            if stage == 0:
+
+                def add(at, carry, rows=rows, columns=columns):
+                    one, two = lax.div(at, here.seq_count), lax.rem(at, here.seq_count)
+                    own[one, two, rows, columns] = (
+                        own[one, two, rows, columns] + self.from_core[one, two, rows, columns]
+                    )
+                    return carry
+
+                lax.fori_loop(0, here.half_count * here.seq_count, add, 0)
+            elif stage == self.stages - 1:
+                total = own[here.chip, here.line, rows, columns].astype(FLOAT)
+                for turn in range(here.half_count - 1):
+                    total = total + self.from_chip[turn, rows, columns].astype(FLOAT)
+                self.share[rows, columns] = total
+            else:
+                _, _, kept, base = self.line_stage(stage, backwards)
+                for turn, at in enumerate(kept):
+
+                    def add(one, carry, rows=rows, columns=columns, at=at, place=base + turn):
+                        own[one, at, rows, columns] = (
+                            own[one, at, rows, columns] + self.from_line[place, one, rows, columns]
+                        )
+                        return carry
+
+                    lax.fori_loop(0, here.half_count, add, 0)
+
+
+class Exchange(Transfer):
+    stages = 1
+
+    def __init__(self, here, slots, source, target, to_rows, bounce, sem):
+        self.here, self.slots, self.source, self.target = here, slots, source, target
+        self.to_rows, self.bounce, self.sem = to_rows, bounce, sem
+        self.first = slots.take(here.seq_count - 1)
+
+    def ends(self, line):
+        if self.to_rows:
+            count = self.target.shape[0]
+            block = self.source.at[pl.ds(line * count, count)]
+            return block, self.target.at[:, self.here.line]
+        return self.source.at[:, line], self.target.at[self.here.line]
+
+    def copies(self, stage):
+        return [
+            self.slots.copy(self.first + turn, *self.ends(line), {"seq": line})
+            for turn, line in enumerate(self.here.other_lines())
+        ]
+
+    def own_in(self):
+        return pltpu.make_async_copy(self.ends(self.here.line)[0], self.bounce, self.sem.at[0])
+
+    def own_out(self):
+        return pltpu.make_async_copy(self.bounce, self.ends(self.here.line)[1], self.sem.at[1])
+
+    def start(self, stage):
+        self.own_in().start()
+        super().start(stage)
+        self.own_in().wait()
+        self.own_out().start()
+
+    def use(self, stage):
+        self.own_out().wait()
+
+
+def waves_of(transfers):
+    def wave(count):
+        for index, transfer in enumerate(transfers):
+            stage = count - index
+            if 1 <= stage <= transfer.stages:
+                transfer.finish(stage - 1)
+            if 0 <= stage < transfer.stages:
+                transfer.start(stage)
+
+    total = max(index + transfer.stages for index, transfer in enumerate(transfers)) + 1
+    return [functools.partial(wave, count) for count in range(total)]
+
+
+def drain_all(transfers):
+    for transfer in transfers:
+        transfer.drain()
+
+
+def gathers_of(here, slots, shards, fulls, bounces, sem, splits):
+    found = []
+    for index, (shard, full, bounce) in enumerate(zip(shards, fulls, bounces)):
+        inward = lambda shard=shard, bounce=bounce, index=index: pltpu.make_async_copy(
+            shard, bounce, sem.at[2 * index]
+        )
+        outward = lambda full=full, bounce=bounce, index=index: pltpu.make_async_copy(
+            bounce, full.at[here.chip, here.core, here.line], sem.at[2 * index + 1]
+        )
+        for order, pieces in enumerate(parts_of(shard.shape, splits[index])):
+
+            def own_done(first=order == 0, inward=inward, outward=outward):
+                if first:
+                    inward().start()
+                    inward().wait()
+                    outward().start()
+                    outward().wait()
+
+            found.append(Gather(here, slots, shard, full, pieces, own_done))
+    return found
+
+
+def slot_count(here_shape, shapes, splits, exchanges):
+    half_count, seq_count = here_shape[0] // 2, here_shape[1]
+    each = half_count + seq_count
+    pieces = sum(len(part) for shape, split in zip(shapes, splits) for part in parts_of(shape, split))
+    return each * pieces + exchanges * (seq_count - 1)
+
+
+def full_shape(shard, dp_count, seq_count):
+    return jax.ShapeDtypeStruct((dp_count // 2, 2, seq_count) + shard.shape, shard.dtype)
+
+
+def gather_kernel(counts, splits, count, *refs):
+    tokens, shards, fulls = refs[0], refs[1 : 1 + count], refs[2 + count : 2 + 2 * count]
+    token_rows = refs[1 + count]
+    rest = refs[2 + 2 * count :]
+    bounces, bounce, send_sem, recv_sem, own_sem, move_sem = rest[:count], *rest[count:]
+    here = Here(*counts)
+    slots = Slots(send_sem, recv_sem)
+    gathers = gathers_of(here, slots, shards, fulls, bounces, own_sem, splits)
+    move = Exchange(here, slots, tokens, token_rows, True, bounce, move_sem)
+    greet(here.near_peers())
+    waves = waves_of(gathers)
+    waves[0]()
+    move.start(0)
+    for wave in waves[1:]:
+        wave()
+    move.finish(0)
+    drain_all(gathers + [move])
+
+
+def gather_first(tokens, shards, counts):
+    dp_count, seq_count = counts
+    row_count, pos_count, width = tokens.shape
+    rows = row_count // seq_count
+    splits = [False] * len(shards)
+    slots = slot_count(counts, [shard.shape for shard in shards], splits, 1)
+    return pl.pallas_call(
+        functools.partial(gather_kernel, counts, splits, len(shards)),
+        out_shape=[jax.ShapeDtypeStruct((rows, seq_count, pos_count, width), tokens.dtype)]
+        + [full_shape(shard, *counts) for shard in shards],
+        in_specs=[ANYWHERE] * (1 + len(shards)),
+        out_specs=[ANYWHERE] * (1 + len(shards)),
+        scratch_shapes=[pltpu.VMEM(shard.shape, shard.dtype) for shard in shards]
+        + [
+            pltpu.VMEM((rows, pos_count, width), tokens.dtype),
+            pltpu.SemaphoreType.DMA((slots,)),
+            pltpu.SemaphoreType.DMA((slots,)),
+            pltpu.SemaphoreType.DMA((2 * len(shards),)),
+            pltpu.SemaphoreType.DMA((2,)),
+        ],
+        name="gather_first",
+        compiler_params=pltpu.CompilerParams(collective_id=0, has_side_effects=True),
+    )(tokens, *shards)
+
+
+def lamb_pieces(weight, first, second, grad, decay):
     first_new = BETA_ONE * first + (1.0 - BETA_ONE) * grad
     second_new = BETA_TWO * second + (1.0 - BETA_TWO) * grad * grad
-    update = first_new / corr_one / (jnp.sqrt(second_new / corr_two) + ADAM_EPS) + decay * weight
-    weight_sq = jnp.reshape(jnp.sum(weight * weight, axis=axis), (-1,))
-    update_sq = jnp.reshape(jnp.sum(update * update, axis=axis), (-1,))
-    return (first_new, second_new, update, weight_sq, update_sq)
+    spread_out = jnp.sqrt(second_new / CORR_TWO) + ADAM_EPS
+    update = first_new / CORR_ONE / spread_out + decay * weight
+    return (first_new, second_new, update)
+
+
+def square_sum(values):
+    return jnp.sum(jnp.sum(values * values, axis=1, keepdims=True), axis=0, keepdims=True)
+
+
+def picked(small, rank, vector_size, bias_size):
+    width = small.shape[1]
+    row = lax.broadcasted_iota(jnp.int32, (width, 128), 0)
+    lane = lax.broadcasted_iota(jnp.int32, (width, 128), 1)
+    dot = functools.partial(jnp.dot, precision=lax.Precision.HIGHEST, preferred_element_type=FLOAT)
+    chosen = (row == lane + rank * vector_size) & (lane < vector_size)
+    vector_grad = dot(small[0:8, :], jnp.where(chosen, 1.0, 0.0))[:, :vector_size]
+    start = rank * bias_size
+    chosen = (row == lane + lax.rem(start, width)) & (lane < bias_size)
+    tail = dot(small[8:16, :], jnp.where(chosen, 1.0, 0.0))
+    tail_row = lax.broadcasted_iota(jnp.int32, tail.shape, 0)
+    tail = jnp.sum(jnp.where(tail_row == lax.div(start, width), tail, 0.0), axis=0, keepdims=True)
+    return vector_grad, tail[:, :bias_size]
+
+
+def scatters_of(here, slots, grads, buffers, shares, own_sem, splits):
+    count = len(grads)
+    found, loads = [], []
+    for index, (grad, share) in enumerate(zip(grads, shares)):
+        own, *arrivals = buffers[index::count]
+        load = lambda grad=grad, own=own, index=index: pltpu.make_async_copy(
+            grad.at[:, here.core], own, own_sem.at[index]
+        )
+        loads.append(load)
+        for order, pieces in enumerate(parts_of(share.shape, splits[index])):
+            wait = (lambda load=load: load().wait()) if order == 0 else (lambda: None)
+            found.append(Scatter(here, slots, grad, own, *arrivals, share, pieces, wait))
+    return found, loads
+
+
+def scatter_buffers(shapes, counts):
+    half_count, seq_count = counts[0] // 2, counts[1]
+    leads = [(half_count, seq_count)] * 2 + [(seq_count - 1, half_count), (half_count - 1,)]
+    return [pltpu.VMEM(lead + shape, BRAIN) for lead in leads for shape in shapes]
+
+
+def scatter_views(grads, shapes, counts):
+    lead = (counts[0] // 2, 2, counts[1])
+    return [grad.reshape(lead + shape) for grad, shape in zip(grads, shapes)]
+
+
+class SmallSum(Transfer):
+    def __init__(self, here, small, sums, arrived, send_sem, recv_sem):
+        self.slots = Slots(send_sem, recv_sem)
+        self.small, self.sums, self.arrived = small, sums, arrived
+        self.peers = [here.core_peer()]
+        self.peers += [{"dp": flipped(here.place, bit + 1)} for bit in range(bits_of(here.half_count))]
+        self.peers += [here.line_peer(bit) for bit in range(here.seq_bits)]
+        self.stages = len(self.peers)
+
+    def copies(self, stage):
+        source = self.sums.at[stage - 1] if stage else self.small
+        return [self.slots.copy(stage, source, self.arrived.at[stage], self.peers[stage])]
+
+    def use(self, stage):
+        before = self.sums[stage - 1] if stage else self.small[...]
+        self.sums[stage] = before + self.arrived[stage]
+
+
+def scatter_kernel(counts, splits, *refs):
+    grads, small, input_rows = refs[0:2], refs[2], refs[3]
+    ready = refs[4:6]
+    weights, firsts, seconds = refs[6:12], refs[12:18], refs[18:24]
+    shares, norm_out, input_grad = refs[24:28], refs[28], refs[29]
+    buffers, bounce = refs[30:38], refs[38]
+    small_sum, small_in, norm_mine, norm_dp, norm_line, norm_seq = refs[39:45]
+    send_sem, recv_sem, own_sem, move_sem, small_send, small_recv, norm_send, norm_recv = refs[45:53]
+    here = Here(*counts)
+    slots = Slots(send_sem, recv_sem)
+    scatters, loads = scatters_of(here, slots, grads, buffers, shares[0:2], own_sem, splits)
+    move = Exchange(here, slots, input_rows, input_grad, False, bounce, move_sem)
+    total = SmallSum(here, small, small_sum, small_in, small_send, small_recv)
+    for load in loads:
+        load().start()
+    dp_peers, seq_peers = here.all_peers()[: here.dp_count - 1], here.all_peers()[here.dp_count - 1 :]
+    greet(dp_peers + seq_peers)
+    waves = waves_of(scatters)
+    more = waves_of([total])
+    for turn in range(max(len(waves), len(more))):
+        if turn < len(waves):
+            waves[turn]()
+        if turn < len(more):
+            more[turn]()
+        if turn == 1:
+            move.start(0)
+
+    rank = here.place * here.seq_count + here.line
+    vector_grad, bias_grad = picked(
+        small_sum[total.stages - 1], rank, shares[2].shape[1], shares[3].shape[1]
+    )
+    shares[2][...] = vector_grad
+    shares[3][...] = bias_grad
+    grads_now = [shares[0], shares[1], ready[0], ready[1], shares[2], shares[3]]
+
+    lane = lax.broadcasted_iota(jnp.int32, (8, 128), 1)
+    row = lax.broadcasted_iota(jnp.int32, (8, 128), 0)
+    tile = jnp.zeros((8, 128), FLOAT)
+    for index in (0, 1, 2, 3, 5):
+        decay = DECAY_RATE if index < 4 else 0.0
+        weight = weights[index][...]
+        update = lamb_pieces(
+            weight, firsts[index][...], seconds[index][...], grads_now[index][...], decay
+        )[2]
+        at = row == (index if index < 4 else 4)
+        tile = jnp.where(at & (lane == 0), square_sum(weight), tile)
+        tile = jnp.where(at & (lane == 1), square_sum(update), tile)
+    norm_mine[0:8, :] = tile
+    weight = weights[4][...]
+    update = lamb_pieces(weight, firsts[4][...], seconds[4][...], vector_grad, 0.0)[2]
+    weight_sq = jnp.sum(weight * weight, axis=1, keepdims=True)
+    update_sq = jnp.sum(update * update, axis=1, keepdims=True)
+    norm_mine[8:16, :] = jnp.where(lane == 0, weight_sq, jnp.where(lane == 1, update_sq, 0.0))
+
+    norm_slots = Slots(norm_send, norm_recv)
+
+    def exchange(source, held, peers, at):
+        base = norm_slots.take(len(peers))
+        copies = [
+            norm_slots.copy(base + turn, source, held.at[at], peer) for turn, peer in enumerate(peers)
+        ]
+        for copy in copies:
+            copy.start()
+        held[at] = source[...]
+        for copy in copies:
+            copy.wait_recv()
+        found = held[0]
+        for turn in range(1, held.shape[0]):
+            found = found + held[turn]
+        return copies, found
+
+    sent, found = exchange(norm_mine, norm_dp, dp_peers, here.place)
+    norm_line[...] = found
+    also, found = exchange(norm_line, norm_seq, seq_peers, here.line)
+    norm_out[...] = found
+    move.finish(0)
+    for copy in sent + also:
+        copy.wait_send()
+    drain_all(scatters + [total, move])
+
+
+def scatter_last(grads, small, input_rows, ready, weights, firsts, seconds, counts):
+    dp_count, seq_count = counts
+    shapes = [weight.shape for weight in weights]
+    splits = [False, False]
+    slots = slot_count(counts, shapes[:2], splits, 1)
+    stages = bits_of(dp_count) + bits_of(seq_count)
+    return pl.pallas_call(
+        functools.partial(scatter_kernel, counts, splits),
+        out_shape=[jax.ShapeDtypeStruct(shapes[at], FLOAT) for at in (0, 1, 4, 5)]
+        + [
+            jax.ShapeDtypeStruct((16, 128), FLOAT),
+            jax.ShapeDtypeStruct((seq_count,) + input_rows.shape[0:1] + input_rows.shape[2:], BRAIN),
+        ],
+        in_specs=[ANYWHERE] * 2 + [WHOLE] + [ANYWHERE] + [WHOLE] * 20,
+        out_specs=[WHOLE] * 5 + [ANYWHERE],
+        scratch_shapes=scatter_buffers(shapes[:2], counts)
+        + [
+            pltpu.VMEM(input_rows.shape[0:1] + input_rows.shape[2:], BRAIN),
+            pltpu.VMEM((stages,) + small.shape, FLOAT),
+            pltpu.VMEM((stages,) + small.shape, FLOAT),
+            pltpu.VMEM((16, 128), FLOAT),
+            pltpu.VMEM((dp_count, 16, 128), FLOAT),
+            pltpu.VMEM((16, 128), FLOAT),
+            pltpu.VMEM((seq_count, 16, 128), FLOAT),
+            pltpu.SemaphoreType.DMA((slots,)),
+            pltpu.SemaphoreType.DMA((slots,)),
+            pltpu.SemaphoreType.DMA((2,)),
+            pltpu.SemaphoreType.DMA((2,)),
+            pltpu.SemaphoreType.DMA((stages,)),
+            pltpu.SemaphoreType.DMA((stages,)),
+            pltpu.SemaphoreType.DMA((dp_count + seq_count,)),
+            pltpu.SemaphoreType.DMA((dp_count + seq_count,)),
+        ],
+        name="scatter_last",
+        compiler_params=pltpu.CompilerParams(
+            collective_id=3, has_side_effects=True, vmem_limit_bytes=56 * 1024 * 1024
+        ),
+    )(*scatter_views(grads, shapes, counts), small, input_rows, *ready, *weights, *firsts, *seconds)
+
+
+def lamb_kernel(*refs):
+    grads, norms = refs[0:6], refs[6]
+    weights, firsts, seconds = refs[7:13], refs[13:19], refs[19:25]
+    grad_out, first_out, second_out, new_out = refs[25:31], refs[31:37], refs[37:43], refs[43:49]
+    copy_out = refs[49:53]
+    weight_norm = jnp.sqrt(norms[:, 0:1])
+    scales = weight_norm / (jnp.sqrt(norms[:, 1:2]) + ADAM_EPS)
+    for index in range(6):
+        grad = grads[index][...]
+        weight = weights[index][...]
+        decay = DECAY_RATE if index < 4 else 0.0
+        first_new, second_new, update = lamb_pieces(
+            weight, firsts[index][...], seconds[index][...], grad, decay
+        )
+        scale = scales[8:16] if index == 4 else scales[min(index, 4) : min(index, 4) + 1]
+        new = weight - LEARN_RATE * scale * update
+        grad_out[index][...] = grad
+        first_out[index][...] = first_new
+        second_out[index][...] = second_new
+        new_out[index][...] = new
+        if index < 4:
+            copy_out[index][...] = new.astype(BRAIN)
+
+
+def lamb_all(grads, norms, weights, firsts, seconds):
+    vmem = pl.BlockSpec(memory_space=pltpu.VMEM)
+    shapes = [jax.ShapeDtypeStruct(weight.shape, FLOAT) for weight in weights]
+    copies = [jax.ShapeDtypeStruct(weight.shape, BRAIN) for weight in weights[:4]]
+    return pl.pallas_call(
+        lamb_kernel,
+        out_shape=shapes * 4 + copies,
+        in_specs=[vmem] * 25,
+        out_specs=[vmem] * 28,
+        name="lamb_update",
+        compiler_params=pltpu.CompilerParams(vmem_limit_bytes=48 * 1024 * 1024),
+    )(*grads, norms, *weights, *firsts, *seconds)
 
 
 def body(
@@ -249,33 +987,40 @@
     m_up_bias,
     v_up_bias,
 ):
-    both = ("dp", "seq")
-    small = jnp.concatenate([vectors.reshape(-1), up_bias]).astype(BRAIN)
-    small = lax.all_gather(small[None], both, axis=0, tiled=True)
-    cut = vectors.size
-    full_vectors = small[:, :cut].reshape(-1, vectors.shape[0], vectors.shape[1])
-    vector_rows = full_vectors.transpose(1, 0, 2).reshape(vectors.shape[0], -1).astype(FLOAT)
-    up_shift = small[:, cut:].reshape(-1).astype(FLOAT)
-    full_qkv = lax.all_gather(w_qkv.astype(BRAIN), both, axis=0, tiled=True)
-    full_out = lax.all_gather(w_out.astype(BRAIN), both, axis=0, tiled=True)
-    full_up = lax.all_gather(w_up.astype(BRAIN), both, axis=0, tiled=True)
-    full_down = lax.all_gather(w_down.astype(BRAIN), both, axis=0, tiled=True)
+    dp_count, seq_count = lax.axis_size("dp"), lax.axis_size("seq")
+    vector_size, bias_size = vectors.shape[1], up_bias.shape[0]
+    small = jnp.concatenate(
+        [
+            jnp.pad(vectors, ((0, 0), (0, 128 - vector_size))),
+            jnp.pad(up_bias[None], ((0, 7), (0, 128 - bias_size))),
+        ]
+    )
+    shards = [part.astype(BRAIN) for part in (small, w_qkv, w_out, w_up, w_down)]
+    counts = (dp_count, seq_count)
+    token_rows, *fulls = gather_first(tokens, shards[:3], counts)
+    small = fulls[0].reshape(dp_count * seq_count, 16, 128)
+    full_vectors = small[:, :8, :vector_size].transpose(1, 0, 2)
+    vector_rows = full_vectors.reshape(8, -1).astype(FLOAT)
+    up_shift = small[:, 8, :bias_size].reshape(-1).astype(FLOAT)
+    as_matrix = lambda full: full.reshape(-1, full.shape[-1])
+    full_qkv, full_out = as_matrix(fulls[1]), as_matrix(fulls[2])
 
     width = tokens.shape[2]
     length = segment_ids.shape[1]
-    token_rows = lax.all_to_all(tokens, "seq", split_axis=0, concat_axis=1, tiled=True)
-    back_rows = lax.all_to_all(cotangent, "seq", split_axis=0, concat_axis=1, tiled=True)
     rows = token_rows.shape[0]
     segments = lax.dynamic_slice_in_dim(segment_ids, lax.axis_index("seq") * rows, rows, 0)
     count = rows * length
     token_part = token_rows.reshape(count, width).astype(FLOAT)
-    back_part = back_rows.reshape(count, width)
 
     normed_one, plain_one, inverse_one = norm_forward(token_part, vector_rows[0], vector_rows[1])
     low_one = normed_one.astype(BRAIN)
     shifts = jnp.concatenate([vector_rows[4], jnp.zeros_like(vector_rows[4]), vector_rows[5]])
     qkv = (matmul(low_one, full_qkv) + shifts).astype(BRAIN)
-    context, lse_rows = attention_forward(segments, qkv, length)
+    context, lse_rows, back_rows, *fulls = attention_forward(
+        segments, qkv, length, cotangent, shards[3:], counts
+    )
+    full_up, full_down = as_matrix(fulls[0]), as_matrix(fulls[1])
+    back_part = back_rows.reshape(count, width)
     resid_one = token_part + matmul(context, full_out) + vector_rows[6]
     normed_two, plain_two, inverse_two = norm_forward(resid_one, vector_rows[2], vector_rows[3])
     low_two = normed_two.astype(BRAIN)
@@ -283,8 +1028,6 @@
     activated, gelu_pull = jax.vjp(gelu_tanh, hidden_pre)
     low_act = activated.astype(BRAIN)
     result = resid_one + matmul(low_act, full_down) + vector_rows[7]
-    mixed = result.astype(BRAIN).reshape(rows, length, width)
-    mixed = lax.all_to_all(mixed, "seq", split_axis=1, concat_axis=0, tiled=True)
 
     back_float = back_part.astype(FLOAT)
     grad_down = inner_rows(low_act, back_part)
@@ -297,13 +1040,20 @@
     branch_grad = resid_grad.astype(BRAIN)
     grad_out = inner_rows(context, branch_grad)
     context_grad = times_transposed(branch_grad, full_out).astype(BRAIN)
-    joined = attention_backward(segments, qkv, context_grad, lse_rows, length)
+    joined, mixed, share_up, share_down = attention_backward(
+        segments,
+        qkv,
+        context_grad,
+        lse_rows,
+        length,
+        result.astype(BRAIN),
+        [grad_up.astype(BRAIN), grad_down.astype(BRAIN)],
+        [w_up.shape, w_down.shape],
+        counts,
+    )
     grad_qkv = inner_rows(low_one, joined)
     one_grad = times_transposed(joined, full_qkv)
     input_rows = resid_grad + norm_backward(one_grad, plain_one, inverse_one, vector_rows[0])
-    input_grad = input_rows.astype(BRAIN).reshape(rows, length, width)
-    input_grad = lax.all_to_all(input_grad, "seq", split_axis=1, concat_axis=0, tiled=True)
-    input_grad = input_grad.astype(FLOAT)
     joined_sum = jnp.sum(joined.astype(FLOAT), axis=0)
     grad_vectors = jnp.stack(
         [
@@ -317,59 +1067,29 @@
             jnp.sum(back_float, axis=0),
         ]
     )
-    devices = width // vectors.shape[1]
-    small_grad = jnp.concatenate(
-        [
-            grad_vectors.reshape(vectors.shape[0], devices, -1).transpose(1, 0, 2).reshape(devices, -1),
-            grad_up_bias.reshape(devices, -1),
-        ],
-        axis=1,
+    small_grad = jnp.concatenate([grad_vectors, grad_up_bias.reshape(-1, width)])
+    small_grad = jnp.pad(small_grad, ((0, 16 - small_grad.shape[0]), (0, 0)))
+    as_row = lambda value: value.reshape(1, -1)
+    weights = (w_qkv, w_out, w_up, w_down, vectors, as_row(up_bias))
+    firsts = (m_qkv, m_out, m_up, m_down, m_vectors, as_row(m_up_bias))
+    seconds = (v_qkv, v_out, v_up, v_down, v_vectors, as_row(v_up_bias))
+    share_qkv, share_out, share_vectors, share_bias, norms, input_grad = scatter_last(
+        [grad_qkv.astype(BRAIN), grad_out.astype(BRAIN)],
+        small_grad,
+        input_rows.astype(BRAIN).reshape(rows, seq_count, length // seq_count, width),
+        [share_up, share_down],
+        weights,
+        firsts,
+        seconds,
+        counts,
     )
-    scatter = lambda value: lax.psum_scatter(value, both, scatter_dimension=0, tiled=True)
-    small_share = scatter(small_grad)[0]
-    shares = (
-        scatter(grad_qkv),
-        scatter(grad_out),
-        scatter(grad_up),
-        scatter(grad_down),
-        small_share[:cut].reshape(vectors.shape),
-        small_share[cut:],
-    )
-    count_float = jnp.asarray(STEP_NUMBER, FLOAT)
-    corr_one = 1.0 - jnp.power(jnp.asarray(BETA_ONE, FLOAT), count_float)
-    corr_two = 1.0 - jnp.power(jnp.asarray(BETA_TWO, FLOAT), count_float)
-    weights = (w_qkv, w_out, w_up, w_down, vectors, up_bias)
-    firsts = (m_qkv, m_out, m_up, m_down, m_vectors, m_up_bias)
-    seconds = (v_qkv, v_out, v_up, v_down, v_vectors, v_up_bias)
-    decays = (DECAY_RATE, DECAY_RATE, DECAY_RATE, DECAY_RATE, 0.0, 0.0)
-    axes_list = (None, None, None, None, 1, None)
-    parts = [
-        lamb_parts(*each, corr_one, corr_two, axis)
-        for *each, axis in zip(weights, firsts, seconds, shares, decays, axes_list)
-    ]
-    totals = lax.psum(
-        jnp.stack(
-            [
-                jnp.concatenate([part[3] for part in parts]),
-                jnp.concatenate([part[4] for part in parts]),
-            ]
-        ),
-        both,
-    )
-    ratios = jnp.sqrt(totals[0]) / (jnp.sqrt(totals[1]) + ADAM_EPS)
-    scales = [ratios[0], ratios[1], ratios[2], ratios[3], ratios[4:12][:, None], ratios[12]]
-    news = [
-        weight - LEARN_RATE * scale * part[2] for weight, scale, part in zip(weights, scales, parts)
-    ]
-    return (
-        mixed,
-        input_grad,
-        *shares,
-        *[part[0] for part in parts],
-        *[part[1] for part in parts],
-        *news,
-        *[new.astype(BRAIN) for new in news[:4]],
-    )
+    shares = [share_qkv, share_out, share_up, share_down, share_vectors, share_bias]
+    results = list(lamb_all(shares, norms, weights, firsts, seconds))
+    mixed = mixed.reshape(tokens.shape)
+    input_grad = input_grad.reshape(tokens.shape).astype(FLOAT)
+    for index in (5, 11, 17, 23):
+        results[index] = results[index].reshape(-1)
+    return (mixed, input_grad, *results)
 
 
 def solution(mesh):

time: 928 us -> 405 us (0.44)
  waiting for transfers between devices: 394 us -> 0 us
  Pallas kernels: 62.6 us -> 278 us
  blocking collectives: 184 us -> 0 us
  local copies, waits for them, and re-layouts: 61.8 us -> 6.86 us
  other arithmetic: 65.8 us -> 22.6 us
  matrix products: 113 us -> 92.2 us
  starting transfers between devices: 18.8 us -> 0 us
  between operations: 18.3 us -> 1.83 us
    reduce_scatter x4 -> x0, waiting for transfers between devices: 283 us -> none  [body(): lax.psum_scatter(value, both, scatter_dimension=0, tiled=True)]
    pallas_call x2 -> x5, Pallas kernels: 62.6 us -> 278 us  [the longest x1 78.5 us: attention_backward(): pl.pallas_call(functools.partial(attend_backward, counts, splits), grid=(...]
    all_gather x4 -> x0, waiting for transfers between devices: 110 us -> none  [the longest x1 60.9 us: body(): full_down = lax.all_gather(w_down.astype(BRAIN), both, axis=0, tiled=True)]
    all_gather x1 -> x0, blocking collectives: 79.1 us -> none  [body(): small = lax.all_gather(small[None], both, axis=0, tiled=True)]
    unnamed x1 -> x0, blocking collectives: 64.8 us -> none
    psum x1 -> x0, blocking collectives: 39.6 us -> none  [body(): lax.psum(jnp.stack([jnp.concatenate([part[3] for part in parts]), jnp.con...]
    unnamed x5, other arithmetic: 22.9 us -> 0.02 us
    unnamed x77 -> x103, local copies, waits for them, and re-layouts: 25 us -> 4.44 us
  transfers between devices with their start and end apart: 12 -> 0, of which waited for: 5 -> 0; matrix products, arithmetic and copies ran while one was open for 17% -> 0% of each run, Pallas kernels for 7% -> 0%
where the time goes in v3:
time: 405 us; the launch traced here: 402 us
  Pallas kernels  278 us (69%)
  matrix products  92.2 us (23%)
  other arithmetic  22.6 us (6%)
  local copies, waits for them, and re-layouts  6.86 us (2%)
    pallas_call x1, Pallas kernels, attention_backward(): pl.pallas_call(functools.partial(attend_backward, counts, splits), grid=(...  78.5 us
    pallas_call x1, Pallas kernels, attention_forward(): pl.pallas_call(functools.partial(attend_forward, counts, splits), grid=(r...  77.3 us
    pallas_call x1, Pallas kernels, scatter_last(): pl.pallas_call(functools.partial(scatter_kernel, counts, splits), out_sha...  67.2 us
    pallas_call x1, Pallas kernels, gather_first(): pl.pallas_call(functools.partial(gather_kernel, counts, splits, len(shard...  52.4 us
    dot_general x4, matrix products, times_transposed(): lax.dot_general(left_side, right_side, (((1,), (1,)), ((), ())), preferre...  33.9 us
    dot_general x4, matrix products, matmul(): return jnp.dot(left_side, right_side, preferred_element_type=FLOAT)  30.1 us
    dot_general x4, matrix products, inner_rows(): lax.dot_general(left_side, right_side, (((0,), (0,)), ((), ())), preferre...  28.3 us

profile of v3, /device:TPU:0, one launch (start us, length us, event | category | flops | bytes accessed | tf_op | source)
XLA Modules:
  0.0 401.6 jit_solution(2102944056807778321)
XLA Ops:
  0.7 0.7 bitcast_convert_fusion.1
  1.3 0.7 convert.14
  2.0 0.6 fusion.30.refs_1_
  2.6 0.7 dynamic-slice_bitcast_fusion
  3.4 1.5 convert_element_type.113.refs_3_
  4.9 1.6 convert_element_type.112.refs_2_
  6.5 1.0 convert_element_type.120.refs_6_
  7.4 1.0 convert_element_type.121.refs_7_
  8.4 0.2 copy.53.refs_0_
  8.7 52.4 %gather_first.1 = (bf16[1,4,256,768]{3,2,1,0:T(8,128)(2,1)}, bf16[4,2,4,16,128]{4,3,2,1,0:T(8,128)(2,1)}, bf16[4,2,4,24,2304]{4,3,2,1,0:T(8,128)(2,1)}, bf16[4,2,4,24,768]{4,3,2,1,0:T(8,128)(2,1)}) custom-call(bf16[4,256,768]{2,1,0:T(8,128)(2,1)} %refs_0_.1, bf16[16,128]{1,0:T(8,128)(2,1)} %fusion.30.refs_1_, ...), custom_call_target="tpu_custom_call" | custom-call | tf_op jit(solution)/shard_map/gather_first/pallas_call | solution.py:718
  61.0 1.8 convert_reduce_fusion.2
  62.9 2.0 fusion.9
  65.0 0.1 reshape.261
  65.1 0.1 add.128
  65.2 0.1 mul.158
  65.3 0.1 mul.152
  65.3 0.1 add.119
  65.4 0.1 add.109
  65.5 0.1 add.115
  65.6 0.1 squeeze.7
  65.7 0.1 squeeze.6
  65.8 0.6 fusion.12
  66.4 0.0 copy-start.4
  66.5 7.9 %add_convert_fusion.refs_2_.refs_3_.refs_4_ = bf16[1024,2304]{1,0:T(8,128)(2,1)} fusion(bf16[1024,768]{1,0:T(8,128)(2,1)S(1)} %bitcast.104, bf16[768,2304]{1,0:T(8,128)(2,1)} %bitcast.120, f32[2304]{0:T(1024)S(1)} %pad_maximum_fusion), kind=kOutput, calls=%fused_computation.12 | convolution fusion | flops 3628597248 | bytes 9839616 | tf_op jit(solution)/shard_map/dot_general | solution.py:31
  74.4 77.3 %attend_forward.1 = (bf16[1024,768]{1,0:T(8,128)(2,1)S(1)}, f32[1,6,8,1024]{3,2,1,0:T(8,128)S(1)}, bf16[1,4,256,768]{3,2,1,0:T(8,128)(2,1)S(1)}, bf16[4,2,4,24,3...) custom-call(s32[1,1024,1]{2,1,0:T(8,128)S(1)} %copy.53.refs_0_, s32[1,1,1024]{2,1,0:T(1,128)S(1)} %get-tuple-element.144.refs_1_, ...), custom_call_target="tpu_custom_call" | custom-call | tf_op jit(solution)/shard_map/attend_forward/pallas_call | solution.py:266
  151.7 0.0 copy-start.29
  151.7 0.3 convert_reduce_fusion.3
  152.1 1.6 fusion.38
  153.7 0.5 multiply_reduce_fusion.2
  154.2 0.3 slice-done.2
  154.5 0.4 slice-done.3
  154.9 8.2 %fusion.35 = f32[1024,3072]{1,0:T(8,128)} fusion(bf16[768,3072]{1,0:T(8,128)(2,1)S(1)} %bitcast.114, f32[1024,768]{1,0:T(8,128)S(1)} %get-tuple-element.153, f32[768]{0:T(1024)S(1)} %add.119, f32[768]{0:T(1024)S(1)} %mul.158, f32[1024]{0:T(1024)S(1)} %add_rsqrt_fusion, f32[1024]{0:T(1024)S(1)} %broadcast_multiply_fusion.4), kind=kOutput, calls=%fused_computation.78 | convolution fusion | flops 4835770368 | bytes 20461568 | tf_op jit(solution)/shard_map/dot_general | solution.py:31
  163.1 12.3 %add_convert_fusion.1 = bf16[1024,768]{1,0:T(8,128)(2,1)} fusion(f32[1024,768]{1,0:T(8,128)S(1)} %get-tuple-element.153, bf16[3072,768]{1,0:T(8,128)(2,1)S(1)} %bitcast.118, f32[768]{0:T(1024)S(1)} %add.128, f32[1024,3072]{1,0:T(8,128)} %fusion.35, f32[3072]{0:T(1024)S(1)} %reshape.261), kind=kOutput, calls=%fused_computation.43 | convolution fusion | flops 4865654784 | bytes 22035456 | tf_op jit(solution)/shard_map/dot_general | solution.py:31
  175.5 16.3 %convert_reduce_fusion = (f32[3072]{0:T(1024)S(1)}, bf16[1024,3072]{1,0:T(8,128)(2,1)}) fusion(f32[1024,3072]{1,0:T(8,128)} %fusion.35, f32[3072]{0:T(1024)S(1)} %reshape.261, bf16[1024,768]{1,0:T(8,128)(2,1)S(1)} %bitcast.88, bf16[3072,768]{1,0:T(8,128)(2,1)S(1)} %bitcast.119), kind=kOutput, calls=%fused_computation.9 | convolution fusion | flops 4904186880 | bytes 25190400 | tf_op jit(solution)/shard_map/dot_general | solution.py:41
  191.8 12.5 %convolution_convert_fusion = bf16[3072,768]{1,0:T(8,128)(2,1)} fusion(bf16[1024,768]{1,0:T(8,128)(2,1)S(1)} %bitcast.89, f32[1024,3072]{1,0:T(8,128)} %fusion.35, f32[3072]{0:T(1024)S(1)} %reshape.261), kind=kOutput, calls=%fused_computation.13 | convolution fusion | flops 4865654784 | bytes 18886656 | tf_op jit(solution)/shard_map/dot_general | solution.py:35
  204.3 7.3 %multiply_reduce_fusion = (f32[768]{0:T(1024)S(1)}, f32[1024]{0:T(1024)S(1)}, f32[1024]{0:T(1024)S(1)}, f32[768]{0:T(1024)S(1)}, f32[1024,768]{1,0:T(8,128)}) fusion(f32[1024,768]{1,0:T(8,128)S(1)} %get-tuple-element.153, f32[1024]{0:T(1024)S(1)} %add_rsqrt_fusion, f32[1024]{0:T(1024)S(1)} %broadcast_multiply_fusion.4, f32[768]{0:T(1024)S(1)} %mul.158, ...), kind=kOutput, calls=%fused_computation.42 | convolution fusion | flops 4838912000 | bytes 17327104 | tf_op jit(solution)/shard_map/dot_general | solution.py:41
  211.6 3.6 convert_reduce_fusion.4
  215.3 0.1 copy-done.35
  215.4 1.9 copy-done.43
  217.2 7.9 %convolution_convert_fusion.1 = bf16[768,3072]{1,0:T(8,128)(2,1)} fusion(bf16[1024,3072]{1,0:T(8,128)(2,1)S(1)} %copy-done.43, f32[1024,768]{1,0:T(8,128)S(1)} %copy-done.35, f32[768]{0:T(1024)S(1)} %add.119, f32[768]{0:T(1024)S(1)} %mul.158, f32[1024]{0:T(1024)S(1)} %add_rsqrt_fusion, f32[1024]{0:T(1024)S(1)} %broadcast_multiply_fusion.4), kind=kOutput, calls=%fused_computation.14 | convolution fusion | flops 4838129664 | bytes 14170112 | tf_op jit(solution)/shard_map/dot_general | solution.py:35
  225.1 2.5 convolution_convert_fusion.4
  227.7 2.6 convolution_convert_fusion.3.refs_5_
  230.3 78.5 %attend_backward.1 = (bf16[1024,2304]{1,0:T(8,128)(2,1)}, bf16[4,1,256,768]{3,2,1,0:T(8,128)(2,1)}, f32[24,3072]{1,0:T(8,128)}, f32[96,768]{1,0:T(8,128)}) custom-call(s32[1,1024,1]{2,1,0:T(8,128)} %copy-done, s32[1,1,1024]{2,1,0:T(1,128)} %copy-done.19, bf16[1024,2304]{1,0:T(8,128)(2,1)} %add_convert_fusion.refs_2_.refs_3_.refs_4_, ...), custom_call_target="tpu_custom_call" | custom-call | tf_op jit(solution)/shard_map/attend_backward/pallas_call | solution.py:301
  308.8 0.0 copy-start.37
  308.8 7.7 %fusion.22 = (f32[1024]{0:T(1024)S(1)}, f32[768]{0:T(1024)S(1)}, f32[1024]{0:T(1024)S(1)}, f32[768]{0:T(1024)S(1)}, f32[1024,768]{1,0:T(8,128)S(1)}) fusion(bf16[1,4,256,768]{3,2,1,0:T(8,128)(2,1)S(1)} %copy-done.33, f32[768]{0:T(1024)S(1)} %mul.152, f32[1024]{0:T(1024)S(1)} %bitcast.110, f32[1024]{0:T(1024)S(1)} %bitcast.108, ...), kind=kOutput, calls=%fused_computation.35 | convolution fusion | flops 3631739392 | bytes 13001728 | tf_op jit(solution)/shard_map/dot_general | solution.py:41
  316.7 2.4 fusion.26
  319.1 0.0 slice-done
  319.1 0.4 slice-done.1
  319.5 0.7 convert_reduce_fusion.1
  320.2 5.3 %convolution_convert_fusion.2 = bf16[768,2304]{1,0:T(8,128)(2,1)} fusion(bf16[1024,768]{1,0:T(8,128)(2,1)S(1)} %get-tuple-element.135, bf16[1024,2304]{1,0:T(8,128)(2,1)S(1)} %bitcast.98), kind=kOutput, calls=%fused_computation.15 | convolution fusion | flops 3625648128 | bytes 9830400 | tf_op jit(solution)/shard_map/dot_general | solution.py:35
  325.5 0.1 concatenate.12
  325.6 0.6 pad.16.refs_2_
  326.2 67.2 %scatter_last.1 = (f32[24,2304]{1,0:T(8,128)}, f32[24,768]{1,0:T(8,128)}, f32[8,24]{1,0:T(8,128)}, f32[1,96]{1,0:T(1,128)}, f32[16,128]{1,0:T(8,128)}, /*index=5*/bf16[4,1,256,768]{3,2,1,0:T(8,128)(2,1)}) custom-call(bf16[4,2,4,24,2304]{4,3,2,1,0:T(8,128)(2,1)} %bitcast.101, bf16[4,2,4,24,768]{4,3,2,1,0:T(8,128)(2,1)} %bitcast.105, f32[16,768]{1,0:T(8,128)} %pad.16.refs_2_, ...), custom_call_target="tpu_custom_call" | custom-call | tf_op jit(solution)/shard_map/scatter_last/pallas_call | solution.py:895
  393.5 0.0 copy-start.2
  393.5 0.0 copy-start.3
  393.5 0.0 copy-start.7
  393.5 0.0 copy-start.8
  393.6 0.0 copy-start.13
  393.6 0.0 copy-start.14
  393.6 0.0 copy-start.21
  393.7 0.0 copy-start.22
  393.7 3.5 bitcast_convert_fusion
  397.5 2.7 lamb_update.1
  400.2 1.1 copy.59
  (111 shorter events, 0.4 us)
Async XLA Ops:
  3.3 71.1 %copy-start.19 = (s32[1,1,1024]{2,1,0:T(1,128)}, s32[1,1,1024]{2,1,0:T(1,128)S(1)}, u32[]{:S(2)}) copy-start(s32[1,1,1024]{2,1,0:T(1,128)S(1)} %get-tuple-element.144.refs_1_) | copy-start | bytes 12292
  8.6 65.8 %copy-start = (s32[1,1024,1]{2,1,0:T(8,128)}, s32[1,1024,1]{2,1,0:T(8,128)S(1)}, u32[]{:S(2)}) copy-start(s32[1,1024,1]{2,1,0:T(8,128)S(1)} %copy.53.refs_0_) | copy-start | bytes 12292
  61.0 3.9 copy-start.39
  61.0 4.8 %copy-start.31 = (bf16[1,4,256,768]{3,2,1,0:T(8,128)(2,1)S(1)}, bf16[1,4,256,768]{3,2,1,0:T(8,128)(2,1)}, u32[]{:S(2)}) copy-start(bf16[1,4,256,768]{3,2,1,0:T(8,128)(2,1)} %get-tuple-element.77) | copy-start | bytes 4718596
  66.4 8.0 %copy-start.4 = (bf16[4,256,768]{2,1,0:T(8,128)(2,1)S(1)}, bf16[4,256,768]{2,1,0:T(8,128)(2,1)}, u32[]{:S(2)}) copy-start(bf16[4,256,768]{2,1,0:T(8,128)(2,1)} %refs_5_.1) | copy-start | bytes 4718596
  74.4 77.6 %copy-start.32 = (bf16[1,4,256,768]{3,2,1,0:T(8,128)(2,1)S(1)}, bf16[1,4,256,768]{3,2,1,0:T(8,128)(2,1)}, u32[]{:S(2)}) copy-start(bf16[1,4,256,768]{3,2,1,0:T(8,128)(2,1)} %get-tuple-element.77) | copy-start | bytes 4718596
  74.4 77.6 %copy-start.40 = (bf16[4,2,4,24,768]{4,3,2,1,0:T(8,128)(2,1)S(1)}, bf16[4,2,4,24,768]{4,3,2,1,0:T(8,128)(2,1)}, u32[]{:S(2)}) copy-start(bf16[4,2,4,24,768]{4,3,2,1,0:T(8,128)(2,1)} %get-tuple-element.82) | copy-start | bytes 3538948
  151.7 1.9 copy-start.17
  151.7 1.9 copy-start.29
  152.0 2.5 slice-start.2
  152.1 2.8 slice-start.3
  153.7 50.7 %copy-start.34 = (f32[1024,768]{1,0:T(8,128)}, f32[1024,768]{1,0:T(8,128)S(1)}, u32[]{:S(2)}) copy-start(f32[1024,768]{1,0:T(8,128)S(1)} %get-tuple-element.153) | copy-start | bytes 9437188
  153.7 9.5 %slice-start.4 = ((s8[4718592]{0:T(1024)(128)(4,1)}), s8[4194304]{0:T(1024)(128)(4,1)S(1)}, s32[]{:S(2)}) async-start(s8[4718592]{0:T(1024)(128)(4,1)} %bitcast.116), calls=%async_computation.4 | async-start | bytes 8388608
  154.9 8.2 %slice-start.5 = ((s8[4718592]{0:T(1024)(128)(4,1)}), s8[524288]{0:T(1024)(128)(4,1)S(1)}, s32[]{:S(2)}) async-start(s8[4718592]{0:T(1024)(128)(4,1)} %bitcast.116), calls=%async_computation.5 | async-start | bytes 1048576
  191.8 12.5 %copy-start.42 = (bf16[1024,3072]{1,0:T(8,128)(2,1)S(1)}, bf16[1024,3072]{1,0:T(8,128)(2,1)}, u32[]{:S(2)}) copy-start(bf16[1024,3072]{1,0:T(8,128)(2,1)} %get-tuple-element.157) | copy-start | bytes 18874372
  211.6 3.8 copy-start.35
  211.6 5.6 %copy-start.43 = (bf16[1024,3072]{1,0:T(8,128)(2,1)S(1)}, bf16[1024,3072]{1,0:T(8,128)(2,1)}, u32[]{:S(2)}) copy-start(bf16[1024,3072]{1,0:T(8,128)(2,1)} %get-tuple-element.157) | copy-start | bytes 18874372
  217.2 10.4 %copy-start.36 = (f32[1024,768]{1,0:T(8,128)}, f32[1024,768]{1,0:T(8,128)S(1)}, u32[]{:S(2)}) copy-start(f32[1024,768]{1,0:T(8,128)S(1)} %get-tuple-element.133) | copy-start | bytes 9437188
  217.2 7.9 %copy-start.30 = (bf16[1024,768]{1,0:T(8,128)(2,1)S(1)}, bf16[1024,768]{1,0:T(8,128)(2,1)}, u32[]{:S(2)}) copy-start(bf16[1024,768]{1,0:T(8,128)(2,1)} %copy-done.29) | copy-start | bytes 4718596
  225.1 2.5 copy-start.41
  230.3 78.6 %copy-start.33 = (bf16[1,4,256,768]{3,2,1,0:T(8,128)(2,1)S(1)}, bf16[1,4,256,768]{3,2,1,0:T(8,128)(2,1)}, u32[]{:S(2)}) copy-start(bf16[1,4,256,768]{3,2,1,0:T(8,128)(2,1)} %get-tuple-element.77) | copy-start | bytes 4718596
  308.8 7.8 %copy-start.37 = (f32[1024,768]{1,0:T(8,128)S(1)}, f32[1024,768]{1,0:T(8,128)}, u32[]{:S(2)}) copy-start(f32[1024,768]{1,0:T(8,128)} %copy-done.36) | copy-start | bytes 9437188
  316.6 2.5 slice-start
  316.7 2.8 slice-start.1
  393.4 3.8 copy-start.1
  393.5 3.8 copy-start.2
  393.5 3.8 copy-start.3
  393.5 3.8 copy-start.5
  393.5 3.8 copy-start.6
  393.5 3.8 copy-start.7
  393.5 3.8 copy-start.8
  393.5 3.8 copy-start.9
  393.5 3.8 copy-start.10
  393.5 3.8 copy-start.11
  393.6 3.8 copy-start.12
  393.6 3.7 copy-start.13
  393.6 3.7 copy-start.14
  393.6 3.7 copy-start.15
  393.6 3.7 copy-start.16
  393.6 3.7 copy-start.18
  393.6 3.7 copy-start.20
  393.6 3.7 copy-start.21
  393.7 3.7 copy-start.22
  393.7 3.7 copy-start.23
  393.7 3.7 copy-start.24
  393.7 3.7 copy-start.25
  393.7 3.7 copy-start.26
  393.7 3.7 copy-start.27
  393.7 3.7 copy-start.28
  393.7 6.5 %copy-start.38 = (bf16[4,1,256,768]{3,2,1,0:T(8,128)(2,1)S(1)}, bf16[4,1,256,768]{3,2,1,0:T(8,128)(2,1)}, u32[]{:S(2)}) copy-start(bf16[4,1,256,768]{3,2,1,0:T(8,128)(2,1)} %get-tuple-element.86) | copy-start | bytes 4718596

commit v4 on v3

--- a/solution.py
+++ b/solution.py
@@ -88,17 +88,16 @@
 
 def attend_forward(counts, splits, *refs):
     seg_col, seg_row, q_ref, k_ref, v_ref = refs[0:5]
-    cotangent, shards = refs[5], refs[6:8]
-    c_ref, lse_ref, back_rows, fulls = refs[8], refs[9], refs[10], refs[11:13]
-    bias, bounces, bounce, send_sem, recv_sem, own_sem, move_sem = refs[13], refs[14:16], *refs[16:]
+    shards, c_ref, lse_ref, fulls = refs[5:8], refs[8], refs[9], refs[10:13]
+    bias, bounces, send_sem, recv_sem, own_sem = refs[13], refs[14:17], *refs[17:]
     length = q_ref.shape[0]
     here = Here(*counts)
     slots = Slots(send_sem, recv_sem)
     gathers = gathers_of(here, slots, shards, fulls, bounces, own_sem, splits)
-    move = Exchange(here, slots, cotangent, back_rows, True, bounce, move_sem)
-    waves = led_by(lambda: greet(here.near_peers()), waves_of(gathers))
+    groups = [gathers[:2]] + [[each] for each in gathers[2:]]
+    waves = led_by(lambda: greet(here.near_peers()), waves_of(groups))
     blocks = windows(length)
-    beside = Beside(waves, HEADS // 2 * len(blocks), extra=(lambda: move.start(0), 5))
+    beside = Beside(waves, HEADS // 2 * len(blocks))
 
     @pl.when(pl.program_id(1) == 0)
     def _():
@@ -130,8 +129,7 @@
     @pl.when((pl.program_id(0) == pl.num_programs(0) - 1) & (pl.program_id(1) == HEADS // 2 - 1))
     def _():
         beside.rest()
-        move.finish(0)
-        drain_all(gathers + [move])
+        drain_all(gathers)
 
 
 def led_by(ahead, waves):
@@ -143,14 +141,11 @@
 
 
 class Beside:
-    def __init__(self, waves, points, extra=None):
-        self.waves, self.points = waves, points
+    def __init__(self, waves, points):
         self.at = {}
         early = len(waves) - 1
         for index in range(early):
             self.at.setdefault(index * points // early, []).append(waves[index])
-        if extra:
-            self.at.setdefault(extra[1], []).append(extra[0])
         self.late = waves[early:]
 
     def point(self, index, per_step):
@@ -169,25 +164,24 @@
 
 def attend_backward(counts, splits, *refs):
     seg_col, seg_row, q_ref, k_ref, v_ref, g_ref, lse_ref = refs[0:7]
-    mixed_rows, grads = refs[7], refs[8:10]
-    out_ref, mixed, shares = refs[10], refs[11], refs[12:14]
+    grads, out_ref, shares = refs[7:10], refs[10], refs[11:14]
     bias, key_sum, value_sum = refs[14:17]
-    buffers, bounce, send_sem, recv_sem, own_sem, move_sem = refs[17:25], *refs[25:]
+    buffers, send_sem, recv_sem, own_sem = refs[17:29], *refs[29:]
     length = q_ref.shape[0]
     pair = pl.program_id(1)
     here = Here(*counts)
     slots = Slots(send_sem, recv_sem)
     scatters, loads = scatters_of(here, slots, grads, buffers, shares, own_sem, splits)
-    move = Exchange(here, slots, mixed_rows, mixed, False, bounce, move_sem)
 
     def begin():
         for load in loads:
             load().start()
         greet(here.near_peers())
 
-    waves = led_by(begin, waves_of(scatters))
+    groups = [[each] for each in scatters[:-2]] + [scatters[-2:]]
+    waves = led_by(begin, waves_of(groups))
     blocks = windows(length)
-    beside = Beside(waves, HEADS // 2 * len(blocks), extra=(lambda: move.start(0), 5))
+    beside = Beside(waves, HEADS // 2 * len(blocks))
 
     @pl.when(pair == 0)
     def _():
@@ -238,8 +232,7 @@
     @pl.when((pl.program_id(0) == pl.num_programs(0) - 1) & (pair == HEADS // 2 - 1))
     def _():
         beside.rest()
-        move.finish(0)
-        drain_all(scatters + [move])
+        drain_all(scatters)
 
 
 def attention_specs(length):
@@ -256,13 +249,12 @@
     return segs, [spec(0), spec(1), spec(2)], plain, lse, bias
 
 
-def attention_forward(segments, qkv, length, cotangent, shards, counts):
+def attention_forward(segments, qkv, length, shards, counts):
     rows = segments.shape[0]
     segs, qkv_specs, plain, lse, bias = attention_specs(length)
     width = HEADS * HEAD_DIM
-    row_count, pos_count, _ = cotangent.shape
-    splits = [True] * len(shards)
-    slots = slot_count(counts, [shard.shape for shard in shards], splits, 1)
+    splits = [False] + [True] * (len(shards) - 1)
+    slots = slot_count(counts, [shard.shape for shard in shards], splits, 0)
     return pl.pallas_call(
         functools.partial(attend_forward, counts, splits),
         grid=(rows, HEADS // 2),
@@ -271,41 +263,35 @@
         out_shape=[
             jax.ShapeDtypeStruct((rows * length, width), BRAIN),
             jax.ShapeDtypeStruct((rows, HEADS // 2, 8, length), FLOAT),
-            jax.ShapeDtypeStruct((rows, counts[1], pos_count, width), BRAIN),
         ]
         + [full_shape(shard, *counts) for shard in shards],
         scratch_shapes=[bias]
         + [pltpu.VMEM(shard.shape, shard.dtype) for shard in shards]
         + [
-            pltpu.VMEM((rows, pos_count, width), BRAIN),
             pltpu.SemaphoreType.DMA((slots,)),
             pltpu.SemaphoreType.DMA((slots,)),
             pltpu.SemaphoreType.DMA((2 * len(shards),)),
-            pltpu.SemaphoreType.DMA((2,)),
         ],
         name="attend_forward",
         compiler_params=pltpu.CompilerParams(
             collective_id=1, has_side_effects=True, vmem_limit_bytes=48 * 1024 * 1024
         ),
-    )(segments[:, :, None], segments[:, None, :], qkv, qkv, qkv, cotangent, *shards)
-
-
-def attention_backward(segments, qkv, context_grad, lse_rows, length, result, grads, shapes, counts):
+    )(segments[:, :, None], segments[:, None, :], qkv, qkv, qkv, *shards)
+
+
+def attention_backward(segments, qkv, context_grad, lse_rows, length, grads, shapes, counts):
     rows = segments.shape[0]
     segs, qkv_specs, plain, lse, bias = attention_specs(length)
     width = HEADS * HEAD_DIM
-    seq_count = counts[1]
-    pos_count = length // seq_count
-    splits = [True] * len(shapes)
-    slots = slot_count(counts, shapes, splits, 1)
+    splits = [True] * (len(shapes) - 1) + [False]
+    slots = slot_count(counts, shapes, splits, 0)
     return pl.pallas_call(
         functools.partial(attend_backward, counts, splits),
         grid=(rows, HEADS // 2),
         in_specs=segs + qkv_specs + [plain, lse] + [ANYWHERE] * 3,
-        out_specs=[pl.BlockSpec((length, 3 * width), lambda r, j: (r, 0)), ANYWHERE] + [WHOLE] * 2,
+        out_specs=[pl.BlockSpec((length, 3 * width), lambda r, j: (r, 0))] + [WHOLE] * 3,
         out_shape=[
             jax.ShapeDtypeStruct((rows * length, 3 * width), BRAIN),
-            jax.ShapeDtypeStruct((seq_count, rows, pos_count, width), BRAIN),
         ]
         + [jax.ShapeDtypeStruct(shape, FLOAT) for shape in shapes],
         scratch_shapes=[
@@ -315,11 +301,9 @@
         ]
         + scatter_buffers(shapes, counts)
         + [
-            pltpu.VMEM((rows, pos_count, width), BRAIN),
             pltpu.SemaphoreType.DMA((slots,)),
             pltpu.SemaphoreType.DMA((slots,)),
             pltpu.SemaphoreType.DMA((len(shapes),)),
-            pltpu.SemaphoreType.DMA((2,)),
         ],
         name="attend_backward",
         compiler_params=pltpu.CompilerParams(
@@ -333,7 +317,6 @@
         qkv,
         context_grad,
         lse_rows,
-        result.reshape(rows, seq_count, pos_count, width),
         *scatter_views(grads, shapes, counts),
     )
 
@@ -639,17 +622,19 @@
         self.own_out().wait()
 
 
-def waves_of(transfers):
+def waves_of(groups):
     def wave(count):
-        for index, transfer in enumerate(transfers):
+        for index, group in enumerate(groups):
             stage = count - index
-            if 1 <= stage <= transfer.stages:
-                transfer.finish(stage - 1)
-            if 0 <= stage < transfer.stages:
-                transfer.start(stage)
-
-    total = max(index + transfer.stages for index, transfer in enumerate(transfers)) + 1
-    return [functools.partial(wave, count) for count in range(total)]
+            for transfer in group:
+                if 1 <= stage <= transfer.stages:
+                    transfer.finish(stage - 1)
+            for transfer in group:
+                if 0 <= stage < transfer.stages:
+                    transfer.start(stage)
+
+    total = max(index + transfer.stages for index, group in enumerate(groups) for transfer in group)
+    return [functools.partial(wave, count) for count in range(total + 1)]
 
 
 def drain_all(transfers):
@@ -700,7 +685,7 @@
     gathers = gathers_of(here, slots, shards, fulls, bounces, own_sem, splits)
     move = Exchange(here, slots, tokens, token_rows, True, bounce, move_sem)
     greet(here.near_peers())
-    waves = waves_of(gathers)
+    waves = waves_of([gathers[:2]] + [[each] for each in gathers[2:]])
     waves[0]()
     move.start(0)
     for wave in waves[1:]:
@@ -713,7 +698,7 @@
     dp_count, seq_count = counts
     row_count, pos_count, width = tokens.shape
     rows = row_count // seq_count
-    splits = [False] * len(shards)
+    splits = [True] * len(shards)
     slots = slot_count(counts, [shard.shape for shard in shards], splits, 1)
     return pl.pallas_call(
         functools.partial(gather_kernel, counts, splits, len(shards)),
@@ -806,39 +791,39 @@
 
 
 def scatter_kernel(counts, splits, *refs):
-    grads, small, input_rows = refs[0:2], refs[2], refs[3]
-    ready = refs[4:6]
+    grads, small, input_rows = refs[0:1], refs[1], refs[2]
+    ready = refs[3:6]
     weights, firsts, seconds = refs[6:12], refs[12:18], refs[18:24]
-    shares, norm_out, input_grad = refs[24:28], refs[28], refs[29]
-    buffers, bounce = refs[30:38], refs[38]
-    small_sum, small_in, norm_mine, norm_dp, norm_line, norm_seq = refs[39:45]
-    send_sem, recv_sem, own_sem, move_sem, small_send, small_recv, norm_send, norm_recv = refs[45:53]
+    shares, norm_out, input_grad = refs[24:27], refs[27], refs[28]
+    buffers, bounce = refs[29:33], refs[33]
+    small_sum, small_in, norm_mine, norm_dp, norm_line, norm_seq = refs[34:40]
+    send_sem, recv_sem, own_sem, move_sem, small_send, small_recv, norm_send, norm_recv = refs[40:48]
     here = Here(*counts)
     slots = Slots(send_sem, recv_sem)
-    scatters, loads = scatters_of(here, slots, grads, buffers, shares[0:2], own_sem, splits)
+    scatters, loads = scatters_of(here, slots, grads, buffers, shares[0:1], own_sem, splits)
     move = Exchange(here, slots, input_rows, input_grad, False, bounce, move_sem)
     total = SmallSum(here, small, small_sum, small_in, small_send, small_recv)
     for load in loads:
         load().start()
     dp_peers, seq_peers = here.all_peers()[: here.dp_count - 1], here.all_peers()[here.dp_count - 1 :]
     greet(dp_peers + seq_peers)
-    waves = waves_of(scatters)
-    more = waves_of([total])
+    waves = waves_of([[each] for each in scatters])
+    more = waves_of([[total]])
     for turn in range(max(len(waves), len(more))):
         if turn < len(waves):
             waves[turn]()
         if turn < len(more):
             more[turn]()
-        if turn == 1:
+        if turn == here.seq_bits + 1:
             move.start(0)
 
     rank = here.place * here.seq_count + here.line
     vector_grad, bias_grad = picked(
-        small_sum[total.stages - 1], rank, shares[2].shape[1], shares[3].shape[1]
+        small_sum[total.stages - 1], rank, shares[1].shape[1], shares[2].shape[1]
     )
-    shares[2][...] = vector_grad
-    shares[3][...] = bias_grad
-    grads_now = [shares[0], shares[1], ready[0], ready[1], shares[2], shares[3]]
+    shares[1][...] = vector_grad
+    shares[2][...] = bias_grad
+    grads_now = [shares[0], *ready, shares[1], shares[2]]
 
     lane = lax.broadcasted_iota(jnp.int32, (8, 128), 1)
     row = lax.broadcasted_iota(jnp.int32, (8, 128), 0)
@@ -889,19 +874,19 @@
 def scatter_last(grads, small, input_rows, ready, weights, firsts, seconds, counts):
     dp_count, seq_count = counts
     shapes = [weight.shape for weight in weights]
-    splits = [False, False]
-    slots = slot_count(counts, shapes[:2], splits, 1)
+    splits = [True]
+    slots = slot_count(counts, shapes[:1], splits, 1)
     stages = bits_of(dp_count) + bits_of(seq_count)
     return pl.pallas_call(
         functools.partial(scatter_kernel, counts, splits),
-        out_shape=[jax.ShapeDtypeStruct(shapes[at], FLOAT) for at in (0, 1, 4, 5)]
+        out_shape=[jax.ShapeDtypeStruct(shapes[at], FLOAT) for at in (0, 4, 5)]
         + [
             jax.ShapeDtypeStruct((16, 128), FLOAT),
             jax.ShapeDtypeStruct((seq_count,) + input_rows.shape[0:1] + input_rows.shape[2:], BRAIN),
         ],
-        in_specs=[ANYWHERE] * 2 + [WHOLE] + [ANYWHERE] + [WHOLE] * 20,
-        out_specs=[WHOLE] * 5 + [ANYWHERE],
-        scratch_shapes=scatter_buffers(shapes[:2], counts)
+        in_specs=[ANYWHERE, WHOLE, ANYWHERE] + [WHOLE] * 21,
+        out_specs=[WHOLE] * 4 + [ANYWHERE],
+        scratch_shapes=scatter_buffers(shapes[:1], counts)
         + [
             pltpu.VMEM(input_rows.shape[0:1] + input_rows.shape[2:], BRAIN),
             pltpu.VMEM((stages,) + small.shape, FLOAT),
@@ -912,7 +897,7 @@
             pltpu.VMEM((seq_count, 16, 128), FLOAT),
             pltpu.SemaphoreType.DMA((slots,)),
             pltpu.SemaphoreType.DMA((slots,)),
-            pltpu.SemaphoreType.DMA((2,)),
+            pltpu.SemaphoreType.DMA((1,)),
             pltpu.SemaphoreType.DMA((2,)),
             pltpu.SemaphoreType.DMA((stages,)),
             pltpu.SemaphoreType.DMA((stages,)),
@@ -997,13 +982,13 @@
     )
     shards = [part.astype(BRAIN) for part in (small, w_qkv, w_out, w_up, w_down)]
     counts = (dp_count, seq_count)
-    token_rows, *fulls = gather_first(tokens, shards[:3], counts)
+    token_rows, *fulls = gather_first(tokens, shards[:2], counts)
     small = fulls[0].reshape(dp_count * seq_count, 16, 128)
     full_vectors = small[:, :8, :vector_size].transpose(1, 0, 2)
     vector_rows = full_vectors.reshape(8, -1).astype(FLOAT)
     up_shift = small[:, 8, :bias_size].reshape(-1).astype(FLOAT)
     as_matrix = lambda full: full.reshape(-1, full.shape[-1])
-    full_qkv, full_out = as_matrix(fulls[1]), as_matrix(fulls[2])
+    full_qkv = as_matrix(fulls[1])
 
     width = tokens.shape[2]
     length = segment_ids.shape[1]
@@ -1016,10 +1001,11 @@
     low_one = normed_one.astype(BRAIN)
     shifts = jnp.concatenate([vector_rows[4], jnp.zeros_like(vector_rows[4]), vector_rows[5]])
     qkv = (matmul(low_one, full_qkv) + shifts).astype(BRAIN)
-    context, lse_rows, back_rows, *fulls = attention_forward(
-        segments, qkv, length, cotangent, shards[3:], counts
-    )
-    full_up, full_down = as_matrix(fulls[0]), as_matrix(fulls[1])
+    context, lse_rows, *fulls = attention_forward(segments, qkv, length, shards[2:], counts)
+    full_out, full_up, full_down = [as_matrix(full) for full in fulls]
+    back_rows = lax.optimization_barrier((cotangent, context))[0]
+    back_rows = lax.all_to_all(back_rows, "seq", split_axis=0, concat_axis=0, tiled=True)
+    back_rows = back_rows.reshape(seq_count, rows, -1, width).transpose(1, 0, 2, 3)
     back_part = back_rows.reshape(count, width)
     resid_one = token_part + matmul(context, full_out) + vector_rows[6]
     normed_two, plain_two, inverse_two = norm_forward(resid_one, vector_rows[2], vector_rows[3])
@@ -1040,15 +1026,16 @@
     branch_grad = resid_grad.astype(BRAIN)
     grad_out = inner_rows(context, branch_grad)
     context_grad = times_transposed(branch_grad, full_out).astype(BRAIN)
-    joined, mixed, share_up, share_down = attention_backward(
+    mixed = result.astype(BRAIN).reshape(rows, seq_count, -1, width).transpose(1, 0, 2, 3)
+    mixed = lax.all_to_all(mixed, "seq", split_axis=0, concat_axis=0, tiled=True)
+    joined, share_down, share_up, share_out = attention_backward(
         segments,
         qkv,
         context_grad,
         lse_rows,
         length,
-        result.astype(BRAIN),
-        [grad_up.astype(BRAIN), grad_down.astype(BRAIN)],
-        [w_up.shape, w_down.shape],
+        [grad_down.astype(BRAIN), grad_up.astype(BRAIN), grad_out.astype(BRAIN)],
+        [w_down.shape, w_up.shape, w_out.shape],
         counts,
     )
     grad_qkv = inner_rows(low_one, joined)
@@ -1073,11 +1060,11 @@
     weights = (w_qkv, w_out, w_up, w_down, vectors, as_row(up_bias))
     firsts = (m_qkv, m_out, m_up, m_down, m_vectors, as_row(m_up_bias))
     seconds = (v_qkv, v_out, v_up, v_down, v_vectors, as_row(v_up_bias))
-    share_qkv, share_out, share_vectors, share_bias, norms, input_grad = scatter_last(
-        [grad_qkv.astype(BRAIN), grad_out.astype(BRAIN)],
+    share_qkv, share_vectors, share_bias, norms, input_grad = scatter_last(
+        [grad_qkv.astype(BRAIN)],
         small_grad,
         input_rows.astype(BRAIN).reshape(rows, seq_count, length // seq_count, width),
-        [share_up, share_down],
+        [share_out, share_up, share_down],
         weights,
         firsts,
         seconds,

time: 405 us -> 386 us (0.953); the launches traced: 402 us -> 378 us
  Pallas kernels: 278 us -> 238 us
  local copies, waits for them, and re-layouts: 6.86 us -> 16.5 us
  starting transfers between devices: 0 us -> 9.58 us
    pallas_call x1, Pallas kernels: 67.2 us -> 53.5 us  [scatter_last(): pl.pallas_call(functools.partial(scatter_kernel, counts, splits), out_sha...]
    pallas_call x1, Pallas kernels: 78.5 us -> 68.7 us  [attention_backward(): pl.pallas_call(functools.partial(attend_backward, counts, splits), grid=(...]
    all_to_all x0 -> x2, starting transfers between devices: none -> 9.58 us  [the longest x1 4.83 us: body(): lax.all_to_all(back_rows, 'seq', split_axis=0, concat_axis=0, tiled=True)]
    pallas_call x1, Pallas kernels: 77.3 us -> 68.1 us  [attention_forward(): pl.pallas_call(functools.partial(attend_forward, counts, splits), grid=(r...]
    unnamed x103 -> x95, local copies, waits for them, and re-layouts: 4.44 us -> 13.1 us
    pallas_call x1, Pallas kernels: 52.4 us -> 44.6 us  [gather_first(): pl.pallas_call(functools.partial(gather_kernel, counts, splits, len(shard...]
  transfers between devices with their start and end apart: 0 -> 2, of which waited for: 0 -> 0; matrix products, arithmetic and copies ran while one was open for 0% -> 20% of each run, Pallas kernels for 0% -> 0%
where the time goes in v4:
time: 386 us; the launch traced here: 378 us
  Pallas kernels  238 us (62%)
  matrix products  91.3 us (24%)
  other arithmetic  21.2 us (5%)
  local copies, waits for them, and re-layouts  16.5 us (4%)
  starting transfers between devices  9.58 us (2%)
    pallas_call x1, Pallas kernels, attention_backward(): pl.pallas_call(functools.partial(attend_backward, counts, splits), grid=(...  68.7 us
    pallas_call x1, Pallas kernels, attention_forward(): pl.pallas_call(functools.partial(attend_forward, counts, splits), grid=(r...  68.1 us
    pallas_call x1, Pallas kernels, scatter_last(): pl.pallas_call(functools.partial(scatter_kernel, counts, splits), out_sha...  53.5 us
    pallas_call x1, Pallas kernels, gather_first(): pl.pallas_call(functools.partial(gather_kernel, counts, splits, len(shard...  44.6 us
    dot_general x4, matrix products, times_transposed(): lax.dot_general(left_side, right_side, (((1,), (1,)), ((), ())), preferre...  34.6 us
    dot_general x4, matrix products, inner_rows(): lax.dot_general(left_side, right_side, (((0,), (0,)), ((), ())), preferre...  28.8 us
    dot_general x4, matrix products, matmul(): return jnp.dot(left_side, right_side, preferred_element_type=FLOAT)  27.9 us
    unnamed x95, local copies, waits for them, and re-layouts  13.1 us
  transfers between devices with their start and end apart: 2, of which 0 were waited for; matrix products, arithmetic and copies ran while one was open for 20% of the time, Pallas kernels for 0%

profile of v4, /device:TPU:0, one launch (start us, length us, event | category | flops | bytes accessed | tf_op | source)
XLA Modules:
  0.0 378.2 jit_solution(14434668853977146250)
XLA Ops:
  0.7 0.7 bitcast_convert_fusion.1
  1.3 0.7 convert.14
  2.0 1.6 convert_element_type.112.refs_2_
  3.7 0.6 fusion.30.refs_1_
  4.3 44.6 %gather_first.1 = (bf16[1,4,256,768]{3,2,1,0:T(8,128)(2,1)}, bf16[4,2,4,16,128]{4,3,2,1,0:T(8,128)(2,1)}, bf16[4,2,4,24,2304]{4,3,2,1,0:T(8,128)(2,1)}) custom-call(bf16[4,256,768]{2,1,0:T(8,128)(2,1)} %refs_0_.1, bf16[16,128]{1,0:T(8,128)(2,1)} %fusion.30.refs_1_, bf16[24,2304]{1,0:T(8,128)(2,1)} %convert_element_type.112.refs_2_), custom_call_target="tpu_custom_call" | custom-call | tf_op jit(solution)/shard_map/gather_first/pallas_call | solution.py:703
  48.9 1.0 slice.58
  49.9 0.7 dynamic-slice_bitcast_fusion
  50.6 0.2 copy.55.refs_0_
  50.9 0.1 add.109
  51.0 0.1 mul.152
  51.1 1.7 convert_reduce_fusion.2
  52.8 0.6 fusion.9
  53.4 0.1 squeeze.7
  53.5 0.1 squeeze.6
  53.7 0.6 fusion.12
  54.3 1.2 copy-done.42
  55.6 5.4 %add_convert_fusion.refs_2_.refs_3_.refs_4_ = bf16[1024,2304]{1,0:T(8,128)(2,1)} fusion(bf16[1024,768]{1,0:T(8,128)(2,1)S(1)} %bitcast.105, bf16[768,2304]{1,0:T(8,128)(2,1)S(1)} %bitcast.118, f32[2304]{0:T(1024)S(1)} %pad_maximum_fusion), kind=kOutput, calls=%fused_computation.12 | convolution fusion | flops 3628597248 | bytes 9839616 | tf_op jit(solution)/shard_map/dot_general | solution.py:31
  61.0 68.1 %attend_forward.1 = (bf16[1024,768]{1,0:T(8,128)(2,1)S(1)}, f32[1,6,8,1024]{3,2,1,0:T(8,128)S(1)}, bf16[4,2,4,24,768]{4,3,2,1,0:T(8,128)(2,1)S(1)}, bf16[4,2,4,2...) custom-call(s32[1,1024,1]{2,1,0:T(8,128)S(1)} %copy.55.refs_0_, s32[1,1,1024]{2,1,0:T(1,128)S(1)} %get-tuple-element.142.refs_1_, ...), custom_call_target="tpu_custom_call" | custom-call | tf_op jit(solution)/shard_map/attend_forward/pallas_call | solution.py:258
  129.1 0.0 copy-start.20
  129.1 0.7 copy-done.20
  129.8 1.1 copy-done.31
  130.9 1.0 copy-done.33
  131.9 4.8 %all-to-all-start.1 = ((bf16[4,256,768]{2,1,0:T(8,128)(2,1)}), bf16[4,256,768]{2,1,0:T(8,128)(2,1)}, u32[]{:S(2)}, u32[]{:S(2)}) async-start(bf16[4,256,768]{2,1,0:T(8,128)(2,1)} %param.22), calls=%async_computation.1 | async-start | bytes 3145728 | tf_op jit(solution)/shard_map/all_to_all | solution.py:1007
  136.8 0.9 fusion.27
  137.7 0.1 add.115
  137.7 0.1 add.127
  137.8 0.1 add.119
  137.9 0.1 mul.158
  138.0 2.9 fusion.38
  141.0 1.6 copy-done.37
  142.6 0.5 multiply_reduce_fusion.2
  143.2 0.1 reshape.253
  143.3 0.0 copy-start.38
  143.3 8.3 %fusion.35 = f32[1024,3072]{1,0:T(8,128)S(1)} fusion(bf16[768,3072]{1,0:T(8,128)(2,1)} %bitcast.113, f32[1024,768]{1,0:T(8,128)} %copy-done.37, f32[768]{0:T(1024)S(1)} %add.119, f32[768]{0:T(1024)S(1)} %mul.158, f32[1024]{0:T(1024)S(1)} %add_rsqrt_fusion, f32[1024]{0:T(1024)S(1)} %broadcast_multiply_fusion.4), kind=kOutput, calls=%fused_computation.78 | convolution fusion | flops 4835770368 | bytes 20461568 | tf_op jit(solution)/shard_map/dot_general | solution.py:31
  151.6 4.5 %copy-done.43 = f32[1024,3072]{1,0:T(8,128)} copy-done((f32[1024,3072]{1,0:T(8,128)}, f32[1024,3072]{1,0:T(8,128)S(1)}, u32[]{:S(2)}) %copy-start.43) | copy-done | bytes 12582936
  156.1 11.2 %add_convert_fusion.1 = bf16[1024,768]{1,0:T(8,128)(2,1)} fusion(f32[1024,768]{1,0:T(8,128)S(1)} %copy-done.38, bf16[3072,768]{1,0:T(8,128)(2,1)} %bitcast.115, f32[768]{0:T(1024)S(1)} %add.127, f32[1024,3072]{1,0:T(8,128)S(1)} %fusion.35, f32[3072]{0:T(1024)S(1)} %reshape.253), kind=kOutput, calls=%fused_computation.45 | convolution fusion | flops 4865654784 | bytes 22035456 | tf_op jit(solution)/shard_map/dot_general | solution.py:31
  167.3 4.7 %all-to-all-start = ((bf16[4,1,256,768]{3,2,1,0:T(8,128)(2,1)}), bf16[4,1,256,768]{3,2,1,0:T(8,128)(2,1)}, u32[]{:S(2)}, u32[]{:S(2)}) async-start(bf16[4,1,256,768]{3,2,1,0:T(8,128)(2,1)} %bitcast.104), calls=%async_computation | async-start | bytes 3145728 | tf_op jit(solution)/shard_map/all_to_all | solution.py:1030
  172.1 16.2 %convert_reduce_fusion = (f32[3072]{0:T(1024)S(1)}, bf16[1024,3072]{1,0:T(8,128)(2,1)S(1)}) fusion(f32[1024,3072]{1,0:T(8,128)} %copy-done.43, f32[3072]{0:T(1024)S(1)} %reshape.253, bf16[1024,768]{1,0:T(8,128)(2,1)} %bitcast.14, bf16[3072,768]{1,0:T(8,128)(2,1)} %bitcast.116), kind=kOutput, calls=%fused_computation.9 | convolution fusion | flops 4904186880 | bytes 25190400 | tf_op jit(solution)/shard_map/dot_general | solution.py:41
  188.3 12.9 %convolution_convert_fusion.1 = bf16[3072,768]{1,0:T(8,128)(2,1)} fusion(bf16[1024,768]{1,0:T(8,128)(2,1)} %bitcast.14, f32[1024,3072]{1,0:T(8,128)} %copy-done.43, f32[3072]{0:T(1024)S(1)} %reshape.253), kind=kOutput, calls=%fused_computation.14 | convolution fusion | flops 4865654784 | bytes 18886656 | tf_op jit(solution)/shard_map/dot_general | solution.py:35
  201.3 8.0 %multiply_reduce_fusion = (f32[768]{0:T(1024)S(1)}, f32[1024]{0:T(1024)S(1)}, f32[1024]{0:T(1024)S(1)}, f32[768]{0:T(1024)S(1)}, f32[1024,768]{1,0:T(8,128)S(1)}) fusion(f32[1024,768]{1,0:T(8,128)S(1)} %copy-done.39, f32[1024]{0:T(1024)S(1)} %add_rsqrt_fusion, f32[1024]{0:T(1024)S(1)} %broadcast_multiply_fusion.4, f32[768]{0:T(1024)S(1)} %mul.158, ...), kind=kOutput, calls=%fused_computation.42 | convolution fusion | flops 4838912000 | bytes 17327104 | tf_op jit(solution)/shard_map/dot_general | solution.py:41
  209.3 2.4 convert_reduce_fusion.4
  211.8 0.0 copy-start.40
  211.8 2.6 convolution_convert_fusion.3.refs_5_
  214.4 2.5 convolution_convert_fusion.4
  216.9 7.8 %convolution_convert_fusion = bf16[768,3072]{1,0:T(8,128)(2,1)} fusion(bf16[1024,3072]{1,0:T(8,128)(2,1)S(1)} %get-tuple-element.155, f32[1024,768]{1,0:T(8,128)S(1)} %copy-done.39, f32[768]{0:T(1024)S(1)} %add.119, f32[768]{0:T(1024)S(1)} %mul.158, f32[1024]{0:T(1024)S(1)} %add_rsqrt_fusion, f32[1024]{0:T(1024)S(1)} %broadcast_multiply_fusion.4), kind=kOutput, calls=%fused_computation.13 | convolution fusion | flops 4838129664 | bytes 14170112 | tf_op jit(solution)/shard_map/dot_general | solution.py:35
  224.6 68.7 %attend_backward.1 = (bf16[1024,2304]{1,0:T(8,128)(2,1)}, f32[96,768]{1,0:T(8,128)}, f32[24,3072]{1,0:T(8,128)}, f32[24,768]{1,0:T(8,128)}) custom-call(s32[1,1024,1]{2,1,0:T(8,128)} %copy-done, s32[1,1,1024]{2,1,0:T(1,128)} %copy-done.22, bf16[1024,2304]{1,0:T(8,128)(2,1)} %add_convert_fusion.refs_2_.refs_3_.refs_4_, ...), custom_call_target="tpu_custom_call" | custom-call | tf_op jit(solution)/shard_map/attend_backward/pallas_call | solution.py:288
  293.3 3.2 convert_reduce_fusion.1
  296.5 0.0 copy-start.41
  296.5 7.7 %fusion.22 = (f32[1024]{0:T(1024)S(1)}, f32[768]{0:T(1024)S(1)}, f32[1024]{0:T(1024)S(1)}, f32[768]{0:T(1024)S(1)}, f32[1024,768]{1,0:T(8,128)S(1)}) fusion(bf16[1,4,256,768]{3,2,1,0:T(8,128)(2,1)S(1)} %copy-done.36, f32[768]{0:T(1024)S(1)} %mul.152, f32[1024]{0:T(1024)S(1)} %bitcast.109, f32[1024]{0:T(1024)S(1)} %bitcast.111, ...), kind=kOutput, calls=%fused_computation.35 | convolution fusion | flops 3631739392 | bytes 13001728 | tf_op jit(solution)/shard_map/dot_general | solution.py:41
  304.3 2.4 fusion.26
  306.7 5.7 %convolution_convert_fusion.2 = bf16[768,2304]{1,0:T(8,128)(2,1)} fusion(bf16[1024,768]{1,0:T(8,128)(2,1)S(1)} %get-tuple-element.133, bf16[1024,2304]{1,0:T(8,128)(2,1)S(1)} %bitcast.100), kind=kOutput, calls=%fused_computation.15 | convolution fusion | flops 3625648128 | bytes 9830400 | tf_op jit(solution)/shard_map/dot_general | solution.py:35
  312.5 1.7 convert_reduce_fusion.3
  314.2 0.1 concatenate.12
  314.3 0.6 pad.16.refs_1_
  314.9 53.5 %scatter_last.1 = (f32[24,2304]{1,0:T(8,128)}, f32[8,24]{1,0:T(8,128)}, f32[1,96]{1,0:T(1,128)}, f32[16,128]{1,0:T(8,128)}, bf16[4,1,256,768]{3,2,1,0:T(8,128)(2,1)}) custom-call(bf16[4,2,4,24,2304]{4,3,2,1,0:T(8,128)(2,1)} %bitcast.103, f32[16,768]{1,0:T(8,128)} %pad.16.refs_1_, bf16[1,4,256,768]{3,2,1,0:T(8,128)(2,1)} %bitcast.98, ...), custom_call_target="tpu_custom_call" | custom-call | tf_op jit(solution)/shard_map/scatter_last/pallas_call | solution.py:880
  368.4 0.0 copy-start.2
  368.4 0.0 copy-start.6
  368.4 0.0 copy-start.7
  368.5 0.0 copy-start.9
  368.5 0.0 copy-start.12
  368.5 0.0 copy-start.16
  368.7 3.5 bitcast_convert_fusion
  372.4 2.7 lamb_update.1
  375.1 2.7 copy.63
  (105 shorter events, 0.4 us)
Async XLA Ops:
  2.0 51.5 %copy-start.14 = (f32[24,768]{1,0:T(8,128)S(1)}, f32[24,768]{1,0:T(8,128)}, u32[]{:S(2)}) copy-start(f32[24,768]{1,0:T(8,128)} %refs_8_.3) | copy-start | bytes 221188
  3.6 49.9 %copy-start.1 = (f32[24,3072]{1,0:T(8,128)S(1)}, f32[24,3072]{1,0:T(8,128)}, u32[]{:S(2)}) copy-start(f32[24,3072]{1,0:T(8,128)} %refs_9_.3) | copy-start | bytes 884740
  4.2 49.4 %copy-start.3 = (f32[96,768]{1,0:T(8,128)S(1)}, f32[96,768]{1,0:T(8,128)}, u32[]{:S(2)}) copy-start(f32[96,768]{1,0:T(8,128)} %refs_10_.3) | copy-start | bytes 884740
  48.9 3.9 %copy-start.35 = (bf16[1,4,256,768]{3,2,1,0:T(8,128)(2,1)S(1)}, bf16[1,4,256,768]{3,2,1,0:T(8,128)(2,1)}, u32[]{:S(2)}) copy-start(bf16[1,4,256,768]{3,2,1,0:T(8,128)(2,1)} %get-tuple-element.76) | copy-start | bytes 4718596
  50.6 10.3 %copy-start.22 = (s32[1,1,1024]{2,1,0:T(1,128)}, s32[1,1,1024]{2,1,0:T(1,128)S(1)}, u32[]{:S(2)}) copy-start(s32[1,1,1024]{2,1,0:T(1,128)S(1)} %get-tuple-element.142.refs_1_) | copy-start | bytes 12292
  50.9 10.1 %copy-start = (s32[1,1024,1]{2,1,0:T(8,128)}, s32[1,1024,1]{2,1,0:T(8,128)S(1)}, u32[]{:S(2)}) copy-start(s32[1,1024,1]{2,1,0:T(8,128)S(1)} %copy.55.refs_0_) | copy-start | bytes 12292
  53.6 2.0 copy-start.42
  129.1 0.7 copy-start.20
  129.8 1.1 copy-start.31
  130.9 1.0 copy-start.33
  131.9 6.1 %copy-start.32 = (bf16[1024,768]{1,0:T(8,128)(2,1)S(1)}, bf16[1024,768]{1,0:T(8,128)(2,1)}, u32[]{:S(2)}) copy-start(bf16[1024,768]{1,0:T(8,128)(2,1)} %copy-done.31) | copy-start | bytes 4718596
  131.9 6.1 %copy-start.34 = (bf16[4,2,4,24,768]{4,3,2,1,0:T(8,128)(2,1)S(1)}, bf16[4,2,4,24,768]{4,3,2,1,0:T(8,128)(2,1)}, u32[]{:S(2)}) copy-start(bf16[4,2,4,24,768]{4,3,2,1,0:T(8,128)(2,1)} %copy-done.33) | copy-start | bytes 3538948
  131.9 35.4 %all-to-all-start.1 = ((bf16[4,256,768]{2,1,0:T(8,128)(2,1)}), bf16[4,256,768]{2,1,0:T(8,128)(2,1)}, u32[]{:S(2)}, u32[]{:S(2)}) async-start(bf16[4,256,768]{2,1,0:T(8,128)(2,1)} %param.22), calls=%async_computation.1 | async-start | bytes 3145728 | tf_op jit(solution)/shard_map/all_to_all | solution.py:1007
  141.0 1.7 copy-start.37
  143.3 12.9 %copy-start.38 = (f32[1024,768]{1,0:T(8,128)S(1)}, f32[1024,768]{1,0:T(8,128)}, u32[]{:S(2)}) copy-start(f32[1024,768]{1,0:T(8,128)} %copy-done.37) | copy-start | bytes 9437188
  151.6 4.5 %copy-start.43 = (f32[1024,3072]{1,0:T(8,128)}, f32[1024,3072]{1,0:T(8,128)S(1)}, u32[]{:S(2)}) copy-start(f32[1024,3072]{1,0:T(8,128)S(1)} %fusion.35) | copy-start | bytes 37748740
  167.3 57.3 %all-to-all-start = ((bf16[4,1,256,768]{3,2,1,0:T(8,128)(2,1)}), bf16[4,1,256,768]{3,2,1,0:T(8,128)(2,1)}, u32[]{:S(2)}, u32[]{:S(2)}) async-start(bf16[4,1,256,768]{3,2,1,0:T(8,128)(2,1)} %bitcast.104), calls=%async_computation | async-start | bytes 3145728 | tf_op jit(solution)/shard_map/all_to_all | solution.py:1030
  188.3 12.9 %copy-start.39 = (f32[1024,768]{1,0:T(8,128)S(1)}, f32[1024,768]{1,0:T(8,128)}, u32[]{:S(2)}) copy-start(f32[1024,768]{1,0:T(8,128)} %copy-done.37) | copy-start | bytes 9437188
  211.8 2.6 copy-start.40
  293.3 3.2 copy-start.36
  293.3 13.4 %slice-start = ((s8[4718592]{0:T(1024)(128)(4,1)}), s8[4194304]{0:T(1024)(128)(4,1)S(1)}, s32[]{:S(2)}) async-start(s8[4718592]{0:T(1024)(128)(4,1)} %bitcast.99), calls=%async_computation.2 | async-start | bytes 8388608
  296.5 7.8 %copy-start.41 = (f32[1024,768]{1,0:T(8,128)S(1)}, f32[1024,768]{1,0:T(8,128)}, u32[]{:S(2)}) copy-start(f32[1024,768]{1,0:T(8,128)} %copy-done.40) | copy-start | bytes 9437188
  296.5 10.2 %slice-start.1 = ((s8[4718592]{0:T(1024)(128)(4,1)}), s8[524288]{0:T(1024)(128)(4,1)S(1)}, s32[]{:S(2)}) async-start(s8[4718592]{0:T(1024)(128)(4,1)} %bitcast.99), calls=%async_computation.3 | async-start | bytes 1048576
  368.4 3.8 copy-start.2
  368.4 3.8 copy-start.4
  368.4 3.8 copy-start.5
  368.4 3.8 copy-start.6
  368.4 3.7 copy-start.7
  368.5 3.7 copy-start.8
  368.5 3.7 copy-start.9
  368.5 3.7 copy-start.10
  368.5 3.7 copy-start.11
  368.5 3.7 copy-start.12
  368.5 3.7 copy-start.13
  368.5 3.7 copy-start.15
  368.5 3.7 copy-start.16
  368.6 3.7 copy-start.17
  368.6 3.7 copy-start.18
  368.6 3.7 copy-start.19
  368.6 3.7 copy-start.21
  368.6 3.7 copy-start.23
  368.6 3.7 copy-start.24
  368.6 3.7 copy-start.25
  368.6 3.7 copy-start.26
  368.6 3.7 copy-start.27
  368.7 3.7 copy-start.28
  368.7 3.7 copy-start.29
  368.7 3.7 copy-start.30
